TPU v7x, 512 devices: a whole 4x4x16 slice. The times are simulated.
512 devices in a mesh: space: 128 (over z, x, core), feat: 4 (over y).
Axes of the slice: x: 4, y: 4, z: 16, core: 2. Of those that a mesh axis runs over, the one named last changes fastest.
Arguments:
- bond_state: bfloat16 [262144, 512], P('space', 'feat'), may hold values from -6 to 6
- block_fill: int32 [2048], P('space'), may hold values from 64 to 128
- w_in: bfloat16 [512, 512], P(None, 'feat'), may hold values from -0.25 to 0.25
- w_down: bfloat16 [512, 64], P('feat'), may hold values from -0.25 to 0.25
- pair_coef: bfloat16 [14336, 128, 128], P('space'), may hold values from -0.5 to 0.5
- pair_source: int32 [14336], P('space'), may hold values from 0 to 15
- pair_owner: int32 [14336, 1], P('space'), may hold values from 0 to 127; in each aligned block of 112 rows (0 to 111, 112 to 223, ...) at most 2 rows name the same one
- pair_target: int32 [14336], P('space'), may hold values from 0 to 15
- w_gate: bfloat16 [64, 512], P(None, 'feat'), may hold values from -0.75 to 0.75
- w_atom_in: bfloat16 [64, 256], P(None, 'feat'), may hold values from -0.75 to 0.75
- atom_state: bfloat16 [256, 65536], P('feat', 'space'), may hold values from -6 to 6
- w_atom: bfloat16 [256, 256], P('feat'), may hold values from -0.375 to 0.375
- bond_ends: int32 [2, 262144], P(None, 'space'), may hold values from 0 to 1535
- w_left: bfloat16 [256, 512], P(None, 'feat'), may hold values from -0.375 to 0.375
- w_right: bfloat16 [256, 512], P(None, 'feat'), may hold values from -0.375 to 0.375
Outputs:
- bond_out: bfloat16 [262144, 512], P('space', 'feat')
- atom_out: bfloat16 [256, 65536], P('feat', 'space')
Inputs may be any that keep to these rules, and one draw needn't show every extreme that they name: `pair_owner`: among the 112 pairs of one domain, at most 2 name the same owner, a bound that some block reaches.
All inputs are finite; a program needn't handle non-finite values.
Results may differ from a plain program's by a relative error of at most 0.008.
Values may be sent and summed in bfloat16 or wider, within the bound.
No kernel may reach another device: no remote copies, remote signals or barrier semaphores. Data moves between devices by JAX's collectives and lax.ppermute only.
A program may use at most 64 MiB of HBM per device.

v0:
```python
import jax
import jax.numpy as jnp
from jax import lax
from jax.sharding import PartitionSpec as P


def copy_for_each(value, axis):
    copies = jnp.broadcast_to(value, (lax.axis_size(axis), *value.shape))
    return lax.all_to_all(copies, axis, split_axis=0, concat_axis=0, tiled=True)


def in_order(pieces, dim):
    pieces = jnp.moveaxis(pieces, 0, dim)
    lengths = pieces.shape
    return pieces.reshape(*lengths[:dim], lengths[dim] * lengths[dim + 1], *lengths[dim + 2 :])


def gathered_copies(value, axis, dim):
    pieces = copy_for_each(value, axis)
    return in_order(pieces, dim)


def in_blocks(value, dim, count):
    lengths = value.shape
    pieces = value.reshape(*lengths[:dim], count, lengths[dim] // count, *lengths[dim + 1 :])
    return jnp.moveaxis(pieces, dim, 0)


def sum_at_owner(value, axis, dim):
    pieces = in_blocks(value, dim, lax.axis_size(axis))
    arrived = lax.all_to_all(pieces, axis, split_axis=0, concat_axis=0, tiled=True)
    return arrived.sum(axis=0)


def passed_along(value, axis, steps):
    count = lax.axis_size(axis)
    pairs = [(source, (source + steps) % count) for source in range(count)]
    return lax.ppermute(value, axis, pairs)


def sum_at_owner_2(value, axis, dim):
    count = lax.axis_size(axis)
    pieces = lax.all_to_all(in_blocks(value, dim, count), axis, 0, 0, tiled=True)
    return jnp.sum(pieces.astype(jnp.float32), axis=0)


def extended(cells, sides, width):
    for axis, dim in sides:
        count = lax.axis_size(axis)
        head = lax.slice_in_dim(cells, 0, width, axis=dim)
        tail = lax.slice_in_dim(cells, cells.shape[dim] - width, cells.shape[dim], axis=dim)
        cells = jnp.concatenate(
            [
                lax.ppermute(tail, axis, [(i, (i + 1) % count) for i in range(count)]),
                cells,
                lax.ppermute(head, axis, [((i + 1) % count, i) for i in range(count)]),
            ],
            axis=dim,
        )
    return cells


def local(
    bond_state,
    block_fill,
    w_in,
    w_down,
    pair_coef,
    pair_source,
    pair_owner,
    pair_target,
    w_gate,
    w_atom_in,
    atom_state,
    w_atom,
    bond_ends,
    w_left,
    w_right,
):
    bond_slots = bond_state.shape[0]
    blocks = block_fill.shape[0]
    block_size = bond_slots // blocks
    pair_count = pair_source.shape[0]
    spaces = lax.axis_size("space")
    feat_count = lax.axis_size("feat")
    capacity = max(2, min(blocks, 2 * pair_count // spaces))
    channels = w_down.shape[1]
    own_channels = channels // feat_count
    atom_cols = atom_state.shape[1]
    contract_first = (((0,), (0,)), ((), ()))
    position = lax.broadcasted_iota(jnp.int32, (blocks, block_size), 1)
    real_mask = (position < block_fill[:, None]).astype(jnp.float32).reshape(bond_slots)
    pre_hidden = jnp.dot(
        gathered_copies(bond_state, "feat", 1), w_in, preferred_element_type=jnp.float32
    )
    hidden = jax.nn.silu(pre_hidden).astype(jnp.bfloat16)
    partial_term = lax.dot_general(
        w_down, hidden, (((0,), (1,)), ((), ())), preferred_element_type=jnp.float32
    )
    angular = sum_at_owner(partial_term * real_mask[None, :], "feat", 0).astype(jnp.bfloat16)
    angular_blocks = angular.reshape(own_channels, blocks, block_size)
    sources = jnp.take(angular_blocks, pair_source, axis=1)
    contrib = jnp.einsum(
        "cpj,pij->pci", sources, pair_coef, preferred_element_type=jnp.float32
    ).astype(jnp.bfloat16)
    owner_ids = pair_owner[:, 0]
    owner_table = (
        owner_ids[:, None] == lax.broadcasted_iota(jnp.int32, (pair_count, spaces), 1)
    ).astype(jnp.int32)
    slot_rank = jnp.sum(jnp.cumsum(owner_table, axis=0) * owner_table, axis=1) - 1
    flat_slot = owner_ids * capacity + slot_rank
    outgoing = (
        jnp.zeros((spaces * capacity, own_channels, block_size), jnp.bfloat16)
        .at[flat_slot]
        .set(contrib)
    )
    labels = jnp.full((spaces * capacity,), blocks, jnp.int32).at[flat_slot].set(pair_target)
    incoming, arrived = (
        lax.all_to_all(
            outgoing.reshape(spaces, capacity, own_channels, block_size),
            "space",
            split_axis=0,
            concat_axis=0,
            tiled=True,
        ),
        lax.all_to_all(
            labels.reshape(spaces, capacity), "space", split_axis=0, concat_axis=0, tiled=True
        ),
    )
    chooser = (
        arrived.reshape(spaces * capacity)[None, :]
        == lax.broadcasted_iota(jnp.int32, (blocks, spaces * capacity), 0)
    ).astype(jnp.bfloat16)
    block_sums = jnp.einsum(
        "kq,qcr->ckr",
        chooser,
        incoming.reshape(spaces * capacity, own_channels, block_size),
        preferred_element_type=jnp.float32,
    )
    message = (block_sums.reshape(own_channels, bond_slots) * real_mask[None, :]).astype(
        jnp.bfloat16
    )
    shard_piece = lax.all_gather(message, "feat", axis=0, tiled=True)
    gate_pre = lax.dot_general(
        shard_piece, w_gate, contract_first, preferred_element_type=jnp.float32
    )
    to_atoms = lax.dot_general(
        shard_piece, w_atom_in, contract_first, preferred_element_type=jnp.float32
    )
    window = 3 * atom_cols
    window_sums = jax.ops.segment_sum(to_atoms, bond_ends[1], num_segments=window).T
    window_counts = jax.ops.segment_sum(real_mask, bond_ends[1], num_segments=window)
    from_upper = (
        passed_along(window_sums[:, :atom_cols].astype(jnp.bfloat16), "space", -1).astype(
            jnp.float32
        ),
        passed_along(window_counts[:atom_cols].astype(jnp.bfloat16), "space", -1).astype(
            jnp.float32
        ),
    )
    from_lower = (
        passed_along(window_sums[:, 2 * atom_cols :].astype(jnp.bfloat16), "space", 1).astype(
            jnp.float32
        ),
        passed_along(window_counts[2 * atom_cols :].astype(jnp.bfloat16), "space", 1).astype(
            jnp.float32
        ),
    )
    atom_sums = window_sums[:, atom_cols : 2 * atom_cols] + from_upper[0] + from_lower[0]
    atom_counts = window_counts[atom_cols : 2 * atom_cols] + from_upper[1] + from_lower[1]
    mean_in = (atom_sums / jnp.maximum(atom_counts, 1.0)[None, :]).astype(jnp.bfloat16)
    partial_pre = lax.dot_general(
        w_atom, mean_in, contract_first, preferred_element_type=jnp.float32
    )
    own_pre = sum_at_owner_2(partial_pre.astype(jnp.bfloat16), "feat", 0)
    atom_out = (atom_state + jax.nn.silu(own_pre)).astype(jnp.bfloat16)
    own_window = extended(atom_out, (("space", 1),), atom_cols)
    neighbours = lax.all_gather(own_window, "feat", axis=0, tiled=True)
    left_rows = jnp.take(neighbours, bond_ends[0], axis=1)
    right_rows = jnp.take(neighbours, bond_ends[1], axis=1)
    mixed_atoms = lax.dot_general(
        left_rows, w_left, contract_first, preferred_element_type=jnp.float32
    ) + lax.dot_general(right_rows, w_right, contract_first, preferred_element_type=jnp.float32)
    update = jax.nn.sigmoid(gate_pre) * (hidden.astype(jnp.float32) + jax.nn.silu(mixed_atoms))
    bond_out = (bond_state + real_mask[:, None] * update).astype(jnp.bfloat16)
    return (bond_out, atom_out)


def solution(mesh):
    placed = (
        P("space", "feat"),
        P("space"),
        P(None, "feat"),
        P("feat", None),
        P("space", None, None),
        P("space"),
        P("space", None),
        P("space"),
        P(None, "feat"),
        P(None, "feat"),
        P("feat", "space"),
        P("feat", None),
        P(None, "space"),
        P(None, "feat"),
        P(None, "feat"),
    )
    return jax.shard_map(
        local,
        mesh=mesh,
        in_specs=placed,
        out_specs=(P("space", "feat"), P("feat", "space")),
        check_vma=False,
    )
```

profile of v0, /device:TPU:6, one launch (start us, length us, event | category | flops | bytes accessed | tf_op | source)
XLA Modules:
  0.0 237.2 jit_solution(6017705378401330278)
XLA Ops:
  0.6 1.3 copy.30
  1.9 1.6 broadcast_in_dim.42
  3.5 4.6 %all-to-all-start = ((bf16[4,2048,128]{1,2,0:T(8,128)(2,1)}), bf16[4,2048,128]{1,2,0:T(8,128)(2,1)S(1)}, u32[]{:S(2)}, u32[]{:S(2)}) async-start(bf16[4,2048,128]{1,2,0:T(8,128)(2,1)} %broadcast_in_dim.42), calls=%async_computation | async-start | bytes 4194304 | tf_op jit(solution)/shard_map/all_to_all | solution.py:9
  8.7 25.8 %all-to-all-done = bf16[4,2048,128]{1,2,0:T(8,128)(2,1)S(1)} async-done(((bf16[4,2048,128]{1,2,0:T(8,128)(2,1)}), bf16[4,2048,128]{1,2,0:T(8,128)(2,1)S(1)}, u32[]{:S(2)}, u32[]{:S(2)}) %all-to-all-start) | async-done | bytes 2097184 | tf_op jit(solution)/shard_map/all_to_all | solution.py:9
  35.3 1.3 convolution_multiply_fusion
  36.5 3.5 %all-to-all-start.1 = ((f32[4,16,2048]{2,1,0:T(8,128)}), f32[4,16,2048]{2,1,0:T(8,128)S(1)}, u32[]{:S(2)}, u32[]{:S(2)}) async-start(f32[4,16,2048]{2,1,0:T(8,128)} %bitcast.7), calls=%async_computation.1 | async-start | bytes 1048576 | tf_op jit(solution)/shard_map/all_to_all | solution.py:31
  40.0 1.1 scatter_custom_fusion.1
  41.9 6.7 %all-to-all-done.1 = f32[4,16,2048]{2,1,0:T(8,128)S(1)} async-done(((f32[4,16,2048]{2,1,0:T(8,128)}), f32[4,16,2048]{2,1,0:T(8,128)S(1)}, u32[]{:S(2)}, u32[]{:S(2)}) %all-to-all-start.1) | async-done | bytes 524320 | tf_op jit(solution)/shard_map/all_to_all | solution.py:31
  48.6 19.4 %all-to-all-start.3 = ((s32[128,1,2]{2,1,0:T(1,128)}), s32[128,1,2]{2,1,0:T(1,128)S(1)}, u32[]{:S(2)}, u32[]{:S(2)}) async-start(s32[128,1,2]{2,1,0:T(1,128)} %bitcast.11), calls=%async_computation.3 | async-start | bytes 131072 | tf_op jit(solution)/shard_map/all_to_all | solution.py:126
  68.7 4.1 %convolution_convert_fusion = bf16[112,16,128]{2,1,0:T(8,128)(2,1)S(1)} fusion(bf16[112,128,128]{2,1,0:T(8,128)(2,1)} %param.21, bf16[112,16,128]{2,1,0:T(8,128)(2,1)S(1)} %gather_fusion, pred[112]{0:T(512)(128)(4,1)S(1)} %compare_and_fusion.2), kind=kOutput, calls=%fused_computation.17 | convolution fusion | flops 59179008 | bytes 4587632 | tf_op jit(solution)/shard_map/cpj,pij->pci/dot_general | solution.py:103
  73.0 3.9 %scatter_fusion = bf16[256,16,128]{2,1,0:T(8,128)(2,1)S(1)} fusion(bf16[256,16,128]{2,1,0:T(8,128)(2,1)S(1)} %broadcast_in_dim.40, s32[112]{0:T(128)S(1)} %fusion.39, bf16[112,16,128]{2,1,0:T(8,128)(2,1)S(1)} %convolution_convert_fusion), kind=kCustom, calls=%fused_computation.3 | custom fusion | bytes 1376704 | tf_op jit(solution)/shard_map/scatter | solution.py:115
  76.9 1.9 copy.32
  78.7 2.9 %all-to-all-done.3 = s32[128,1,2]{2,1,0:T(1,128)S(1)} async-done(((s32[128,1,2]{2,1,0:T(1,128)}), s32[128,1,2]{2,1,0:T(1,128)S(1)}, u32[]{:S(2)}, u32[]{:S(2)}) %all-to-all-start.3) | async-done | bytes 1056 | tf_op jit(solution)/shard_map/all_to_all | solution.py:126
  81.6 13.2 %all-to-all-start.2 = ((bf16[128,2,16,128]{3,1,2,0:T(2,128)(2,1)}), bf16[128,2,16,128]{3,1,2,0:T(2,128)(2,1)S(1)}, u32[]{:S(2)}, u32[]{:S(2)}) async-start(bf16[128,2,16,128]{3,1,2,0:T(2,128)(2,1)} %copy.32), calls=%async_computation.2 | async-start | bytes 2097152 | tf_op jit(solution)/shard_map/all_to_all | solution.py:119
  94.9 13.1 %scatter_custom_fusion.3 = f32[1536]{0:T(1024)S(1)} fusion(s32[2048]{0:T(1024)S(1)} %bitcast.67, f32[2048]{0:T(1024)S(1)} %convert_bitcast_fusion.1, f32[]{:T(128)} %constant.34.clone.1), kind=kCustom, calls=%fused_computation.63 | custom fusion | flops 2048 | bytes 6148 | tf_op jit(solution)/shard_map/scatter-add | solution.py:152
  108.0 2.5 %collective-permute-start.2 = (bf16[512]{0:T(512)(128)(2,1)S(1)}, bf16[512]{0:T(512)(128)(2,1)S(1)}, u32[]{:S(2)}, u32[]{:S(2)}) collective-permute-start(bf16[512]{0:T(512)(128)(2,1)S(1)} %get-tuple-element.13), channel_id=1, source_target_pairs={{0,508},{4,0},{8,4},{12,8},{16,12},{20,16},{24,20},{28,24},{32,28}... | collective-permute-start | bytes 3080 | tf_op jit(solution)/shard_map/ppermute | solution.py:38
  110.5 1.9 collective-permute-start.3
  113.9 35.5 %all-to-all-done.2 = bf16[128,2,16,128]{3,1,2,0:T(2,128)(2,1)S(1)} async-done(((bf16[128,2,16,128]{3,1,2,0:T(2,128)(2,1)}), bf16[128,2,16,128]{3,1,2,0:T(2,128)(2,1)S(1)}, u32[]{:S(2)}, u32[]{:S(2)}) %all-to-all-start.2) | async-done | bytes 1048608 | tf_op jit(solution)/shard_map/all_to_all | solution.py:119
  150.7 12.6 %all_gather.6 = bf16[64,2048]{1,0:T(8,128)(2,1)S(1)} all-gather(bf16[16,2048]{1,0:T(8,128)(2,1)S(1)} %fusion.26), channel_id=1, replica_groups=mesh['space'=128,'feat'=4] {'feat'}, dimensions={0}, use_global_device_ids=true | all-gather | bytes 327680 | tf_op jit(solution)/shard_map/all_gather | solution.py:143
  163.6 11.7 %scatter_custom_fusion.2 = f32[1536,64]{1,0:T(8,128)S(1)} fusion(s32[2048]{0:T(1024)S(1)} %bitcast.69, f32[2048,64]{1,0:T(8,128)S(1)} %fusion.49, f32[]{:T(128)} %constant.34.clone.1), kind=kCustom, calls=%fused_computation.33 | custom fusion | flops 131072 | bytes 393220 | tf_op jit(solution)/shard_map/scatter-add | solution.py:151
  175.4 1.9 collective-permute-start
  177.3 2.4 %collective-permute-start.1 = (bf16[64,512]{0,1:T(8,128)(2,1)S(1)}, bf16[64,512]{0,1:T(8,128)(2,1)S(1)}, u32[]{:S(2)}, u32[]{:S(2)}) collective-permute-start(bf16[64,512]{0,1:T(8,128)(2,1)S(1)} %get-tuple-element.10), channel_id=1, source_target_pairs={{0,4},{4,8},{8,12},{12,16},{16,20},{20,24},{24,28},{28,32},{32,36}... | collective-permute-start | bytes 196616 | tf_op jit(solution)/shard_map/ppermute | solution.py:38
  179.8 3.8 %collective-permute-done.1 = bf16[64,512]{0,1:T(8,128)(2,1)S(1)} collective-permute-done((bf16[64,512]{0,1:T(8,128)(2,1)S(1)}, bf16[64,512]{0,1:T(8,128)(2,1)S(1)}, u32[]{:S(2)}, u32[]{:S(2)}) %collective-permute-start.1) | collective-permute-done | bytes 65568 | tf_op jit(solution)/shard_map/ppermute | solution.py:38
  184.7 3.4 %all-to-all-start.4 = ((bf16[4,64,512]{2,1,0:T(8,128)(2,1)}), bf16[4,64,512]{2,1,0:T(8,128)(2,1)S(1)}, u32[]{:S(2)}, u32[]{:S(2)}) async-start(bf16[4,64,512]{2,1,0:T(8,128)(2,1)} %bitcast.18), calls=%async_computation.4 | async-start | bytes 524288 | tf_op jit(solution)/shard_map/all_to_all | solution.py:43
  188.1 6.7 %all-to-all-done.4 = bf16[4,64,512]{2,1,0:T(8,128)(2,1)S(1)} async-done(((bf16[4,64,512]{2,1,0:T(8,128)(2,1)}), bf16[4,64,512]{2,1,0:T(8,128)(2,1)S(1)}, u32[]{:S(2)}, u32[]{:S(2)}) %all-to-all-start.4) | async-done | bytes 262176 | tf_op jit(solution)/shard_map/all_to_all | solution.py:43
  194.9 1.9 collective-permute-start.4
  196.9 3.6 %collective-permute-start.5 = (bf16[64,512]{1,0:T(8,128)(2,1)S(1)}, bf16[64,512]{1,0:T(8,128)(2,1)S(1)}, u32[]{:S(2)}, u32[]{:S(2)}) collective-permute-start(bf16[64,512]{1,0:T(8,128)(2,1)S(1)} %add_convert_fusion), channel_id=1, source_target_pairs={{4,0},{8,4},{12,8},{16,12},{20,16},{24,20},{28,24},{32,28},{36,32}... | collective-permute-start | bytes 196616 | tf_op jit(solution)/shard_map/ppermute | solution.py:56
  200.5 3.1 %collective-permute-done.5 = bf16[64,512]{1,0:T(8,128)(2,1)S(1)} collective-permute-done((bf16[64,512]{1,0:T(8,128)(2,1)S(1)}, bf16[64,512]{1,0:T(8,128)(2,1)S(1)}, u32[]{:S(2)}, u32[]{:S(2)}) %collective-permute-start.5) | collective-permute-done | bytes 65568 | tf_op jit(solution)/shard_map/ppermute | solution.py:56
  203.6 14.3 %all_gather.7 = bf16[256,1536]{1,0:T(8,128)(2,1)S(1)} all-gather(bf16[64,1536]{1,0:T(8,128)(2,1)S(1)} %pad_maximum_fusion), channel_id=1, replica_groups=mesh['space'=128,'feat'=4] {'feat'}, dimensions={0}, use_global_device_ids=true | all-gather | bytes 983040 | tf_op jit(solution)/shard_map/all_gather | solution.py:178
  218.2 7.5 %gather_fusion.1 = bf16[2048,256]{1,0:T(8,128)(2,1)S(1)} fusion(bf16[256,1536]{0,1:T(8,128)(2,1)S(1)} %copy.36, s32[2048]{0:T(1024)S(1)} %fusion.33), kind=kCustom, calls=%fused_computation.clone | custom fusion | bytes 2105344 | tf_op jit(solution)/shard_map/jit(_take)/gather | solution.py:179
  225.7 7.5 %gather_fusion.2 = bf16[2048,256]{1,0:T(8,128)(2,1)S(1)} fusion(bf16[256,1536]{0,1:T(8,128)(2,1)S(1)} %copy.36, s32[2048]{0:T(1024)S(1)} %fusion.34), kind=kCustom, calls=%fused_computation.1.clone | custom fusion | bytes 2105344 | tf_op jit(solution)/shard_map/jit(_take)/gather | solution.py:180
  235.4 1.8 fusion.6
  (74 shorter events, 9.8 us)
Async XLA Ops:
  0.6 33.8 %copy-start = (bf16[512,128]{1,0:T(8,128)(2,1)S(1)}, bf16[512,128]{1,0:T(8,128)(2,1)}, u32[]{:S(2)}) copy-start(bf16[512,128]{1,0:T(8,128)(2,1)} %param.19) | copy-start | bytes 393220
  3.5 4.6 %copy-start.10 = (s32[112,1]{0,1:T(1,128)S(1)}, s32[112,1]{0,1:T(1,128)}, u32[]{:S(2)}) copy-start(s32[112,1]{0,1:T(1,128)} %param.23) | copy-start | bytes 1348
  3.5 5.0 %copy-start.11 = (s32[16]{0:T(128)S(1)}, s32[16]{0:T(128)}, u32[]{:S(2)}) copy-start(s32[16]{0:T(128)} %param.18) | copy-start | bytes 196
  3.5 30.9 %all-to-all-start = ((bf16[4,2048,128]{1,2,0:T(8,128)(2,1)}), bf16[4,2048,128]{1,2,0:T(8,128)(2,1)S(1)}, u32[]{:S(2)}, u32[]{:S(2)}) async-start(bf16[4,2048,128]{1,2,0:T(8,128)(2,1)} %broadcast_in_dim.42), calls=%async_computation | async-start | bytes 4194304 | tf_op jit(solution)/shard_map/all_to_all | solution.py:9
  34.5 0.7 copy-start.13
  35.2 1.3 copy-start.1
  35.2 4.8 %copy-start.15 = (s32[112]{0:T(128)S(1)}, s32[112]{0:T(128)}, u32[]{:S(2)}) copy-start(s32[112]{0:T(128)} %param.22) | copy-start | bytes 1348
  36.5 12.1 %all-to-all-start.1 = ((f32[4,16,2048]{2,1,0:T(8,128)}), f32[4,16,2048]{2,1,0:T(8,128)S(1)}, u32[]{:S(2)}, u32[]{:S(2)}) async-start(f32[4,16,2048]{2,1,0:T(8,128)} %bitcast.7), calls=%async_computation.1 | async-start | bytes 1048576 | tf_op jit(solution)/shard_map/all_to_all | solution.py:31
  48.6 33.0 %all-to-all-start.3 = ((s32[128,1,2]{2,1,0:T(1,128)}), s32[128,1,2]{2,1,0:T(1,128)S(1)}, u32[]{:S(2)}, u32[]{:S(2)}) async-start(s32[128,1,2]{2,1,0:T(1,128)} %bitcast.11), calls=%async_computation.3 | async-start | bytes 131072 | tf_op jit(solution)/shard_map/all_to_all | solution.py:126
  76.9 18.0 %copy-start.8 = (s32[2,2048]{1,0:T(2,128)S(1)}, s32[2,2048]{1,0:T(2,128)}, u32[]{:S(2)}) copy-start(s32[2,2048]{1,0:T(2,128)} %param.29) | copy-start | bytes 49156
  81.6 67.8 %all-to-all-start.2 = ((bf16[128,2,16,128]{3,1,2,0:T(2,128)(2,1)}), bf16[128,2,16,128]{3,1,2,0:T(2,128)(2,1)S(1)}, u32[]{:S(2)}, u32[]{:S(2)}) async-start(bf16[128,2,16,128]{3,1,2,0:T(2,128)(2,1)} %copy.32), calls=%async_computation.2 | async-start | bytes 2097152 | tf_op jit(solution)/shard_map/all_to_all | solution.py:119
  94.9 68.4 %copy-start.9 = (bf16[64,64]{1,0:T(8,128)(2,1)S(1)}, bf16[64,64]{1,0:T(8,128)(2,1)}, u32[]{:S(2)}) copy-start(bf16[64,64]{1,0:T(8,128)(2,1)} %param.26) | copy-start | bytes 24580
  108.0 71.8 %collective-permute-start.2 = (bf16[512]{0:T(512)(128)(2,1)S(1)}, bf16[512]{0:T(512)(128)(2,1)S(1)}, u32[]{:S(2)}, u32[]{:S(2)}) collective-permute-start(bf16[512]{0:T(512)(128)(2,1)S(1)} %get-tuple-element.13), channel_id=1, source_target_pairs={{0,508},{4,0},{8,4},{12,8},{16,12},{20,16},{24,20},{28,24},{32,28}... | collective-permute-start | bytes 3080 | tf_op jit(solution)/shard_map/ppermute | solution.py:38
  110.5 69.2 %collective-permute-start.3 = (bf16[512]{0:T(512)(128)(2,1)S(1)}, bf16[512]{0:T(512)(128)(2,1)S(1)}, u32[]{:S(2)}, u32[]{:S(2)}) collective-permute-start(bf16[512]{0:T(512)(128)(2,1)S(1)} %get-tuple-element.14), channel_id=1, source_target_pairs={{0,4},{4,8},{8,12},{12,16},{16,20},{20,24},{24,28},{28,32},{32,36}... | collective-permute-start | bytes 3080 | tf_op jit(solution)/shard_map/ppermute | solution.py:38
  150.7 32.9 %copy-start.12 = (bf16[64,256]{1,0:T(8,128)(2,1)S(1)}, bf16[64,256]{1,0:T(8,128)(2,1)}, u32[]{:S(2)}) copy-start(bf16[64,256]{1,0:T(8,128)(2,1)} %param.28) | copy-start | bytes 98308
  175.3 19.6 %copy-start.7 = (bf16[64,512]{1,0:T(8,128)(2,1)S(1)}, bf16[64,512]{1,0:T(8,128)(2,1)}, u32[]{:S(2)}) copy-start(bf16[64,512]{1,0:T(8,128)(2,1)} %param.27) | copy-start | bytes 196612
  175.4 4.4 %collective-permute-start = (bf16[64,512]{0,1:T(8,128)(2,1)S(1)}, bf16[64,512]{0,1:T(8,128)(2,1)S(1)}, u32[]{:S(2)}, u32[]{:S(2)}) collective-permute-start(bf16[64,512]{0,1:T(8,128)(2,1)S(1)} %get-tuple-element.9), channel_id=1, source_target_pairs={{0,508},{4,0},{8,4},{12,8},{16,12},{20,16},{24,20},{28,24},{32,28}... | collective-permute-start | bytes 196616 | tf_op jit(solution)/shard_map/ppermute | solution.py:38
  177.3 6.3 %collective-permute-start.1 = (bf16[64,512]{0,1:T(8,128)(2,1)S(1)}, bf16[64,512]{0,1:T(8,128)(2,1)S(1)}, u32[]{:S(2)}, u32[]{:S(2)}) collective-permute-start(bf16[64,512]{0,1:T(8,128)(2,1)S(1)} %get-tuple-element.10), channel_id=1, source_target_pairs={{0,4},{4,8},{8,12},{12,16},{16,20},{20,24},{24,28},{28,32},{32,36}... | collective-permute-start | bytes 196616 | tf_op jit(solution)/shard_map/ppermute | solution.py:38
  184.7 10.1 %all-to-all-start.4 = ((bf16[4,64,512]{2,1,0:T(8,128)(2,1)}), bf16[4,64,512]{2,1,0:T(8,128)(2,1)S(1)}, u32[]{:S(2)}, u32[]{:S(2)}) async-start(bf16[4,64,512]{2,1,0:T(8,128)(2,1)} %bitcast.18), calls=%async_computation.4 | async-start | bytes 524288 | tf_op jit(solution)/shard_map/all_to_all | solution.py:43
  194.9 30.8 %copy-start.4 = (bf16[64,512]{1,0:T(8,128)(2,1)}, bf16[64,512]{1,0:T(8,128)(2,1)S(1)}, u32[]{:S(2)}) copy-start(bf16[64,512]{1,0:T(8,128)(2,1)S(1)} %add_convert_fusion) | copy-start | bytes 196612
  194.9 5.6 %collective-permute-start.4 = (bf16[64,512]{1,0:T(8,128)(2,1)S(1)}, bf16[64,512]{1,0:T(8,128)(2,1)S(1)}, u32[]{:S(2)}, u32[]{:S(2)}) collective-permute-start(bf16[64,512]{1,0:T(8,128)(2,1)S(1)} %add_convert_fusion), channel_id=1, source_target_pairs={{0,4},{4,8},{8,12},{12,16},{16,20},{20,24},{24,28},{28,32},{32,36}... | collective-permute-start | bytes 196616 | tf_op jit(solution)/shard_map/ppermute | solution.py:54
  196.9 6.8 %collective-permute-start.5 = (bf16[64,512]{1,0:T(8,128)(2,1)S(1)}, bf16[64,512]{1,0:T(8,128)(2,1)S(1)}, u32[]{:S(2)}, u32[]{:S(2)}) collective-permute-start(bf16[64,512]{1,0:T(8,128)(2,1)S(1)} %add_convert_fusion), channel_id=1, source_target_pairs={{4,0},{8,4},{12,8},{16,12},{20,16},{24,20},{28,24},{32,28},{36,32}... | collective-permute-start | bytes 196616 | tf_op jit(solution)/shard_map/ppermute | solution.py:56
  225.7 7.5 %copy-start.5 = (bf16[256,128]{1,0:T(8,128)(2,1)S(1)}, bf16[256,128]{1,0:T(8,128)(2,1)}, u32[]{:S(2)}) copy-start(bf16[256,128]{1,0:T(8,128)(2,1)} %param.30) | copy-start | bytes 196612
  233.2 0.8 copy-start.6
  234.0 1.2 copy-start.2
  234.0 1.4 copy-start.3
  234.1 1.4 copy-start.14
where the time goes:
time: 241 us; the launch traced here: 237 us
  waiting for transfers between devices  84.5 us (35%)
  starting transfers between devices  58.4 us (24%)
  local copies, waits for them, and re-layouts  29 us (12%)
  blocking collectives  26.8 us (11%)
  other arithmetic  26.3 us (11%)
  matrix products  11 us (5%)
    all_to_all x1, waiting for transfers between devices, local(): lax.all_to_all(outgoing.reshape(spaces, capacity, own_channels, block_siz...  35.5 us
    all_to_all x1, waiting for transfers between devices, copy_for_each(): return lax.all_to_all(copies, axis, split_axis=0, concat_axis=0, tiled=True)  25.8 us
    all_to_all x1, starting transfers between devices, local(): lax.all_to_all(labels.reshape(spaces, capacity), 'space', split_axis=0, c...  19.4 us
    all_gather x1, blocking collectives, local(): neighbours = lax.all_gather(own_window, 'feat', axis=0, tiled=True)  14.3 us
    all_to_all x1, starting transfers between devices, local(): lax.all_to_all(outgoing.reshape(spaces, capacity, own_channels, block_siz...  13.2 us
    scatter-add x1, other arithmetic, local(): jax.ops.segment_sum(real_mask, bond_ends[1], num_segments=window)  13.1 us
    all_gather x1, blocking collectives, local(): shard_piece = lax.all_gather(message, 'feat', axis=0, tiled=True)  12.6 us
    scatter-add x1, other arithmetic, local(): jax.ops.segment_sum(to_atoms, bond_ends[1], num_segments=window)  11.7 us
  transfers between devices with their start and end apart: 11, of which 7 were waited for; matrix products, arithmetic and copies ran while one was open for 17% of the time, Pallas kernels for 0%

commit v1 on v0

v1 whole, which is shorter than its diff:
```python
import functools

import jax
import jax.numpy as jnp
from jax import lax
from jax.experimental import pallas as pl
from jax.experimental.pallas import tpu as pltpu
from jax.sharding import PartitionSpec as P

BF16 = jnp.bfloat16
F32 = jnp.float32
BLOCK = 128
LANES = 128
SLOTS = 2
SPAN = 4
HALO = 3
LEFT_FIRST = (((0,), (0,)), ((), ()))
BOTH_LAST = (((1,), (1,)), ((), ()))


def vmem():
    return pl.BlockSpec(memory_space=pltpu.VMEM)


def smem():
    return pl.BlockSpec(memory_space=pltpu.SMEM)


def dot(a, b, dims):
    return lax.dot_general(a, b, dims, preferred_element_type=F32)


def exchanged(value, axis, groups=None):
    return lax.all_to_all(
        value, axis, split_axis=0, concat_axis=0, tiled=True, axis_index_groups=groups
    )


def for_each(value, axis):
    return jnp.broadcast_to(value, (lax.axis_size(axis), *value.shape))


def angular_body(fill_ref, place_ref, x_ref, w_ref, down_ref, hidden_ref, angular_ref):
    quarters = x_ref.shape[0]
    own_blocks = angular_ref.shape[1]
    channels = angular_ref.shape[2]
    first = place_ref[0] * own_blocks
    x = jnp.concatenate([x_ref[k] for k in range(quarters)], axis=1)
    total = None
    for q in range(quarters):
        pre = jnp.dot(x, w_ref[q], preferred_element_type=F32)
        hidden = jax.nn.silu(pre).astype(BF16)
        hidden_ref[q] = hidden
        part = dot(down_ref[q], hidden, BOTH_LAST)
        total = part if total is None else total + part
    for b in range(own_blocks):
        piece = total[:, b * BLOCK : (b + 1) * BLOCK]
        real = lax.broadcasted_iota(jnp.int32, piece.shape, 1) < fill_ref[first + b]
        piece = jnp.where(real, piece, 0.0).astype(BF16)
        for q in range(quarters):
            angular_ref[q, b] = piece[q * channels : (q + 1) * channels]


def angular_call(fill, place, x, w, down, own_blocks):
    quarters, bonds, width = x.shape
    channels = down.shape[1] // quarters
    return pl.pallas_call(
        angular_body,
        out_shape=(
            jax.ShapeDtypeStruct((quarters, bonds, w.shape[2]), BF16),
            jax.ShapeDtypeStruct((quarters, own_blocks, channels, BLOCK), BF16),
        ),
        in_specs=[smem(), smem(), vmem(), vmem(), vmem()],
        out_specs=(vmem(), vmem()),
        cost_estimate=pl.CostEstimate(
            flops=600_000_000, bytes_accessed=2_000_000, transcendentals=262_144
        ),
        name="angular",
    )(fill, place, x, w, down)


def contribution_body(chunk, source_ref, slot_ref, angular_ref, coef_ref, out_ref):
    step = pl.program_id(0)

    @pl.when(step == 0)
    def _():
        out_ref[...] = jnp.zeros_like(out_ref)

    for k in range(chunk):
        pair = step * chunk + k
        part = dot(angular_ref[source_ref[pair]], coef_ref[k], BOTH_LAST)
        out_ref[slot_ref[pair]] = part.astype(BF16)


def contribution_call(sources, slots, angular, coef, slot_count):
    pairs = coef.shape[0]
    chunk = next(c for c in (16, 14, 8, 7, 4, 2, 1) if pairs % c == 0)
    blocks, channels, rows = angular.shape
    return pl.pallas_call(
        functools.partial(contribution_body, chunk),
        out_shape=jax.ShapeDtypeStruct((slot_count, channels, rows), BF16),
        grid=(pairs // chunk,),
        in_specs=[
            smem(),
            smem(),
            pl.BlockSpec(angular.shape, lambda i: (0, 0, 0)),
            pl.BlockSpec((chunk, *coef.shape[1:]), lambda i: (i, 0, 0)),
        ],
        out_specs=pl.BlockSpec((slot_count, channels, rows), lambda i: (0, 0, 0)),
        cost_estimate=pl.CostEstimate(
            flops=60_000_000, bytes_accessed=5_000_000, transcendentals=0
        ),
        name="contribution",
    )(sources, slots, angular, coef)


def message_body(
    label_ref,
    fill_ref,
    place_ref,
    ends_ref,
    arrived_ref,
    message_ref,
    own_ref,
    near_ref,
    far_ref,
    sums,
    padded,
):
    blocks = fill_ref.shape[0]
    slots, channels, rows = arrived_ref.shape
    bonds = blocks * rows
    spans = HALO * SPAN
    sums[...] = jnp.zeros_like(sums)

    def add(step, carry):
        for k in range(8):
            slot = step * 8 + k
            label = label_ref[slot]
            sums[label] += arrived_ref[slot].astype(F32)
        return carry

    lax.fori_loop(0, slots // 8, add, 0)
    pieces = []
    masks = []
    for b in range(blocks):
        real = lax.broadcasted_iota(jnp.int32, (channels, rows), 1) < fill_ref[b]
        piece = jnp.where(real, sums[b], 0.0)
        message_ref[:, b * rows : (b + 1) * rows] = piece.astype(BF16)
        pieces.append(piece)
        masks.append(jnp.where(real[:1], 1.0, 0.0))
    message = jnp.concatenate(pieces, axis=1)
    mask = jnp.concatenate(masks, axis=1)
    ends = ends_ref[1:2, :]
    high = ends // LANES
    low = ends % LANES
    stacked = []
    tallies = []
    for h in range(spans):
        here = high == h
        stacked.append(jnp.where(here, message, 0.0).astype(BF16))
        tallies.append(jnp.where(here, mask, 0.0))
    tallies.append(jnp.zeros((16 - spans, bonds), F32))
    stacked.append(jnp.concatenate(tallies, axis=0).astype(BF16))
    chosen = jnp.where(
        low == lax.broadcasted_iota(jnp.int32, (LANES, bonds), 0), 1.0, 0.0
    ).astype(BF16)
    window = dot(jnp.concatenate(stacked, axis=0), chosen, BOTH_LAST)
    counts = window[spans * channels : spans * channels + spans]
    upper = jnp.floor(counts * (1.0 / 256.0))
    lower = counts - 256.0 * upper
    padded[...] = jnp.zeros_like(padded)
    width = SPAN * channels
    for k in range(HALO):
        group = jnp.concatenate(
            [
                window[k * width : (k + 1) * width],
                upper[k * SPAN : (k + 1) * SPAN],
                lower[k * SPAN : (k + 1) * SPAN],
            ],
            axis=0,
        )
        own_ref[k] = group
        padded[HALO + k] = group.astype(BF16)
    domain = place_ref[0]
    near = domain % 4
    far = (domain + 2) % 4
    for m in range(4):
        start = jnp.where(m == near, 0, m - near + HALO)
        across = (m < 2) != (far < 2)
        start_far = jnp.where(across, m - far + HALO, 0)
        for k in range(HALO):
            near_ref[m, k] = padded[start + k]
            far_ref[m, k] = padded[start_far + k]


def message_call(labels, fill, place, ends, arrived):
    slots, channels, rows = arrived.shape
    blocks = fill.shape[0]
    depth = SPAN * channels + 2 * SPAN
    return pl.pallas_call(
        message_body,
        out_shape=(
            jax.ShapeDtypeStruct((channels, blocks * rows), BF16),
            jax.ShapeDtypeStruct((HALO, depth, LANES), F32),
            jax.ShapeDtypeStruct((4, HALO, depth, LANES), BF16),
            jax.ShapeDtypeStruct((4, HALO, depth, LANES), BF16),
        ),
        in_specs=[smem(), smem(), smem(), vmem(), vmem()],
        out_specs=(vmem(), vmem(), vmem(), vmem()),
        scratch_shapes=[
            pltpu.VMEM((blocks + 1, channels, rows), F32),
            pltpu.VMEM((3 * HALO, depth, LANES), BF16),
        ],
        cost_estimate=pl.CostEstimate(
            flops=120_000_000, bytes_accessed=2_000_000, transcendentals=0
        ),
        name="message",
    )(labels, fill, place, ends, arrived)


def mean_body(own_ref, near_ref, far_ref, out_ref):
    copies = out_ref.shape[0]
    depth = own_ref.shape[1]
    channels = (depth - 2 * SPAN) // SPAN
    width = SPAN * channels
    for k in range(HALO):
        total = own_ref[k]
        for m in range(4):
            total += near_ref[m, k].astype(F32) + far_ref[m, k].astype(F32)
        for h in range(SPAN):
            count = 256.0 * total[width + h : width + h + 1]
            count += total[width + SPAN + h : width + SPAN + h + 1]
            mean = total[h * channels : (h + 1) * channels] / jnp.maximum(count, 1.0)
            mean = mean.astype(BF16)
            row = (k * SPAN + h) * channels
            for m in range(copies):
                out_ref[m, row : row + channels] = mean


def mean_call(own, near, far, copies):
    channels = (own.shape[1] - 2 * SPAN) // SPAN
    return pl.pallas_call(
        mean_body,
        out_shape=jax.ShapeDtypeStruct((copies, HALO * SPAN * channels, LANES), BF16),
        in_specs=[vmem()] * 3,
        out_specs=vmem(),
        cost_estimate=pl.CostEstimate(
            flops=1_000_000, bytes_accessed=600_000, transcendentals=0
        ),
        name="mean",
    )(own, near, far)


def update_body(
    fill_ref,
    place_ref,
    mean_ref,
    atoms_ref,
    left_ref,
    right_ref,
    gate_ref,
    message_ref,
    hidden_ref,
    bonds_ref,
    ends_ref,
    bond_out_ref,
    atom_out_ref,
    table_left,
    table_right,
    kept,
):
    quarters = mean_ref.shape[0]
    channels = message_ref.shape[1]
    features = atoms_ref.shape[1]
    window = HALO * SPAN * LANES
    inputs = quarters * features
    tile = 2 * LANES
    atom_dim = window
    states = jnp.concatenate(
        [atoms_ref[f, :, window : window + inputs] for f in range(quarters)], axis=0
    )
    sides = jnp.concatenate([left_ref[...], right_ref[...]], axis=1)
    width = left_ref.shape[1]
    own_start = window // HALO
    for c in range(window // tile):
        columns = slice(c * tile, (c + 1) * tile)
        mean = jnp.concatenate(
            [
                jnp.concatenate(
                    [
                        mean_ref[f, (2 * c + e) * channels : (2 * c + e + 1) * channels]
                        for f in range(quarters)
                    ],
                    axis=0,
                )
                for e in range(2)
            ],
            axis=1,
        )
        mean_in = jnp.concatenate(
            [
                dot(
                    atoms_ref[f, :, window + inputs : window + inputs + features],
                    mean,
                    LEFT_FIRST,
                ).astype(BF16)
                for f in range(quarters)
            ],
            axis=0,
        )
        pre = dot(states, mean_in, LEFT_FIRST)
        state = jnp.concatenate([atoms_ref[f, :, columns] for f in range(quarters)], axis=0)
        updated = (state.astype(F32) + jax.nn.silu(pre)).astype(BF16)
        place = c * tile - own_start
        if 0 <= place < own_start:
            kept[:, place : place + tile] = updated
        table = dot(updated, sides, LEFT_FIRST).astype(BF16)
        table_left[:, c * width : (c + 1) * width] = table[:, :width]
        table_right[:, c * width : (c + 1) * width] = table[:, width:]
    own = pl.multiple_of(place_ref[0] * features, features)
    atom_out_ref[...] = kept[pl.ds(own, features), :]
    bonds = bonds_ref.shape[0]
    per_quarter = bonds // quarters
    lane = lax.broadcasted_iota(jnp.int32, (tile, tile), 1)
    row = lax.broadcasted_iota(jnp.int32, (BLOCK, width), 0)
    for t in range(bonds // tile):
        rows = slice(t * tile, (t + 1) * tile)
        mixed = None
        for side, table in ((0, table_left), (1, table_right)):
            end = ends_ref[rows, side : side + 1]
            chosen = jnp.where(end % tile == lane, 1.0, 0.0).astype(BF16)
            found = jnp.dot(chosen, table[...], preferred_element_type=F32)
            high = jnp.broadcast_to(end // tile, (tile, width))
            for c in range(window // tile):
                part = jnp.where(high == c, found[:, c * width : (c + 1) * width], 0.0)
                mixed = part if mixed is None else mixed + part
        message = jnp.concatenate([message_ref[f, :, rows] for f in range(quarters)], axis=0)
        gate = dot(message, gate_ref[...], LEFT_FIRST)
        q = t * tile // per_quarter
        start = t * tile - q * per_quarter
        hidden = hidden_ref[q, start : start + tile].astype(F32)
        update = jax.nn.sigmoid(gate) * (hidden + jax.nn.silu(mixed))
        for e in range(tile // BLOCK):
            part = slice(e * BLOCK, (e + 1) * BLOCK)
            real = row < fill_ref[t * (tile // BLOCK) + e]
            here = slice(t * tile + e * BLOCK, t * tile + (e + 1) * BLOCK)
            bond_out_ref[here] = (
                bonds_ref[here].astype(F32) + jnp.where(real, update[part], 0.0)
            ).astype(BF16)


def update_call(fill, place, mean, atoms, left, right, gate, message, hidden, bonds, ends):
    features = atoms.shape[1]
    window = HALO * SPAN * LANES
    width = left.shape[1]
    tile = 2 * LANES
    return pl.pallas_call(
        update_body,
        out_shape=(
            jax.ShapeDtypeStruct(bonds.shape, BF16),
            jax.ShapeDtypeStruct((features, window // HALO), BF16),
        ),
        in_specs=[smem(), smem()] + [vmem()] * 9,
        out_specs=(vmem(), vmem()),
        scratch_shapes=[
            pltpu.VMEM((tile, window // tile * width), BF16),
            pltpu.VMEM((tile, window // tile * width), BF16),
            pltpu.VMEM((mean.shape[0] * features, window // HALO), BF16),
        ],
        cost_estimate=pl.CostEstimate(
            flops=2_500_000_000, bytes_accessed=4_000_000, transcendentals=2_000_000
        ),
        name="update",
    )(fill, place, mean, atoms, left, right, gate, message, hidden, bonds, ends)


def local(
    bond_state,
    block_fill,
    w_in,
    w_down,
    pair_coef,
    pair_source,
    pair_owner,
    pair_target,
    w_gate,
    w_atom_in,
    atom_state,
    w_atom,
    bond_ends,
    w_left,
    w_right,
):
    spaces = lax.axis_size("space")
    feats = lax.axis_size("feat")
    space = lax.axis_index("space").astype(jnp.int32).reshape(1)
    feat = lax.axis_index("feat").astype(jnp.int32).reshape(1)
    bonds, width = bond_state.shape
    blocks = block_fill.shape[0]
    pairs = pair_source.shape[0]
    near_groups = [[4 * i + k for k in range(4)] for i in range(spaces // 4)]
    far_groups = [[(4 * i + 2 + k) % spaces for k in range(4)] for i in range(spaces // 4)]

    x = exchanged(bond_state.reshape(feats, bonds // feats, width), "feat")
    w = exchanged(for_each(w_in, "feat"), "feat")
    down = exchanged(for_each(w_down.T, "feat"), "feat")
    hidden, angular = angular_call(block_fill, feat, x, w, down, blocks // feats)
    angular = exchanged(angular, "feat")
    angular = angular.reshape(blocks, *angular.shape[2:])

    owners = pair_owner[:, 0]
    before = lax.broadcasted_iota(jnp.int32, (pairs, pairs), 1) < lax.broadcasted_iota(
        jnp.int32, (pairs, pairs), 0
    )
    rank = jnp.sum(jnp.where(before & (owners[:, None] == owners[None, :]), 1, 0), axis=1)
    slots = owners * SLOTS + rank
    wanted = slots[:, None] == lax.broadcasted_iota(jnp.int32, (pairs, spaces * SLOTS), 1)
    labels = blocks + jnp.sum(jnp.where(wanted, pair_target[:, None] - blocks, 0), axis=0)
    outgoing = contribution_call(pair_source, slots, angular, pair_coef, spaces * SLOTS)
    outgoing, labels, hidden = lax.optimization_barrier((outgoing, labels, hidden))
    arrived = exchanged(outgoing.reshape(spaces, SLOTS, *outgoing.shape[1:]), "space")
    arrived = arrived.reshape(outgoing.shape)
    hidden = exchanged(hidden, "feat")
    upward = [(i, (i + 1) % spaces) for i in range(spaces)]
    downward = [((i + 1) % spaces, i) for i in range(spaces)]
    atom_near, labels = lax.optimization_barrier((atom_state, labels))
    pack = jnp.concatenate(
        [
            lax.ppermute(atom_near, "space", upward),
            atom_near,
            lax.ppermute(atom_near, "space", downward),
            w_atom,
            w_atom_in,
        ],
        axis=1,
    )
    pack = exchanged(for_each(pack, "feat"), "feat")
    labels = exchanged(labels.reshape(spaces, SLOTS), "space").reshape(spaces * SLOTS)

    message, own, near, far = message_call(labels, block_fill, space, bond_ends, arrived)
    near = exchanged(near, "space", near_groups)
    far = exchanged(far, "space", far_groups)
    message = exchanged(for_each(message, "feat"), "feat")
    mean = exchanged(mean_call(own, near, far, feats), "feat")
    return update_call(
        block_fill,
        feat,
        mean,
        pack,
        w_left,
        w_right,
        w_gate,
        message,
        hidden,
        bond_state,
        bond_ends.T,
    )


def solution(mesh):
    placed = (
        P("space", "feat"),
        P("space"),
        P(None, "feat"),
        P("feat", None),
        P("space", None, None),
        P("space"),
        P("space", None),
        P("space"),
        P(None, "feat"),
        P(None, "feat"),
        P("feat", "space"),
        P("feat", None),
        P(None, "space"),
        P(None, "feat"),
        P(None, "feat"),
    )
    return jax.shard_map(
        local,
        mesh=mesh,
        in_specs=placed,
        out_specs=(P("space", "feat"), P("feat", "space")),
        check_vma=False,
    )
```

time: 241 us -> 238 us (0.988)
  blocking collectives: 26.8 us -> 79.6 us
  starting transfers between devices: 58.4 us -> 33.4 us
  Pallas kernels: 0 us -> 24.9 us
  other arithmetic: 26.3 us -> 3.68 us
  local copies, waits for them, and re-layouts: 29 us -> 10.2 us
  matrix products: 11 us -> 0 us
    all_to_all x0 -> x5, blocking collectives: none -> 79.6 us  [exchanged(): lax.all_to_all(value, axis, split_axis=0, concat_axis=0, tiled=True, axis...]
    all_gather x2 -> x0, blocking collectives: 26.8 us -> none  [the longest x1 14.3 us: local(): neighbours = lax.all_gather(own_window, 'feat', axis=0, tiled=True)]
    pallas_call x0 -> x5, Pallas kernels: none -> 24.9 us  [the longest x1 8.83 us: update_call(): pl.pallas_call(update_body, out_shape=(jax.ShapeDtypeStruct(bonds.shape,...]
    scatter-add x2 -> x0, other arithmetic: 24.7 us -> none  [the longest x1 13.1 us: local(): jax.ops.segment_sum(real_mask, bond_ends[1], num_segments=window)]
    all_to_all x5 -> x7, starting transfers between devices: 44.1 us -> 27.9 us  [exchanged(): lax.all_to_all(value, axis, split_axis=0, concat_axis=0, tiled=True, axis...]
    gather x3 -> x0, local copies, waits for them, and re-layouts: 15.7 us -> none  [the longest x1 7.5 us: local(): right_rows = jnp.take(neighbours, bond_ends[1], axis=1)]
    dot_general x9 -> x0, matrix products: 11 us -> none  [the longest x1 4.08 us: local(): jnp.einsum('cpj,pij->pci', sources, pair_coef, preferred_element_type=jnp...]
    ppermute x6 -> x2, starting transfers between devices: 14.3 us -> 5.56 us  [the longest x1 3.53 us: local(): lax.ppermute(atom_near, 'space', downward)]
  transfers between devices with their start and end apart: 11 -> 9, of which waited for: 7 -> 9; matrix products, arithmetic and copies ran while one was open for 17% -> 3% of each run, Pallas kernels for 0% -> 2%
where the time goes in v1:
time: 238 us; the launch traced here: 237 us
  waiting for transfers between devices  84 us (35%)
  blocking collectives  79.6 us (33%)
  starting transfers between devices  33.4 us (14%)
  Pallas kernels  24.9 us (10%)
  local copies, waits for them, and re-layouts  10.2 us (4%)
  other arithmetic  3.68 us (2%)
    all_to_all x7, waiting for transfers between devices, exchanged(): lax.all_to_all(value, axis, split_axis=0, concat_axis=0, tiled=True, axis...  82.1 us
    all_to_all x5, blocking collectives, exchanged(): lax.all_to_all(value, axis, split_axis=0, concat_axis=0, tiled=True, axis...  79.6 us
    all_to_all x7, starting transfers between devices, exchanged(): lax.all_to_all(value, axis, split_axis=0, concat_axis=0, tiled=True, axis...  27.9 us
    pallas_call x1, Pallas kernels, update_call(): pl.pallas_call(update_body, out_shape=(jax.ShapeDtypeStruct(bonds.shape,...  8.83 us
    pallas_call x1, Pallas kernels, contribution_call(): pl.pallas_call(functools.partial(contribution_body, chunk), out_shape=jax...  6.98 us
    broadcast_in_dim x4, local copies, waits for them, and re-layouts, for_each(): return jnp.broadcast_to(value, (lax.axis_size(axis), *value.shape))  5.34 us
  transfers between devices with their start and end apart: 9, of which 9 were waited for; matrix products, arithmetic and copies ran while one was open for 3% of the time, Pallas kernels for 2%

profile of v1, /device:TPU:6, one launch (start us, length us, event | category | flops | bytes accessed | tf_op | source)
XLA Modules:
  0.0 236.6 jit_solution(1968724316281621176)
XLA Ops:
  1.4 10.0 %all_to_all.64.down_ref = bf16[4,64,128]{2,1,0:T(8,128)(2,1)} all-to-all(bf16[4,64,128]{2,1,0:T(8,128)(2,1)S(1)} %broadcast_in_dim.37), channel_id=1, replica_groups=mesh['space'=128,'feat'=4] {'feat'}, dimensions={0} | all-to-all | bytes 131072 | tf_op jit(solution)/shard_map/all_to_all | solution.py:34
  11.4 3.5 %all-to-all-start = ((bf16[4,512,128]{2,1,0:T(8,128)(2,1)}), bf16[4,512,128]{2,1,0:T(8,128)(2,1)S(1)}, u32[]{:S(2)}, u32[]{:S(2)}) async-start(bf16[4,512,128]{2,1,0:T(8,128)(2,1)} %bitcast.20), calls=%async_computation | async-start | bytes 1048576 | tf_op jit(solution)/shard_map/all_to_all | solution.py:34
  14.9 0.9 select_reduce_fusion.1
  16.4 6.7 %all-to-all-done.x_ref = bf16[4,512,128]{2,1,0:T(8,128)(2,1)S(1)} async-done(((bf16[4,512,128]{2,1,0:T(8,128)(2,1)}), bf16[4,512,128]{2,1,0:T(8,128)(2,1)S(1)}, u32[]{:S(2)}, u32[]{:S(2)}) %all-to-all-start) | async-done | bytes 524320 | tf_op jit(solution)/shard_map/all_to_all | solution.py:34
  23.1 1.9 broadcast_in_dim.36
  25.1 3.5 %all-to-all-start.1 = ((bf16[4,512,128]{2,1,0:T(8,128)(2,1)}), bf16[4,512,128]{2,1,0:T(8,128)(2,1)S(1)}, u32[]{:S(2)}, u32[]{:S(2)}) async-start(bf16[4,512,128]{2,1,0:T(8,128)(2,1)} %broadcast_in_dim.36), calls=%async_computation.1 | async-start | bytes 1048576 | tf_op jit(solution)/shard_map/all_to_all | solution.py:34
  29.3 7.3 %all-to-all-done.1.w_ref = bf16[4,512,128]{2,1,0:T(8,128)(2,1)S(1)} async-done(((bf16[4,512,128]{2,1,0:T(8,128)(2,1)}), bf16[4,512,128]{2,1,0:T(8,128)(2,1)S(1)}, u32[]{:S(2)}, u32[]{:S(2)}) %all-to-all-start.1) | async-done | bytes 524320 | tf_op jit(solution)/shard_map/all_to_all | solution.py:34
  37.4 3.3 %angular.1 = (bf16[4,512,128]{2,1,0:T(8,128)(2,1)}, bf16[4,4,16,128]{3,2,1,0:T(8,128)(2,1)}) custom-call(s32[16]{0:T(128)} %fill_ref.5, s32[1]{0:T(128)} %bitcast.place_ref, bf16[4,512,128]{2,1,0:T(8,128)(2,1)} %copy-done.2, bf16[4,512,128]{2,1,0:T(8,128)(2,1)} %copy-done.3, bf16[4,64,128]{2,1,0:T(8,128)(2,1)} %all_to_all.64.down_ref), custom_call_target="tpu_custom_call" | custom-call | flops 600000000 | bytes 2000000 | tf_op jit(solution)/shard_map/angular/pallas_call | solution.py:67
  40.7 3.4 %all-to-all-start.3 = ((bf16[4,4,16,128]{3,2,1,0:T(8,128)(2,1)}), bf16[4,4,16,128]{3,2,1,0:T(8,128)(2,1)S(1)}, u32[]{:S(2)}, u32[]{:S(2)}) async-start(bf16[4,4,16,128]{3,2,1,0:T(8,128)(2,1)} %get-tuple-element.13), calls=%async_computation.3 | async-start | bytes 131072 | tf_op jit(solution)/shard_map/all_to_all | solution.py:34
  44.7 5.1 %all-to-all-done.3 = bf16[4,4,16,128]{3,2,1,0:T(8,128)(2,1)S(1)} async-done(((bf16[4,4,16,128]{3,2,1,0:T(8,128)(2,1)}), bf16[4,4,16,128]{3,2,1,0:T(8,128)(2,1)S(1)}, u32[]{:S(2)}, u32[]{:S(2)}) %all-to-all-start.3) | async-done | bytes 65568 | tf_op jit(solution)/shard_map/all_to_all | solution.py:34
  50.4 7.0 %contribution.1 = bf16[256,16,128]{2,1,0:T(8,128)(2,1)} custom-call(s32[112]{0:T(128)} %source_ref.1, s32[112]{0:T(128)} %multiply_add_fusion.slot_ref, bf16[16,16,128]{2,1,0:T(8,128)(2,1)} %bitcast.22, bf16[112,128,128]{2,1,0:T(8,128)(2,1)} %coef_ref.1), custom_call_target="tpu_custom_call" | custom-call | flops 60000000 | bytes 5000000 | tf_op jit(solution)/shard_map/contribution/pallas_call | solution.py:99
  57.5 32.9 %all_to_all.65 = s32[128,1,2]{2,1,0:T(1,128)S(1)} all-to-all(s32[128,1,2]{2,1,0:T(1,128)S(1)} %bitcast.21), channel_id=1, replica_groups=mesh['space'=128,'feat'=4] {'space'}, dimensions={0} | all-to-all | bytes 2048 | tf_op jit(solution)/shard_map/all_to_all | solution.py:34
  90.4 12.8 %all_to_all.66.hidden_ref = bf16[4,512,128]{2,1,0:T(8,128)(2,1)} all-to-all(bf16[4,512,128]{2,1,0:T(8,128)(2,1)S(1)} %copy-done.4), channel_id=1, replica_groups=mesh['space'=128,'feat'=4] {'feat'}, dimensions={0} | all-to-all | bytes 1048576 | tf_op jit(solution)/shard_map/all_to_all | solution.py:34
  103.3 7.0 %all-to-all-start.5 = ((bf16[128,2,16,128]{3,2,1,0:T(8,128)(2,1)}), bf16[128,2,16,128]{3,2,1,0:T(8,128)(2,1)S(1)}, u32[]{:S(2)}, u32[]{:S(2)}) async-start(bf16[128,2,16,128]{3,2,1,0:T(8,128)(2,1)} %bitcast.18), calls=%async_computation.5 | async-start | bytes 2097152 | tf_op jit(solution)/shard_map/all_to_all | solution.py:34
  110.3 2.0 collective-permute-start
  112.3 3.5 %collective-permute-start.1 = (bf16[64,512]{1,0:T(8,128)(2,1)S(1)}, bf16[64,512]{1,0:T(8,128)(2,1)S(1)}, u32[]{:S(2)}, u32[]{:S(2)}) collective-permute-start(bf16[64,512]{1,0:T(8,128)(2,1)S(1)} %copy-done.9), channel_id=1, source_target_pairs={{4,0},{8,4},{12,8},{16,12},{20,16},{24,20},{28,24},{32,28},{36,32}... | collective-permute-start | bytes 196616 | tf_op jit(solution)/shard_map/ppermute | solution.py:432
  116.2 1.6 collective-permute-done.1
  117.9 44.9 %all-to-all-done.5 = bf16[128,2,16,128]{3,2,1,0:T(8,128)(2,1)S(1)} async-done(((bf16[128,2,16,128]{3,2,1,0:T(8,128)(2,1)}), bf16[128,2,16,128]{3,2,1,0:T(8,128)(2,1)S(1)}, u32[]{:S(2)}, u32[]{:S(2)}) %all-to-all-start.5) | async-done | bytes 1048608 | tf_op jit(solution)/shard_map/all_to_all | solution.py:34
  162.8 1.2 broadcast_in_dim.40
  163.9 3.5 %all-to-all-start.9 = ((bf16[4,64,1856]{2,1,0:T(8,128)(2,1)}), bf16[4,64,1856]{2,1,0:T(8,128)(2,1)S(1)}, u32[]{:S(2)}, u32[]{:S(2)}) async-start(bf16[4,64,1856]{2,1,0:T(8,128)(2,1)} %broadcast_in_dim.40), calls=%async_computation.9 | async-start | bytes 1966080 | tf_op jit(solution)/shard_map/all_to_all | solution.py:34
  169.4 3.9 %message.1 = (bf16[16,2048]{1,0:T(8,128)(2,1)}, f32[3,72,128]{2,1,0:T(8,128)}, bf16[4,3,72,128]{3,2,1,0:T(8,128)(2,1)}, bf16[4,3,72,128]{3,2,1,0:T(8,128)(2,1)}) custom-call(s32[256]{0:T(256)} %reshape.37.label_ref, s32[16]{0:T(128)} %fill_ref.5, s32[1]{0:T(128)} %bitcast.8.place_ref, s32[2,2048]{1,0:T(2,128)} %ends_ref.1, bf16[256,16,128]{2,1,0:T(8,128)(2,1)} %bitcast.17), custom_call_target="tpu_custom_call" | custom-call | flops 120000000 | bytes 2000000 | tf_op jit(solution)/shard_map/message/pallas_call | solution.py:201
  173.3 8.5 %all-to-all-done.9.atoms_ref = bf16[4,64,1856]{2,1,0:T(8,128)(2,1)S(1)} async-done(((bf16[4,64,1856]{2,1,0:T(8,128)(2,1)}), bf16[4,64,1856]{2,1,0:T(8,128)(2,1)S(1)}, u32[]{:S(2)}, u32[]{:S(2)}) %all-to-all-start.9) | async-done | bytes 950304 | tf_op jit(solution)/shard_map/all_to_all | solution.py:34
  181.9 11.2 %all_to_all.67.near_ref = bf16[4,3,72,128]{3,2,1,0:T(8,128)(2,1)} all-to-all(bf16[4,3,72,128]{3,2,1,0:T(8,128)(2,1)} %get-tuple-element.19), channel_id=1, replica_groups={{0,4,8,12},{16,20,24,28},{32,36,40,44},{48,52,56,60},{64,68,72,76},{80,..., dimensions={0} | all-to-all | bytes 442368 | tf_op jit(solution)/shard_map/all_to_all | solution.py:34
  193.1 12.6 %all_to_all.68.far_ref = bf16[4,3,72,128]{3,2,1,0:T(8,128)(2,1)} all-to-all(bf16[4,3,72,128]{3,2,1,0:T(8,128)(2,1)} %get-tuple-element.20), channel_id=1, replica_groups={{8,12,16,20},{24,28,32,36},{40,44,48,52},{56,60,64,68},{72,76,80,84},{8..., dimensions={0} | all-to-all | bytes 442368 | tf_op jit(solution)/shard_map/all_to_all | solution.py:34
  205.7 1.6 broadcast_in_dim.41
  207.3 3.4 %all-to-all-start.10 = ((bf16[4,16,2048]{2,1,0:T(8,128)(2,1)}), bf16[4,16,2048]{2,1,0:T(8,128)(2,1)S(1)}, u32[]{:S(2)}, u32[]{:S(2)}) async-start(bf16[4,16,2048]{2,1,0:T(8,128)(2,1)} %broadcast_in_dim.41), calls=%async_computation.10 | async-start | bytes 524288 | tf_op jit(solution)/shard_map/all_to_all | solution.py:34
  210.7 1.9 mean.1
  212.5 4.9 %all-to-all-done.10.message_ref = bf16[4,16,2048]{2,1,0:T(8,128)(2,1)S(1)} async-done(((bf16[4,16,2048]{2,1,0:T(8,128)(2,1)}), bf16[4,16,2048]{2,1,0:T(8,128)(2,1)S(1)}, u32[]{:S(2)}, u32[]{:S(2)}) %all-to-all-start.10) | async-done | bytes 262176 | tf_op jit(solution)/shard_map/all_to_all | solution.py:34
  217.4 3.5 %all-to-all-start.8 = ((bf16[4,192,128]{2,1,0:T(8,128)(2,1)}), bf16[4,192,128]{2,1,0:T(8,128)(2,1)S(1)}, u32[]{:S(2)}, u32[]{:S(2)}) async-start(bf16[4,192,128]{2,1,0:T(8,128)(2,1)} %mean.1), calls=%async_computation.8 | async-start | bytes 393216 | tf_op jit(solution)/shard_map/all_to_all | solution.py:34
  221.0 1.4 copy.22
  222.3 4.7 %all-to-all-done.8.mean_ref = bf16[4,192,128]{2,1,0:T(8,128)(2,1)S(1)} async-done(((bf16[4,192,128]{2,1,0:T(8,128)(2,1)}), bf16[4,192,128]{2,1,0:T(8,128)(2,1)S(1)}, u32[]{:S(2)}, u32[]{:S(2)}) %all-to-all-start.8) | async-done | bytes 196640 | tf_op jit(solution)/shard_map/all_to_all | solution.py:34
  227.7 8.8 %update.1 = (bf16[2048,128]{1,0:T(8,128)(2,1)}, bf16[64,512]{1,0:T(8,128)(2,1)}) custom-call(s32[16]{0:T(128)} %fill_ref.5, s32[1]{0:T(128)} %bitcast.place_ref, bf16[4,192,128]{2,1,0:T(8,128)(2,1)} %copy-done.7, bf16[4,64,1856]{2,1,0:T(8,128)(2,1)} %copy-done.1, bf16[256,128]{1,0:T(8,128)(2,1)} %left_ref.1, bf16[256,128]{1,0:T(8,128)(2,1)} %right_ref.1, ...), custom_call_target="tpu_custom_call" | custom-call | flops 2500000000 | bytes 4000000 | tf_op jit(solution)/shard_map/update/pallas_call | solution.py:358
  (42 shorter events, 7.3 us)
Async XLA Ops:
  0.6 43.5 %copy-start.12 = (s32[112,1]{0,1:T(1,128)S(1)}, s32[112,1]{0,1:T(1,128)}, u32[]{:S(2)}) copy-start(s32[112,1]{0,1:T(1,128)} %param.21) | copy-start | bytes 1348
  11.4 11.8 %all-to-all-start = ((bf16[4,512,128]{2,1,0:T(8,128)(2,1)}), bf16[4,512,128]{2,1,0:T(8,128)(2,1)S(1)}, u32[]{:S(2)}, u32[]{:S(2)}) async-start(bf16[4,512,128]{2,1,0:T(8,128)(2,1)} %bitcast.20), calls=%async_computation | async-start | bytes 1048576 | tf_op jit(solution)/shard_map/all_to_all | solution.py:34
  23.1 13.4 %copy-start.2 = (bf16[4,512,128]{2,1,0:T(8,128)(2,1)}, bf16[4,512,128]{2,1,0:T(8,128)(2,1)S(1)}, u32[]{:S(2)}) copy-start(bf16[4,512,128]{2,1,0:T(8,128)(2,1)S(1)} %all-to-all-done.x_ref) | copy-start | bytes 1572868
  25.1 11.5 %all-to-all-start.1 = ((bf16[4,512,128]{2,1,0:T(8,128)(2,1)}), bf16[4,512,128]{2,1,0:T(8,128)(2,1)S(1)}, u32[]{:S(2)}, u32[]{:S(2)}) async-start(bf16[4,512,128]{2,1,0:T(8,128)(2,1)} %broadcast_in_dim.36), calls=%async_computation.1 | async-start | bytes 1048576 | tf_op jit(solution)/shard_map/all_to_all | solution.py:34
  36.6 0.8 copy-start.3
  40.7 49.7 %copy-start.4 = (bf16[4,512,128]{2,1,0:T(8,128)(2,1)S(1)}, bf16[4,512,128]{2,1,0:T(8,128)(2,1)}, u32[]{:S(2)}) copy-start(bf16[4,512,128]{2,1,0:T(8,128)(2,1)} %get-tuple-element.23) | copy-start | bytes 1572868
  40.7 9.0 %all-to-all-start.3 = ((bf16[4,4,16,128]{3,2,1,0:T(8,128)(2,1)}), bf16[4,4,16,128]{3,2,1,0:T(8,128)(2,1)S(1)}, u32[]{:S(2)}, u32[]{:S(2)}) async-start(bf16[4,4,16,128]{3,2,1,0:T(8,128)(2,1)} %get-tuple-element.13), calls=%async_computation.3 | async-start | bytes 131072 | tf_op jit(solution)/shard_map/all_to_all | solution.py:34
  49.7 0.6 copy-start.6
  50.4 59.9 %copy-start.9 = (bf16[64,512]{1,0:T(8,128)(2,1)S(1)}, bf16[64,512]{1,0:T(8,128)(2,1)}, u32[]{:S(2)}) copy-start(bf16[64,512]{1,0:T(8,128)(2,1)} %param.25) | copy-start | bytes 196612
  50.4 67.5 %copy-start.10 = (bf16[64,256]{1,0:T(8,128)(2,1)S(1)}, bf16[64,256]{1,0:T(8,128)(2,1)}, u32[]{:S(2)}) copy-start(bf16[64,256]{1,0:T(8,128)(2,1)} %param.26) | copy-start | bytes 98308
  50.4 67.5 %copy-start.11 = (bf16[64,64]{1,0:T(8,128)(2,1)S(1)}, bf16[64,64]{1,0:T(8,128)(2,1)}, u32[]{:S(2)}) copy-start(bf16[64,64]{1,0:T(8,128)(2,1)} %param.24) | copy-start | bytes 24580
  103.3 59.5 %all-to-all-start.5 = ((bf16[128,2,16,128]{3,2,1,0:T(8,128)(2,1)}), bf16[128,2,16,128]{3,2,1,0:T(8,128)(2,1)S(1)}, u32[]{:S(2)}, u32[]{:S(2)}) async-start(bf16[128,2,16,128]{3,2,1,0:T(8,128)(2,1)} %bitcast.18), calls=%async_computation.5 | async-start | bytes 2097152 | tf_op jit(solution)/shard_map/all_to_all | solution.py:34
  110.3 5.9 %collective-permute-start = (bf16[64,512]{1,0:T(8,128)(2,1)S(1)}, bf16[64,512]{1,0:T(8,128)(2,1)S(1)}, u32[]{:S(2)}, u32[]{:S(2)}) collective-permute-start(bf16[64,512]{1,0:T(8,128)(2,1)S(1)} %copy-done.9), channel_id=1, source_target_pairs={{0,4},{4,8},{8,12},{12,16},{16,20},{20,24},{24,28},{28,32},{32,36}... | collective-permute-start | bytes 196616 | tf_op jit(solution)/shard_map/ppermute | solution.py:430
  112.3 5.5 %collective-permute-start.1 = (bf16[64,512]{1,0:T(8,128)(2,1)S(1)}, bf16[64,512]{1,0:T(8,128)(2,1)S(1)}, u32[]{:S(2)}, u32[]{:S(2)}) collective-permute-start(bf16[64,512]{1,0:T(8,128)(2,1)S(1)} %copy-done.9), channel_id=1, source_target_pairs={{4,0},{8,4},{12,8},{16,12},{20,16},{24,20},{28,24},{32,28},{36,32}... | collective-permute-start | bytes 196616 | tf_op jit(solution)/shard_map/ppermute | solution.py:432
  117.9 103.1 %copy-start.8 = (s32[2,2048]{1,0:T(2,128)S(1)}, s32[2,2048]{1,0:T(2,128)}, u32[]{:S(2)}) copy-start(s32[2,2048]{1,0:T(2,128)} %ends_ref.1) | copy-start | bytes 49156
  162.8 6.7 %copy-start = (bf16[128,2,16,128]{3,2,1,0:T(8,128)(2,1)}, bf16[128,2,16,128]{3,2,1,0:T(8,128)(2,1)S(1)}, u32[]{:S(2)}) copy-start(bf16[128,2,16,128]{3,2,1,0:T(8,128)(2,1)S(1)} %all-to-all-done.5) | copy-start | bytes 3145732
  163.9 18.0 %all-to-all-start.9 = ((bf16[4,64,1856]{2,1,0:T(8,128)(2,1)}), bf16[4,64,1856]{2,1,0:T(8,128)(2,1)S(1)}, u32[]{:S(2)}, u32[]{:S(2)}) async-start(bf16[4,64,1856]{2,1,0:T(8,128)(2,1)} %broadcast_in_dim.40), calls=%async_computation.9 | async-start | bytes 1966080 | tf_op jit(solution)/shard_map/all_to_all | solution.py:34
  181.9 45.2 %copy-start.1 = (bf16[4,64,1856]{2,1,0:T(8,128)(2,1)}, bf16[4,64,1856]{2,1,0:T(8,128)(2,1)S(1)}, u32[]{:S(2)}) copy-start(bf16[4,64,1856]{2,1,0:T(8,128)(2,1)S(1)} %all-to-all-done.9.atoms_ref) | copy-start | bytes 2850820
  207.3 10.1 %all-to-all-start.10 = ((bf16[4,16,2048]{2,1,0:T(8,128)(2,1)}), bf16[4,16,2048]{2,1,0:T(8,128)(2,1)S(1)}, u32[]{:S(2)}, u32[]{:S(2)}) async-start(bf16[4,16,2048]{2,1,0:T(8,128)(2,1)} %broadcast_in_dim.41), calls=%async_computation.10 | async-start | bytes 524288 | tf_op jit(solution)/shard_map/all_to_all | solution.py:34
  217.4 9.7 %copy-start.5 = (bf16[4,16,2048]{2,1,0:T(8,128)(2,1)}, bf16[4,16,2048]{2,1,0:T(8,128)(2,1)S(1)}, u32[]{:S(2)}) copy-start(bf16[4,16,2048]{2,1,0:T(8,128)(2,1)S(1)} %all-to-all-done.10.message_ref) | copy-start | bytes 786436
  217.4 9.7 %all-to-all-start.8 = ((bf16[4,192,128]{2,1,0:T(8,128)(2,1)}), bf16[4,192,128]{2,1,0:T(8,128)(2,1)S(1)}, u32[]{:S(2)}, u32[]{:S(2)}) async-start(bf16[4,192,128]{2,1,0:T(8,128)(2,1)} %mean.1), calls=%async_computation.8 | async-start | bytes 393216 | tf_op jit(solution)/shard_map/all_to_all | solution.py:34
  227.1 0.7 copy-start.7

commit v2 on v1

v2 whole, which is shorter than its diff:
```python
import functools

import jax
import jax.numpy as jnp
from jax import lax
from jax.experimental import pallas as pl
from jax.experimental.pallas import tpu as pltpu
from jax.sharding import PartitionSpec as P


BF16 = jnp.bfloat16
F32 = jnp.float32
BLOCK = 128
LANES = 128
SLOTS = 2
SPAN = 4
HALO = 3
ROOM = 24 << 20
LEFT_FIRST = (((0,), (0,)), ((), ()))
BOTH_LAST = (((1,), (1,)), ((), ()))


def vmem():
    return pl.BlockSpec(memory_space=pltpu.VMEM)


def smem():
    return pl.BlockSpec(memory_space=pltpu.SMEM)


def dot(a, b, dims):
    return lax.dot_general(a, b, dims, preferred_element_type=F32)


def exchanged(value, axis, groups=None):
    return lax.all_to_all(
        value, axis, split_axis=0, concat_axis=0, tiled=True, axis_index_groups=groups
    )


def for_each(value, axis):
    return jnp.broadcast_to(value, (lax.axis_size(axis), *value.shape))


def moved(value, axis, steps):
    count = lax.axis_size(axis)
    return lax.ppermute(value, axis, [(i, (i + steps) % count) for i in range(count)])


def swapped(places, count, step):
    out = []
    for place in places:
        below = (place - step) % count
        out += [(place, below), (below, place)]
    return out


def angular_body(fill_ref, place_ref, pack_ref, hidden_ref, angular_ref):
    quarters, own_blocks, channels = angular_ref.shape[:3]
    bonds, width = hidden_ref.shape[1:]
    inputs = quarters * width
    feat = place_ref[0]
    first = feat * own_blocks
    x = jnp.concatenate([pack_ref[k, :bonds] for k in range(quarters)], axis=1)
    total = None
    for q in range(quarters):
        pre = jnp.dot(x, pack_ref[q, bonds : bonds + inputs], preferred_element_type=F32)
        hidden = jax.nn.silu(pre).astype(BF16)
        hidden_ref[(q - feat + quarters) % quarters] = hidden
        part = dot(pack_ref[q, bonds + inputs :], hidden, BOTH_LAST)
        total = part if total is None else total + part
    for b in range(own_blocks):
        piece = total[:, b * BLOCK : (b + 1) * BLOCK]
        real = lax.broadcasted_iota(jnp.int32, piece.shape, 1) < fill_ref[first + b]
        piece = jnp.where(real, piece, 0.0).astype(BF16)
        for q in range(quarters):
            angular_ref[q, b] = piece[q * channels : (q + 1) * channels]


def angular_call(fill, place, pack, bonds, own_blocks, channels):
    quarters, _, width = pack.shape
    return pl.pallas_call(
        angular_body,
        out_shape=(
            jax.ShapeDtypeStruct((quarters, bonds, width), BF16),
            jax.ShapeDtypeStruct((quarters, own_blocks, channels, BLOCK), BF16),
        ),
        in_specs=[smem(), smem(), vmem()],
        out_specs=(vmem(), vmem()),
        cost_estimate=pl.CostEstimate(
            flops=600_000_000, bytes_accessed=2_000_000, transcendentals=262_144
        ),
        compiler_params=pltpu.CompilerParams(vmem_limit_bytes=ROOM),
        name="angular",
    )(fill, place, pack)


def contribution_body(
    chunks, source_ref, slot_ref, label_ref, angular_ref, coef_hbm, out_ref, coef_ref, sems
):
    channels, rows = angular_ref.shape[1:]
    half = channels // 2
    stride = SLOTS * half + 1
    per_chunk = coef_ref.shape[0] // chunks
    copies = []
    for c in range(chunks):
        here = pl.ds(c * per_chunk, per_chunk)
        copies.append(pltpu.make_async_copy(coef_hbm.at[here], coef_ref.at[here], sems.at[c]))
        copies[c].start()
    out_ref[...] = jnp.zeros_like(out_ref)

    def tag(step, carry):
        for k in range(4):
            owner = step * 4 + k
            out_ref[owner * stride + stride - 1] = label_ref[owner]
        return carry

    lax.fori_loop(0, label_ref.shape[0] // 4, tag, 0)
    for c in range(chunks):
        copies[c].wait()

        def multiply(step, carry):
            for k in range(7):
                pair = c * per_chunk + step * 7 + k
                part = dot(angular_ref[source_ref[pair]], coef_ref[pair], BOTH_LAST)
                part = part.astype(BF16).reshape(half, 2, rows)
                out_ref[pl.ds(slot_ref[pair], half)] = part
            return carry

        lax.fori_loop(0, per_chunk // 7, multiply, 0)


def contribution_call(sources, slots, labels, angular, coef):
    pairs = coef.shape[0]
    chunks = next(c for c in (4, 2, 1) if pairs % (7 * c) == 0)
    _, channels, rows = angular.shape
    stride = SLOTS * channels // 2 + 1
    return pl.pallas_call(
        functools.partial(contribution_body, chunks),
        out_shape=jax.ShapeDtypeStruct((labels.shape[0] * stride, 2, rows), BF16),
        in_specs=[
            smem(),
            smem(),
            vmem(),
            vmem(),
            pl.BlockSpec(memory_space=pltpu.HBM),
        ],
        out_specs=vmem(),
        scratch_shapes=[
            pltpu.VMEM(coef.shape, BF16),
            pltpu.SemaphoreType.DMA((chunks,)),
        ],
        cost_estimate=pl.CostEstimate(
            flops=60_000_000, bytes_accessed=5_000_000, transcendentals=0
        ),
        compiler_params=pltpu.CompilerParams(vmem_limit_bytes=ROOM),
        name="contribution",
    )(sources, slots, labels, angular, coef)


def message_body(
    fill_ref,
    place_ref,
    ends_ref,
    arrived_ref,
    message_ref,
    own_ref,
    near_ref,
    next_ref,
    over_ref,
    sums,
    padded,
    labels,
    label_ref,
    sem,
):
    blocks = fill_ref.shape[0]
    channels, rows = sums.shape[1:]
    half = channels // 2
    stride = SLOTS * half + 1
    sources = arrived_ref.shape[0] // stride
    bonds = blocks * rows
    spans = HALO * SPAN
    total = jnp.zeros((2, rows), F32)
    for source in range(sources):
        total += arrived_ref[source * stride + stride - 1].astype(F32)
    labels[...] = total.astype(jnp.int32)
    copy = pltpu.make_async_copy(labels, label_ref, sem)
    copy.start()
    sums[...] = jnp.zeros_like(sums)
    copy.wait()

    def add(step, carry):
        for k in range(4):
            source = step * 4 + k
            for slot in range(SLOTS):
                part = arrived_ref[pl.ds(source * stride + slot * half, half)]
                sums[label_ref[slot, source]] += part.reshape(channels, rows).astype(F32)
        return carry

    lax.fori_loop(0, sources // 4, add, 0)
    pieces = []
    masks = []
    for b in range(blocks):
        real = lax.broadcasted_iota(jnp.int32, (channels, rows), 1) < fill_ref[b]
        piece = jnp.where(real, sums[b], 0.0)
        message_ref[b * channels : (b + 1) * channels] = piece.astype(BF16)
        pieces.append(piece)
        masks.append(jnp.where(real[:1], 1.0, 0.0))
    message = jnp.concatenate(pieces, axis=1)
    mask = jnp.concatenate(masks, axis=1)
    ends = ends_ref[1:2, :]
    high = ends // LANES
    low = ends % LANES
    stacked = []
    tallies = []
    for h in range(spans):
        here = high == h
        stacked.append(jnp.where(here, message, 0.0).astype(BF16))
        tallies.append(jnp.where(here, mask, 0.0))
    tallies.append(jnp.zeros((16 - spans, bonds), F32))
    stacked.append(jnp.concatenate(tallies, axis=0).astype(BF16))
    chosen = jnp.where(
        low == lax.broadcasted_iota(jnp.int32, (LANES, bonds), 0), 1.0, 0.0
    ).astype(BF16)
    window = dot(jnp.concatenate(stacked, axis=0), chosen, BOTH_LAST)
    counts = window[spans * channels : spans * channels + spans]
    upper = jnp.floor(counts * (1.0 / 256.0))
    lower = counts - 256.0 * upper
    padded[...] = jnp.zeros_like(padded)
    width = SPAN * channels
    for k in range(HALO):
        group = jnp.concatenate(
            [
                window[k * width : (k + 1) * width],
                upper[k * SPAN : (k + 1) * SPAN],
                lower[k * SPAN : (k + 1) * SPAN],
            ],
            axis=0,
        )
        own_ref[k] = group
        padded[HALO + k] = group.astype(BF16)
    near = place_ref[0] % 4
    for m in range(4):
        start = jnp.where(m == near, 0, m - near + HALO)
        for k in range(HALO):
            near_ref[m, k] = padded[start + k]
    first = HALO + jnp.where(near == 3, 1, 0)
    next_ref[0] = padded[first]
    next_ref[1] = padded[first + 1]
    over_ref[...] = padded[HALO + jnp.where(near >= 2, 2, 0)]


def message_call(fill, place, ends, arrived, channels):
    rows = arrived.shape[2]
    blocks = fill.shape[0]
    depth = SPAN * channels + 2 * SPAN
    return pl.pallas_call(
        message_body,
        out_shape=(
            jax.ShapeDtypeStruct((blocks * channels, rows), BF16),
            jax.ShapeDtypeStruct((HALO, depth, LANES), F32),
            jax.ShapeDtypeStruct((4, HALO, depth, LANES), BF16),
            jax.ShapeDtypeStruct((2, depth, LANES), BF16),
            jax.ShapeDtypeStruct((depth, LANES), BF16),
        ),
        in_specs=[smem(), smem(), vmem(), vmem()],
        out_specs=(vmem(), vmem(), vmem(), vmem(), vmem()),
        scratch_shapes=[
            pltpu.VMEM((blocks + 1, channels, rows), F32),
            pltpu.VMEM((3 * HALO, depth, LANES), BF16),
            pltpu.VMEM((SLOTS, LANES), jnp.int32),
            pltpu.SMEM((SLOTS, LANES), jnp.int32),
            pltpu.SemaphoreType.DMA(()),
        ],
        cost_estimate=pl.CostEstimate(
            flops=120_000_000, bytes_accessed=2_000_000, transcendentals=0
        ),
        compiler_params=pltpu.CompilerParams(vmem_limit_bytes=ROOM),
        name="message",
    )(fill, place, ends, arrived)


def mean_body(place_ref, own_ref, near_ref, next_ref, over_ref, message_ref, out_ref, total):
    copies = out_ref.shape[0]
    depth = own_ref.shape[1]
    channels = (depth - 2 * SPAN) // SPAN
    width = SPAN * channels
    spot = place_ref[0] % 4
    for k in range(HALO):
        value = own_ref[k]
        for m in range(4):
            value += near_ref[m, k].astype(F32)
        total[k] = value
    first = jnp.where(spot == 3, 1, 0)
    total[first] += next_ref[0].astype(F32)
    total[first + 1] += next_ref[1].astype(F32)
    total[jnp.where(spot >= 2, 2, 0)] += over_ref[...].astype(F32)
    for k in range(HALO):
        value = total[k]
        for h in range(SPAN):
            count = 256.0 * value[width + h : width + h + 1]
            count += value[width + SPAN + h : width + SPAN + h + 1]
            mean = value[h * channels : (h + 1) * channels] / jnp.maximum(count, 1.0)
            mean = mean.astype(BF16)
            row = (k * SPAN + h) * channels
            for m in range(copies):
                out_ref[m, row : row + channels] = mean
    for m in range(copies):
        out_ref[m, HALO * width :] = message_ref[...]


def mean_call(place, own, near, beside, over, message, copies):
    depth = own.shape[1]
    width = depth - 2 * SPAN
    rows = HALO * width + message.shape[0]
    return pl.pallas_call(
        mean_body,
        out_shape=jax.ShapeDtypeStruct((copies, rows, LANES), BF16),
        in_specs=[smem()] + [vmem()] * 5,
        out_specs=vmem(),
        scratch_shapes=[pltpu.VMEM((HALO, depth, LANES), F32)],
        cost_estimate=pl.CostEstimate(
            flops=1_000_000, bytes_accessed=600_000, transcendentals=0
        ),
        compiler_params=pltpu.CompilerParams(vmem_limit_bytes=ROOM),
        name="mean",
    )(place, own, near, beside, over, message)


def update_body(
    fill_ref,
    place_ref,
    mean_ref,
    atoms_ref,
    left_ref,
    right_ref,
    gate_ref,
    hidden_ref,
    bonds_ref,
    ends_ref,
    bond_out_ref,
    atom_out_ref,
    table_left,
    table_right,
    kept,
):
    quarters = mean_ref.shape[0]
    channels = gate_ref.shape[0] // quarters
    feat = place_ref[0]
    near = [(feat - q + quarters) % quarters for q in range(quarters)]
    after = HALO * SPAN * channels
    features = atoms_ref.shape[1]
    window = HALO * SPAN * LANES
    inputs = quarters * features
    tile = 2 * LANES
    states = jnp.concatenate(
        [atoms_ref[near[f], :, window : window + inputs] for f in range(quarters)], axis=0
    )
    sides = jnp.concatenate([left_ref[...], right_ref[...]], axis=1)
    width = left_ref.shape[1]
    own_start = window // HALO
    for c in range(window // tile):
        columns = slice(c * tile, (c + 1) * tile)
        mean = jnp.concatenate(
            [
                jnp.concatenate(
                    [
                        mean_ref[f, (2 * c + e) * channels : (2 * c + e + 1) * channels]
                        for f in range(quarters)
                    ],
                    axis=0,
                )
                for e in range(2)
            ],
            axis=1,
        )
        mean_in = jnp.concatenate(
            [
                dot(
                    atoms_ref[near[f], :, window + inputs : window + inputs + features],
                    mean,
                    LEFT_FIRST,
                ).astype(BF16)
                for f in range(quarters)
            ],
            axis=0,
        )
        pre = dot(states, mean_in, LEFT_FIRST)
        state = jnp.concatenate([atoms_ref[near[f], :, columns] for f in range(quarters)], axis=0)
        updated = (state.astype(F32) + jax.nn.silu(pre)).astype(BF16)
        place = c * tile - own_start
        if 0 <= place < own_start:
            kept[:, place : place + tile] = updated
        table = dot(updated, sides, LEFT_FIRST).astype(BF16)
        table_left[:, c * width : (c + 1) * width] = table[:, :width]
        table_right[:, c * width : (c + 1) * width] = table[:, width:]
    own = pl.multiple_of(feat * features, features)
    atom_out_ref[...] = kept[pl.ds(own, features), :]
    bonds = bonds_ref.shape[0]
    per_quarter = bonds // quarters
    lane = lax.broadcasted_iota(jnp.int32, (tile, tile), 1)
    row = lax.broadcasted_iota(jnp.int32, (BLOCK, width), 0)
    for t in range(bonds // tile):
        rows = slice(t * tile, (t + 1) * tile)
        mixed = None
        for side, table in ((0, table_left), (1, table_right)):
            end = ends_ref[rows, side : side + 1]
            chosen = jnp.where(end % tile == lane, 1.0, 0.0).astype(BF16)
            found = jnp.dot(chosen, table[...], preferred_element_type=F32)
            high = jnp.broadcast_to(end // tile, (tile, width))
            for c in range(window // tile):
                part = jnp.where(high == c, found[:, c * width : (c + 1) * width], 0.0)
                mixed = part if mixed is None else mixed + part
        message = jnp.concatenate(
            [
                jnp.concatenate(
                    [
                        mean_ref[f, after + b * channels : after + (b + 1) * channels]
                        for f in range(quarters)
                    ],
                    axis=0,
                )
                for b in range(t * (tile // BLOCK), (t + 1) * (tile // BLOCK))
            ],
            axis=1,
        )
        gate = dot(message, gate_ref[...], LEFT_FIRST)
        q = t * tile // per_quarter
        start = t * tile - q * per_quarter
        hidden = hidden_ref[near[q], start : start + tile].astype(F32)
        update = jax.nn.sigmoid(gate) * (hidden + jax.nn.silu(mixed))
        for e in range(tile // BLOCK):
            part = slice(e * BLOCK, (e + 1) * BLOCK)
            real = row < fill_ref[t * (tile // BLOCK) + e]
            here = slice(t * tile + e * BLOCK, t * tile + (e + 1) * BLOCK)
            bond_out_ref[here] = (
                bonds_ref[here].astype(F32) + jnp.where(real, update[part], 0.0)
            ).astype(BF16)


def update_call(fill, place, mean, atoms, left, right, gate, hidden, bonds, ends):
    features = atoms.shape[1]
    window = HALO * SPAN * LANES
    width = left.shape[1]
    tile = 2 * LANES
    return pl.pallas_call(
        update_body,
        out_shape=(
            jax.ShapeDtypeStruct(bonds.shape, BF16),
            jax.ShapeDtypeStruct((features, window // HALO), BF16),
        ),
        in_specs=[smem(), smem()] + [vmem()] * 8,
        out_specs=(vmem(), vmem()),
        scratch_shapes=[
            pltpu.VMEM((tile, window // tile * width), BF16),
            pltpu.VMEM((tile, window // tile * width), BF16),
            pltpu.VMEM((mean.shape[0] * features, window // HALO), BF16),
        ],
        cost_estimate=pl.CostEstimate(
            flops=2_500_000_000, bytes_accessed=4_000_000, transcendentals=2_000_000
        ),
        compiler_params=pltpu.CompilerParams(vmem_limit_bytes=ROOM),
        name="update",
    )(fill, place, mean, atoms, left, right, gate, hidden, bonds, ends)


def local(
    bond_state,
    block_fill,
    w_in,
    w_down,
    pair_coef,
    pair_source,
    pair_owner,
    pair_target,
    w_gate,
    w_atom_in,
    atom_state,
    w_atom,
    bond_ends,
    w_left,
    w_right,
):
    spaces = lax.axis_size("space")
    feats = lax.axis_size("feat")
    space = lax.axis_index("space").astype(jnp.int32).reshape(1)
    feat = lax.axis_index("feat").astype(jnp.int32).reshape(1)
    bonds, width = bond_state.shape
    blocks = block_fill.shape[0]
    pairs = pair_source.shape[0]
    channels = w_down.shape[1] // feats
    own_bonds = bonds // feats
    near_groups = [[4 * i + k for k in range(4)] for i in range(spaces // 4)]
    first_of = [4 * i for i in range(spaces // 4)]
    next_pairs = swapped(first_of, spaces, 1)
    over_pairs = swapped([i + k for i in first_of for k in (0, 1)], spaces, 2)
    half = channels // 2
    stride = SLOTS * half + 1

    lower = lax.ppermute(atom_state, "space", [(i, (i + 1) % spaces) for i in range(spaces)])
    upper = lax.ppermute(atom_state, "space", [((i + 1) % spaces, i) for i in range(spaces)])
    parts = (
        bond_state.reshape(feats, own_bonds, width),
        for_each(w_in, "feat"),
        for_each(w_down.T, "feat"),
    )
    entered = exchanged(jnp.concatenate(parts, axis=1), "feat")
    owners = pair_owner[:, 0]
    before = lax.broadcasted_iota(jnp.int32, (pairs, pairs), 1) < lax.broadcasted_iota(
        jnp.int32, (pairs, pairs), 0
    )
    same = before & (owners[:, None] == owners[None, :])
    rank = jnp.sum(jnp.where(same, 1, 0), axis=1)
    slots = owners * stride + rank * half
    flat = owners * SLOTS + rank
    wanted = flat[:, None] == lax.broadcasted_iota(jnp.int32, (pairs, spaces * SLOTS), 1)
    labels = blocks + jnp.sum(jnp.where(wanted, pair_target[:, None] - blocks, 0), axis=0)
    lane = lax.broadcasted_iota(jnp.int32, (spaces, SLOTS, LANES), 2)
    labels = jnp.where(lane == space[0], labels.reshape(spaces, SLOTS, 1), 0).astype(BF16)
    ends = bond_ends.T
    entered, ends, slots, labels = lax.optimization_barrier((entered, ends, slots, labels))
    hidden, angular = angular_call(block_fill, feat, entered, own_bonds, blocks // feats, channels)
    angular = exchanged(angular, "feat")
    angular = angular.reshape(blocks, *angular.shape[2:])
    outgoing = contribution_call(pair_source, slots, labels, angular, pair_coef)
    outgoing, hidden = lax.optimization_barrier((outgoing, hidden))
    arrived = exchanged(outgoing.reshape(spaces, stride, *outgoing.shape[1:]), "space")
    arrived = arrived.reshape(outgoing.shape)
    atoms = jnp.concatenate([lower, atom_state, upper, w_atom, w_atom_in], axis=1)
    turned = [hidden[k] if k == 0 else moved(hidden[k], "feat", k) for k in range(feats)]
    hidden = jnp.stack(turned)
    atoms = jnp.stack(
        [atoms if k == 0 else moved(atoms, "feat", k) for k in range(feats)]
    )
    arrived, hidden, atoms = lax.optimization_barrier((arrived, hidden, atoms))
    message, own, near, beside, over = message_call(block_fill, space, bond_ends, arrived, channels)
    near = exchanged(near, "space", near_groups)
    beside = lax.ppermute(beside, "space", next_pairs)
    over = lax.ppermute(over, "space", over_pairs)
    mean = mean_call(space, own, near, beside, over, message, feats)
    mean = exchanged(mean, "feat")
    return update_call(
        block_fill, feat, mean, atoms, w_left, w_right, w_gate, hidden, bond_state, ends
    )


def solution(mesh):
    placed = (
        P("space", "feat"),
        P("space"),
        P(None, "feat"),
        P("feat", None),
        P("space", None, None),
        P("space"),
        P("space", None),
        P("space"),
        P(None, "feat"),
        P(None, "feat"),
        P("feat", "space"),
        P("feat", None),
        P(None, "space"),
        P(None, "feat"),
        P(None, "feat"),
    )
    return jax.shard_map(
        local,
        mesh=mesh,
        in_specs=placed,
        out_specs=(P("space", "feat"), P("feat", "space")),
        check_vma=False,
    )
```

time: 238 us -> 181 us (0.76)
  the two profiles are of different devices: /device:TPU:6 before, /device:TPU:1 now
where the time goes in v2:
time: 181 us; the launch traced here: 180 us
  starting transfers between devices  91.4 us (50%)
  waiting for transfers between devices  39.5 us (22%)
  Pallas kernels  20.6 us (11%)
  blocking collectives  18.6 us (10%)
  local copies, waits for them, and re-layouts  5.41 us (3%)
  other arithmetic  3.65 us (2%)
    all_to_all x3, starting transfers between devices, exchanged(): lax.all_to_all(value, axis, split_axis=0, concat_axis=0, tiled=True, axis...  58.8 us
    all_to_all x3, waiting for transfers between devices, exchanged(): lax.all_to_all(value, axis, split_axis=0, concat_axis=0, tiled=True, axis...  32.5 us
    all_to_all x2, blocking collectives, exchanged(): lax.all_to_all(value, axis, split_axis=0, concat_axis=0, tiled=True, axis...  18.6 us
    ppermute x6, starting transfers between devices, moved(): lax.ppermute(value, axis, [(i, (i + steps) % count) for i in range(count)])  18.6 us
    ppermute x1, starting transfers between devices, local(): over = lax.ppermute(over, 'space', over_pairs)  7.88 us
    pallas_call x1, Pallas kernels, update_call(): pl.pallas_call(update_body, out_shape=(jax.ShapeDtypeStruct(bonds.shape,...  7.4 us
    pallas_call x1, Pallas kernels, contribution_call(): pl.pallas_call(functools.partial(contribution_body, chunks), out_shape=ja...  7.36 us
    ppermute x1, waiting for transfers between devices, local(): lax.ppermute(atom_state, 'space', [((i + 1) % spaces, i) for i in range(s...  3.99 us
  transfers between devices with their start and end apart: 13, of which 5 were waited for; matrix products, arithmetic and copies ran while one was open for 1% of the time, Pallas kernels for 0%

profile of v2, /device:TPU:1, one launch (start us, length us, event | category | flops | bytes accessed | tf_op | source)
XLA Modules:
  0.0 180.2 jit_solution(14831254108442756455)
XLA Ops:
  0.6 1.0 broadcast_in_dim.40
  1.6 0.7 broadcast_in_dim.41
  2.3 2.1 %pad_maximum_fusion = bf16[4,1088,128]{2,1,0:T(8,128)(2,1)} fusion(bf16[4,64,128]{2,1,0:T(8,128)(2,1)S(1)} %broadcast_in_dim.41, bf16[4,512,128]{2,1,0:T(8,128)(2,1)S(1)} %broadcast_in_dim.40, bf16[4,512,128]{2,1,0:T(8,128)(2,1)} %bitcast.31), kind=kLoop, calls=%fused_computation | loop fusion | flops 3342336 | bytes 2228224 | tf_op jit(solution)/shard_map/concatenate | solution.py:508
  4.5 5.1 %all-to-all-start = ((bf16[4,1088,128]{2,1,0:T(8,128)(2,1)}), bf16[4,1088,128]{2,1,0:T(8,128)(2,1)S(1)}, u32[]{:S(2)}, u32[]{:S(2)}) async-start(bf16[4,1088,128]{2,1,0:T(8,128)(2,1)} %pad_maximum_fusion), calls=%async_computation | async-start | bytes 2228224 | tf_op jit(solution)/shard_map/all_to_all | solution.py:36
  10.1 0.4 copy.19
  10.5 0.2 select_convert_fusion.label_ref
  10.7 9.2 %all-to-all-done.pack_ref = bf16[4,1088,128]{2,1,0:T(8,128)(2,1)S(1)} async-done(((bf16[4,1088,128]{2,1,0:T(8,128)(2,1)}), bf16[4,1088,128]{2,1,0:T(8,128)(2,1)S(1)}, u32[]{:S(2)}, u32[]{:S(2)}) %all-to-all-start) | async-done | bytes 1114144 | tf_op jit(solution)/shard_map/all_to_all | solution.py:36
  19.9 2.0 %angular.1 = (bf16[4,512,128]{2,1,0:T(8,128)(2,1)S(1)}, bf16[4,4,16,128]{3,2,1,0:T(8,128)(2,1)S(1)}) custom-call(s32[16]{0:T(128)S(1)} %copy-done.4, s32[1]{0:T(128)} %bitcast.place_ref, bf16[4,1088,128]{2,1,0:T(8,128)(2,1)S(1)} %all-to-all-done.pack_ref), custom_call_target="tpu_custom_call" | custom-call | flops 600000000 | bytes 2000000 | tf_op jit(solution)/shard_map/angular/pallas_call | solution.py:82
  21.9 6.8 %all_to_all.25 = bf16[4,4,16,128]{3,2,1,0:T(8,128)(2,1)S(1)} all-to-all(bf16[4,4,16,128]{3,2,1,0:T(8,128)(2,1)S(1)} %get-tuple-element.21), channel_id=1, replica_groups=mesh['space'=128,'feat'=4] {'feat'}, dimensions={0} | all-to-all | bytes 131072 | tf_op jit(solution)/shard_map/all_to_all | solution.py:36
  28.7 2.0 %copy-done = bf16[112,128,128]{2,1,0:T(8,128)(2,1)S(1)} copy-done((bf16[112,128,128]{2,1,0:T(8,128)(2,1)S(1)}, bf16[112,128,128]{2,1,0:T(8,128)(2,1)}, u32[]{:S(2)}) %copy-start) | copy-done | bytes 3670040
  30.7 7.4 %contribution.1 = bf16[2176,2,128]{2,1,0:T(2,128)(2,1)} custom-call(s32[112]{0:T(128)S(1)} %copy-done.5, s32[112]{0:T(128)S(1)} %multiply_add_fusion.slot_ref, bf16[128,2,128]{2,1,0:T(2,128)(2,1)S(1)} %select_convert_fusion.label_ref, bf16[16,16,128]{2,1,0:T(8,128)(2,1)S(1)} %bitcast.32, bf16[112,128,128]{2,1,0:T(8,128)(2,1)S(1)} %copy-done), custom_call_target="tpu_custom_call" | custom-call | flops 60000000 | bytes 5000000 | tf_op jit(solution)/shard_map/contribution/pallas_call | solution.py:138
  38.1 26.7 %all-to-all-start.2 = ((bf16[128,17,2,128]{3,2,1,0:T(2,128)(2,1)}), bf16[128,17,2,128]{3,2,1,0:T(2,128)(2,1)S(1)}, u32[]{:S(2)}, u32[]{:S(2)}) async-start(bf16[128,17,2,128]{3,2,1,0:T(2,128)(2,1)} %bitcast.9), calls=%async_computation.2 | async-start | bytes 2228224 | tf_op jit(solution)/shard_map/all_to_all | solution.py:36
  64.8 3.5 %collective-permute-start.3 = (bf16[64,512]{1,0:T(8,128)(2,1)S(1)}, bf16[64,512]{1,0:T(8,128)(2,1)S(1)}, u32[]{:S(2)}, u32[]{:S(2)}) collective-permute-start(bf16[64,512]{1,0:T(8,128)(2,1)S(1)} %copy-done.9), channel_id=1, source_target_pairs={{0,4},{4,8},{8,12},{12,16},{16,20},{20,24},{24,28},{28,32},{32,36}... | collective-permute-start | bytes 196616 | tf_op jit(solution)/shard_map/ppermute | solution.py:501
  68.4 1.9 %collective-permute-start.4 = (bf16[64,512]{1,0:T(8,128)(2,1)S(1)}, bf16[64,512]{1,0:T(8,128)(2,1)S(1)}, u32[]{:S(2)}, u32[]{:S(2)}) collective-permute-start(bf16[64,512]{1,0:T(8,128)(2,1)S(1)} %copy-done.9), channel_id=1, source_target_pairs={{4,0},{8,4},{12,8},{16,12},{20,16},{24,20},{28,24},{32,28},{36,32}... | collective-permute-start | bytes 196616 | tf_op jit(solution)/shard_map/ppermute | solution.py:502
  70.3 4.0 %collective-permute-done.4 = bf16[64,512]{1,0:T(8,128)(2,1)S(1)} collective-permute-done((bf16[64,512]{1,0:T(8,128)(2,1)S(1)}, bf16[64,512]{1,0:T(8,128)(2,1)S(1)}, u32[]{:S(2)}, u32[]{:S(2)}) %collective-permute-start.4) | collective-permute-done | bytes 65568 | tf_op jit(solution)/shard_map/ppermute | solution.py:502
  74.4 2.2 %collective-permute-start.5 = (bf16[64,1856]{1,0:T(8,128)(2,1)S(1)}, bf16[64,1856]{1,0:T(8,128)(2,1)S(1)}, u32[]{:S(2)}, u32[]{:S(2)}) collective-permute-start(bf16[64,1856]{1,0:T(8,128)(2,1)S(1)} %constant_dynamic-update-slice_fusion), channel_id=1, source_target_pairs={{0,1},{1,2},{2,3},{3,0},{4,5},{5,6},{6,7},{7,4},{8,9},{9,10},{10,1... | collective-permute-start | bytes 712712 | tf_op jit(solution)/shard_map/ppermute | solution.py:47
  76.6 3.7 %collective-permute-start.6 = (bf16[64,1856]{1,0:T(8,128)(2,1)S(1)}, bf16[64,1856]{1,0:T(8,128)(2,1)S(1)}, u32[]{:S(2)}, u32[]{:S(2)}) collective-permute-start(bf16[64,1856]{1,0:T(8,128)(2,1)S(1)} %constant_dynamic-update-slice_fusion), channel_id=1, source_target_pairs={{0,2},{1,3},{2,0},{3,1},{4,6},{5,7},{6,4},{7,5},{8,10},{9,11},{10,... | collective-permute-start | bytes 712712 | tf_op jit(solution)/shard_map/ppermute | solution.py:47
  80.3 2.6 %collective-permute-start.7 = (bf16[64,1856]{1,0:T(8,128)(2,1)S(1)}, bf16[64,1856]{1,0:T(8,128)(2,1)S(1)}, u32[]{:S(2)}, u32[]{:S(2)}) collective-permute-start(bf16[64,1856]{1,0:T(8,128)(2,1)S(1)} %constant_dynamic-update-slice_fusion), channel_id=1, source_target_pairs={{0,3},{1,0},{2,1},{3,2},{4,7},{5,4},{6,5},{7,6},{8,11},{9,8},{10,9... | collective-permute-start | bytes 712712 | tf_op jit(solution)/shard_map/ppermute | solution.py:47
  83.0 2.7 %collective-permute-start = (bf16[512,128]{1,0:T(8,128)(2,1)S(1)}, bf16[512,128]{1,0:T(8,128)(2,1)S(1)}, u32[]{:S(2)}, u32[]{:S(2)}) collective-permute-start(bf16[512,128]{1,0:T(8,128)(2,1)S(1)} %get-tuple-element.37), channel_id=1, source_target_pairs={{0,1},{1,2},{2,3},{3,0},{4,5},{5,6},{6,7},{7,4},{8,9},{9,10},{10,1... | collective-permute-start | bytes 393224 | tf_op jit(solution)/shard_map/ppermute | solution.py:47
  85.6 3.4 %collective-permute-start.1 = (bf16[512,128]{1,0:T(8,128)(2,1)S(1)}, bf16[512,128]{1,0:T(8,128)(2,1)S(1)}, u32[]{:S(2)}, u32[]{:S(2)}) collective-permute-start(bf16[512,128]{1,0:T(8,128)(2,1)S(1)} %get-tuple-element.36), channel_id=1, source_target_pairs={{0,2},{1,3},{2,0},{3,1},{4,6},{5,7},{6,4},{7,5},{8,10},{9,11},{10,... | collective-permute-start | bytes 393224 | tf_op jit(solution)/shard_map/ppermute | solution.py:47
  89.1 4.0 %collective-permute-start.2 = (bf16[512,128]{1,0:T(8,128)(2,1)S(1)}, bf16[512,128]{1,0:T(8,128)(2,1)S(1)}, u32[]{:S(2)}, u32[]{:S(2)}) collective-permute-start(bf16[512,128]{1,0:T(8,128)(2,1)S(1)} %get-tuple-element.35), channel_id=1, source_target_pairs={{0,3},{1,0},{2,1},{3,2},{4,7},{5,4},{6,5},{7,6},{8,11},{9,8},{10,9... | collective-permute-start | bytes 393224 | tf_op jit(solution)/shard_map/ppermute | solution.py:47
  93.3 1.8 %collective-permute-done.2 = bf16[512,128]{1,0:T(8,128)(2,1)S(1)} collective-permute-done((bf16[512,128]{1,0:T(8,128)(2,1)S(1)}, bf16[512,128]{1,0:T(8,128)(2,1)S(1)}, u32[]{:S(2)}, u32[]{:S(2)}) %collective-permute-start.2) | collective-permute-done | bytes 131104 | tf_op jit(solution)/shard_map/ppermute | solution.py:47
  95.1 0.9 pad_maximum_fusion.2.hidden_ref
  95.9 23.3 %all-to-all-done.2 = bf16[128,17,2,128]{3,2,1,0:T(2,128)(2,1)S(1)} async-done(((bf16[128,17,2,128]{3,2,1,0:T(2,128)(2,1)}), bf16[128,17,2,128]{3,2,1,0:T(2,128)(2,1)S(1)}, u32[]{:S(2)}, u32[]{:S(2)}) %all-to-all-start.2) | async-done | bytes 1114144 | tf_op jit(solution)/shard_map/all_to_all | solution.py:36
  119.2 3.8 %message.1 = (bf16[256,128]{1,0:T(8,128)(2,1)S(1)}, f32[3,72,128]{2,1,0:T(8,128)S(1)}, bf16[4,3,72,128]{3,2,1,0:T(8,128)(2,1)}, bf16[2,72,128]{2,1,0:T(8,128)(2,1)S(1)}, bf16[72,128]{1,0:T(8,128)(2,1)S(1)}) custom-call(s32[16]{0:T(128)S(1)} %copy-done.4, s32[1]{0:T(128)} %bitcast.1.place_ref, s32[2,2048]{1,0:T(2,128)S(1)} %copy-done.3, ...), custom_call_target="tpu_custom_call" | custom-call | flops 120000000 | bytes 2000000 | tf_op jit(solution)/shard_map/message/pallas_call | solution.py:258
  123.1 27.0 %all-to-all-start.3 = ((bf16[4,3,72,128]{3,2,1,0:T(8,128)(2,1)}), bf16[4,3,72,128]{3,2,1,0:T(8,128)(2,1)S(1)}, u32[]{:S(2)}, u32[]{:S(2)}) async-start(bf16[4,3,72,128]{3,2,1,0:T(8,128)(2,1)} %get-tuple-element.27), calls=%async_computation.3 | async-start | bytes 442368 | tf_op jit(solution)/shard_map/all_to_all | solution.py:36
  150.1 0.7 collective-permute-start.8
  150.8 7.9 %collective-permute-start.9 = (bf16[72,128]{1,0:T(8,128)(2,1)S(1)}, bf16[72,128]{1,0:T(8,128)(2,1)S(1)}, u32[]{:S(2)}, u32[]{:S(2)}) collective-permute-start(bf16[72,128]{1,0:T(8,128)(2,1)S(1)} %get-tuple-element.29), channel_id=1, source_target_pairs={{0,504},{504,0},{4,508},{508,4},{16,8},{8,16},{20,12},{12,20},{32,... | collective-permute-start | bytes 55304 | tf_op jit(solution)/shard_map/ppermute | solution.py:540
  158.7 1.1 collective-permute-done.9.over_ref
  159.9 11.8 %all_to_all.26.mean_ref = bf16[4,448,128]{2,1,0:T(8,128)(2,1)S(1)} all-to-all(bf16[4,448,128]{2,1,0:T(8,128)(2,1)S(1)} %mean.1), channel_id=1, replica_groups=mesh['space'=128,'feat'=4] {'feat'}, dimensions={0} | all-to-all | bytes 917504 | tf_op jit(solution)/shard_map/all_to_all | solution.py:36
  171.7 1.0 copy-done.2
  172.8 7.4 %update.1 = (bf16[2048,128]{1,0:T(8,128)(2,1)}, bf16[64,512]{1,0:T(8,128)(2,1)}) custom-call(s32[16]{0:T(128)S(1)} %copy-done.4, s32[1]{0:T(128)} %bitcast.place_ref, bf16[4,448,128]{2,1,0:T(8,128)(2,1)S(1)} %all_to_all.26.mean_ref, bf16[4,64,1856]{2,1,0:T(8,128)(2,1)S(1)} %pad_maximum_fusion.1.atoms_ref, bf16[256,128]{1,0:T(8,128)(2,1)S(1)} %copy-done.6, ...), custom_call_target="tpu_custom_call" | custom-call | flops 2500000000 | bytes 4000000 | tf_op jit(solution)/shard_map/update/pallas_call | solution.py:447
  (50 shorter events, 0.9 us)
Async XLA Ops:
  4.5 5.1 %copy-start.13 = (s32[112,1]{0,1:T(1,128)S(1)}, s32[112,1]{0,1:T(1,128)}, u32[]{:S(2)}) copy-start(s32[112,1]{0,1:T(1,128)} %param.21) | copy-start | bytes 1348
  4.5 5.3 %copy-start.12 = (s32[112]{0:T(128)S(1)}, s32[112]{0:T(128)}, u32[]{:S(2)}) copy-start(s32[112]{0:T(128)} %param.22) | copy-start | bytes 1348
  4.5 5.6 %copy-start.3 = (s32[2,2048]{1,0:T(2,128)S(1)}, s32[2,2048]{1,0:T(2,128)}, u32[]{:S(2)}) copy-start(s32[2,2048]{1,0:T(2,128)} %ends_ref.1) | copy-start | bytes 49156
  4.5 15.4 %all-to-all-start = ((bf16[4,1088,128]{2,1,0:T(8,128)(2,1)}), bf16[4,1088,128]{2,1,0:T(8,128)(2,1)S(1)}, u32[]{:S(2)}, u32[]{:S(2)}) async-start(bf16[4,1088,128]{2,1,0:T(8,128)(2,1)} %pad_maximum_fusion), calls=%async_computation | async-start | bytes 2228224 | tf_op jit(solution)/shard_map/all_to_all | solution.py:36
  9.6 10.3 %copy-start.4 = (s32[16]{0:T(128)S(1)}, s32[16]{0:T(128)}, u32[]{:S(2)}) copy-start(s32[16]{0:T(128)} %fill_ref.5) | copy-start | bytes 196
  19.9 8.8 %copy-start.5 = (s32[112]{0:T(128)S(1)}, s32[112]{0:T(128)}, u32[]{:S(2)}) copy-start(s32[112]{0:T(128)} %source_ref.1) | copy-start | bytes 1348
  28.7 2.0 %copy-start = (bf16[112,128,128]{2,1,0:T(8,128)(2,1)S(1)}, bf16[112,128,128]{2,1,0:T(8,128)(2,1)}, u32[]{:S(2)}) copy-start(bf16[112,128,128]{2,1,0:T(8,128)(2,1)} %coef_hbm.1) | copy-start | bytes 11010052
  38.1 26.7 %copy-start.9 = (bf16[64,512]{1,0:T(8,128)(2,1)S(1)}, bf16[64,512]{1,0:T(8,128)(2,1)}, u32[]{:S(2)}) copy-start(bf16[64,512]{1,0:T(8,128)(2,1)} %param.25) | copy-start | bytes 196612
  38.1 36.2 %copy-start.10 = (bf16[64,256]{1,0:T(8,128)(2,1)S(1)}, bf16[64,256]{1,0:T(8,128)(2,1)}, u32[]{:S(2)}) copy-start(bf16[64,256]{1,0:T(8,128)(2,1)} %param.26) | copy-start | bytes 98308
  38.1 36.2 %copy-start.11 = (bf16[64,64]{1,0:T(8,128)(2,1)S(1)}, bf16[64,64]{1,0:T(8,128)(2,1)}, u32[]{:S(2)}) copy-start(bf16[64,64]{1,0:T(8,128)(2,1)} %param.24) | copy-start | bytes 24580
  38.1 81.1 %all-to-all-start.2 = ((bf16[128,17,2,128]{3,2,1,0:T(2,128)(2,1)}), bf16[128,17,2,128]{3,2,1,0:T(2,128)(2,1)S(1)}, u32[]{:S(2)}, u32[]{:S(2)}) async-start(bf16[128,17,2,128]{3,2,1,0:T(2,128)(2,1)} %bitcast.9), calls=%async_computation.2 | async-start | bytes 2228224 | tf_op jit(solution)/shard_map/all_to_all | solution.py:36
  64.8 5.5 %collective-permute-start.3 = (bf16[64,512]{1,0:T(8,128)(2,1)S(1)}, bf16[64,512]{1,0:T(8,128)(2,1)S(1)}, u32[]{:S(2)}, u32[]{:S(2)}) collective-permute-start(bf16[64,512]{1,0:T(8,128)(2,1)S(1)} %copy-done.9), channel_id=1, source_target_pairs={{0,4},{4,8},{8,12},{12,16},{16,20},{20,24},{24,28},{28,32},{32,36}... | collective-permute-start | bytes 196616 | tf_op jit(solution)/shard_map/ppermute | solution.py:501
  68.4 6.0 %collective-permute-start.4 = (bf16[64,512]{1,0:T(8,128)(2,1)S(1)}, bf16[64,512]{1,0:T(8,128)(2,1)S(1)}, u32[]{:S(2)}, u32[]{:S(2)}) collective-permute-start(bf16[64,512]{1,0:T(8,128)(2,1)S(1)} %copy-done.9), channel_id=1, source_target_pairs={{4,0},{8,4},{12,8},{16,12},{20,16},{24,20},{28,24},{32,28},{36,32}... | collective-permute-start | bytes 196616 | tf_op jit(solution)/shard_map/ppermute | solution.py:502
  74.4 14.7 %collective-permute-start.5 = (bf16[64,1856]{1,0:T(8,128)(2,1)S(1)}, bf16[64,1856]{1,0:T(8,128)(2,1)S(1)}, u32[]{:S(2)}, u32[]{:S(2)}) collective-permute-start(bf16[64,1856]{1,0:T(8,128)(2,1)S(1)} %constant_dynamic-update-slice_fusion), channel_id=1, source_target_pairs={{0,1},{1,2},{2,3},{3,0},{4,5},{5,6},{6,7},{7,4},{8,9},{9,10},{10,1... | collective-permute-start | bytes 712712 | tf_op jit(solution)/shard_map/ppermute | solution.py:47
  76.6 16.5 %collective-permute-start.6 = (bf16[64,1856]{1,0:T(8,128)(2,1)S(1)}, bf16[64,1856]{1,0:T(8,128)(2,1)S(1)}, u32[]{:S(2)}, u32[]{:S(2)}) collective-permute-start(bf16[64,1856]{1,0:T(8,128)(2,1)S(1)} %constant_dynamic-update-slice_fusion), channel_id=1, source_target_pairs={{0,2},{1,3},{2,0},{3,1},{4,6},{5,7},{6,4},{7,5},{8,10},{9,11},{10,... | collective-permute-start | bytes 712712 | tf_op jit(solution)/shard_map/ppermute | solution.py:47
  80.3 12.8 %collective-permute-start.7 = (bf16[64,1856]{1,0:T(8,128)(2,1)S(1)}, bf16[64,1856]{1,0:T(8,128)(2,1)S(1)}, u32[]{:S(2)}, u32[]{:S(2)}) collective-permute-start(bf16[64,1856]{1,0:T(8,128)(2,1)S(1)} %constant_dynamic-update-slice_fusion), channel_id=1, source_target_pairs={{0,3},{1,0},{2,1},{3,2},{4,7},{5,4},{6,5},{7,6},{8,11},{9,8},{10,9... | collective-permute-start | bytes 712712 | tf_op jit(solution)/shard_map/ppermute | solution.py:47
  83.0 10.3 %collective-permute-start = (bf16[512,128]{1,0:T(8,128)(2,1)S(1)}, bf16[512,128]{1,0:T(8,128)(2,1)S(1)}, u32[]{:S(2)}, u32[]{:S(2)}) collective-permute-start(bf16[512,128]{1,0:T(8,128)(2,1)S(1)} %get-tuple-element.37), channel_id=1, source_target_pairs={{0,1},{1,2},{2,3},{3,0},{4,5},{5,6},{6,7},{7,4},{8,9},{9,10},{10,1... | collective-permute-start | bytes 393224 | tf_op jit(solution)/shard_map/ppermute | solution.py:47
  85.6 7.6 %collective-permute-start.1 = (bf16[512,128]{1,0:T(8,128)(2,1)S(1)}, bf16[512,128]{1,0:T(8,128)(2,1)S(1)}, u32[]{:S(2)}, u32[]{:S(2)}) collective-permute-start(bf16[512,128]{1,0:T(8,128)(2,1)S(1)} %get-tuple-element.36), channel_id=1, source_target_pairs={{0,2},{1,3},{2,0},{3,1},{4,6},{5,7},{6,4},{7,5},{8,10},{9,11},{10,... | collective-permute-start | bytes 393224 | tf_op jit(solution)/shard_map/ppermute | solution.py:47
  89.1 6.0 %collective-permute-start.2 = (bf16[512,128]{1,0:T(8,128)(2,1)S(1)}, bf16[512,128]{1,0:T(8,128)(2,1)S(1)}, u32[]{:S(2)}, u32[]{:S(2)}) collective-permute-start(bf16[512,128]{1,0:T(8,128)(2,1)S(1)} %get-tuple-element.35), channel_id=1, source_target_pairs={{0,3},{1,0},{2,1},{3,2},{4,7},{5,4},{6,5},{7,6},{8,11},{9,8},{10,9... | collective-permute-start | bytes 393224 | tf_op jit(solution)/shard_map/ppermute | solution.py:47
  123.1 48.7 %copy-start.1 = (bf16[2048,128]{1,0:T(8,128)(2,1)S(1)}, bf16[2048,128]{1,0:T(8,128)(2,1)}, u32[]{:S(2)}) copy-start(bf16[2048,128]{1,0:T(8,128)(2,1)} %bonds_ref.1) | copy-start | bytes 1572868
  123.1 48.6 %copy-start.6 = (bf16[256,128]{1,0:T(8,128)(2,1)S(1)}, bf16[256,128]{1,0:T(8,128)(2,1)}, u32[]{:S(2)}) copy-start(bf16[256,128]{1,0:T(8,128)(2,1)} %left_ref.1) | copy-start | bytes 196612
  123.1 48.6 %copy-start.7 = (bf16[256,128]{1,0:T(8,128)(2,1)S(1)}, bf16[256,128]{1,0:T(8,128)(2,1)}, u32[]{:S(2)}) copy-start(bf16[256,128]{1,0:T(8,128)(2,1)} %right_ref.1) | copy-start | bytes 196612
  123.1 48.6 %copy-start.8 = (bf16[64,128]{1,0:T(8,128)(2,1)S(1)}, bf16[64,128]{1,0:T(8,128)(2,1)}, u32[]{:S(2)}) copy-start(bf16[64,128]{1,0:T(8,128)(2,1)} %gate_ref.1) | copy-start | bytes 49156
  123.1 36.7 %all-to-all-start.3 = ((bf16[4,3,72,128]{3,2,1,0:T(8,128)(2,1)}), bf16[4,3,72,128]{3,2,1,0:T(8,128)(2,1)S(1)}, u32[]{:S(2)}, u32[]{:S(2)}) async-start(bf16[4,3,72,128]{3,2,1,0:T(8,128)(2,1)} %get-tuple-element.27), calls=%async_computation.3 | async-start | bytes 442368 | tf_op jit(solution)/shard_map/all_to_all | solution.py:36
  150.1 9.7 %collective-permute-start.8 = (bf16[2,72,128]{2,1,0:T(8,128)(2,1)S(1)}, bf16[2,72,128]{2,1,0:T(8,128)(2,1)S(1)}, u32[]{:S(2)}, u32[]{:S(2)}) collective-permute-start(bf16[2,72,128]{2,1,0:T(8,128)(2,1)S(1)} %get-tuple-element.28), channel_id=1, source_target_pairs={{0,508},{508,0},{16,12},{12,16},{32,28},{28,32},{48,44},{44,48},{6... | collective-permute-start | bytes 110600 | tf_op jit(solution)/shard_map/ppermute | solution.py:539
  150.8 9.0 %collective-permute-start.9 = (bf16[72,128]{1,0:T(8,128)(2,1)S(1)}, bf16[72,128]{1,0:T(8,128)(2,1)S(1)}, u32[]{:S(2)}, u32[]{:S(2)}) collective-permute-start(bf16[72,128]{1,0:T(8,128)(2,1)S(1)} %get-tuple-element.29), channel_id=1, source_target_pairs={{0,504},{504,0},{4,508},{508,4},{16,8},{8,16},{20,12},{12,20},{32,... | collective-permute-start | bytes 55304 | tf_op jit(solution)/shard_map/ppermute | solution.py:540
  171.7 1.0 copy-start.2

commit v3 on v2

--- a/solution.py
+++ b/solution.py
@@ -16,6 +16,7 @@
 SPAN = 4
 HALO = 3
 ROOM = 24 << 20
+WIDE = 58 << 20
 LEFT_FIRST = (((0,), (0,)), ((), ()))
 BOTH_LAST = (((1,), (1,)), ((), ()))
 
@@ -36,10 +37,6 @@
     return lax.all_to_all(
         value, axis, split_axis=0, concat_axis=0, tiled=True, axis_index_groups=groups
     )
-
-
-def for_each(value, axis):
-    return jnp.broadcast_to(value, (lax.axis_size(axis), *value.shape))
 
 
 def moved(value, axis, steps):
@@ -53,6 +50,48 @@
         below = (place - step) % count
         out += [(place, below), (below, place)]
     return out
+
+
+def entry_body(x_hbm, w_hbm, down_ref, out_ref, sems):
+    quarters = out_ref.shape[0]
+    bonds = x_hbm.shape[0] // quarters
+    inputs = w_hbm.shape[0]
+    copies = []
+    for q in range(quarters):
+        copies.append(
+            pltpu.make_async_copy(
+                x_hbm.at[pl.ds(q * bonds, bonds)], out_ref.at[q, pl.ds(0, bonds)], sems.at[2 * q]
+            )
+        )
+        copies.append(
+            pltpu.make_async_copy(w_hbm, out_ref.at[q, pl.ds(bonds, inputs)], sems.at[2 * q + 1])
+        )
+    for copy in copies:
+        copy.start()
+    down = down_ref[...].astype(F32).T.astype(BF16)
+    for q in range(quarters):
+        out_ref[q, bonds + inputs :] = down
+    for copy in copies:
+        copy.wait()
+
+
+def entry_call(x, w, down, quarters):
+    bonds, width = x.shape
+    rows = bonds // quarters + w.shape[0] + down.shape[1]
+    return pl.pallas_call(
+        entry_body,
+        out_shape=jax.ShapeDtypeStruct((quarters, rows, width), BF16),
+        in_specs=[
+            pl.BlockSpec(memory_space=pl.ANY),
+            pl.BlockSpec(memory_space=pl.ANY),
+            vmem(),
+        ],
+        out_specs=vmem(),
+        scratch_shapes=[pltpu.SemaphoreType.DMA((2 * quarters,))],
+        cost_estimate=pl.CostEstimate(flops=0, bytes_accessed=2_000_000, transcendentals=0),
+        compiler_params=pltpu.CompilerParams(vmem_limit_bytes=WIDE),
+        name="entry",
+    )(x, w, down)
 
 
 def angular_body(fill_ref, place_ref, pack_ref, hidden_ref, angular_ref):
@@ -96,7 +135,7 @@
 
 
 def contribution_body(
-    chunks, source_ref, slot_ref, label_ref, angular_ref, coef_hbm, out_ref, coef_ref, sems
+    chunks, group, source_ref, slot_ref, label_ref, angular_ref, coef_hbm, out_ref, coef_ref, sems
 ):
     channels, rows = angular_ref.shape[1:]
     half = channels // 2
@@ -116,27 +155,37 @@
         return carry
 
     lax.fori_loop(0, label_ref.shape[0] // 4, tag, 0)
+    blank = jnp.zeros((channels, rows), BF16)
     for c in range(chunks):
         copies[c].wait()
-
-        def multiply(step, carry):
-            for k in range(7):
-                pair = c * per_chunk + step * 7 + k
-                part = dot(angular_ref[source_ref[pair]], coef_ref[pair], BOTH_LAST)
+        for first in range(c * per_chunk, (c + 1) * per_chunk, group):
+            pairs = range(first, first + group)
+            left = []
+            right = []
+            for k, pair in enumerate(pairs):
+                value = angular_ref[source_ref[pair]]
+                sides = [value, blank] if k % 2 == 0 else [blank, value]
+                left.append(jnp.concatenate(sides, axis=1))
+            for k in range(0, group, 2):
+                sides = [coef_ref[first + k], coef_ref[first + k + 1]]
+                right.append(jnp.concatenate(sides, axis=1))
+            found = dot(jnp.concatenate(left, axis=0), jnp.concatenate(right, axis=0), BOTH_LAST)
+            for k, pair in enumerate(pairs):
+                column = k // 2 * rows
+                part = found[k * channels : (k + 1) * channels, column : column + rows]
                 part = part.astype(BF16).reshape(half, 2, rows)
                 out_ref[pl.ds(slot_ref[pair], half)] = part
-            return carry
-
-        lax.fori_loop(0, per_chunk // 7, multiply, 0)
 
 
 def contribution_call(sources, slots, labels, angular, coef):
     pairs = coef.shape[0]
-    chunks = next(c for c in (4, 2, 1) if pairs % (7 * c) == 0)
+    chunks, group = next(
+        (c, g) for g in (4, 2) for c in (4, 2, 1) if pairs % (c * g) == 0
+    )
     _, channels, rows = angular.shape
     stride = SLOTS * channels // 2 + 1
     return pl.pallas_call(
-        functools.partial(contribution_body, chunks),
+        functools.partial(contribution_body, chunks, group),
         out_shape=jax.ShapeDtypeStruct((labels.shape[0] * stride, 2, rows), BF16),
         in_specs=[
             smem(),
@@ -153,7 +202,7 @@
         cost_estimate=pl.CostEstimate(
             flops=60_000_000, bytes_accessed=5_000_000, transcendentals=0
         ),
-        compiler_params=pltpu.CompilerParams(vmem_limit_bytes=ROOM),
+        compiler_params=pltpu.CompilerParams(vmem_limit_bytes=WIDE),
         name="contribution",
     )(sources, slots, labels, angular, coef)
 
@@ -486,7 +535,7 @@
     feats = lax.axis_size("feat")
     space = lax.axis_index("space").astype(jnp.int32).reshape(1)
     feat = lax.axis_index("feat").astype(jnp.int32).reshape(1)
-    bonds, width = bond_state.shape
+    bonds, _ = bond_state.shape
     blocks = block_fill.shape[0]
     pairs = pair_source.shape[0]
     channels = w_down.shape[1] // feats
@@ -500,12 +549,8 @@
 
     lower = lax.ppermute(atom_state, "space", [(i, (i + 1) % spaces) for i in range(spaces)])
     upper = lax.ppermute(atom_state, "space", [((i + 1) % spaces, i) for i in range(spaces)])
-    parts = (
-        bond_state.reshape(feats, own_bonds, width),
-        for_each(w_in, "feat"),
-        for_each(w_down.T, "feat"),
-    )
-    entered = exchanged(jnp.concatenate(parts, axis=1), "feat")
+    entered = entry_call(bond_state, w_in, w_down, feats)
+    entered = exchanged(entered, "feat")
     owners = pair_owner[:, 0]
     before = lax.broadcasted_iota(jnp.int32, (pairs, pairs), 1) < lax.broadcasted_iota(
         jnp.int32, (pairs, pairs), 0
@@ -522,6 +567,7 @@
     entered, ends, slots, labels = lax.optimization_barrier((entered, ends, slots, labels))
     hidden, angular = angular_call(block_fill, feat, entered, own_bonds, blocks // feats, channels)
     angular = exchanged(angular, "feat")
+    angular, lower, upper = lax.optimization_barrier((angular, lower, upper))
     angular = angular.reshape(blocks, *angular.shape[2:])
     outgoing = contribution_call(pair_source, slots, labels, angular, pair_coef)
     outgoing, hidden = lax.optimization_barrier((outgoing, hidden))

time: 181 us -> 165 us (0.912)
  the two profiles are of different devices: /device:TPU:1 before, /device:TPU:6 now
where the time goes in v3:
time: 165 us; the launch traced here: 162 us
  starting transfers between devices  62.5 us (38%)
  waiting for transfers between devices  58.1 us (35%)
  Pallas kernels  22 us (13%)
  blocking collectives  12.1 us (7%)
  local copies, waits for them, and re-layouts  3.74 us (2%)
  other arithmetic  2.73 us (2%)
    all_to_all x4, waiting for transfers between devices, exchanged(): lax.all_to_all(value, axis, split_axis=0, concat_axis=0, tiled=True, axis...  47.3 us
    all_to_all x4, starting transfers between devices, exchanged(): lax.all_to_all(value, axis, split_axis=0, concat_axis=0, tiled=True, axis...  30.2 us
    ppermute x6, starting transfers between devices, moved(): lax.ppermute(value, axis, [(i, (i + steps) % count) for i in range(count)])  19 us
    all_to_all x1, blocking collectives, exchanged(): lax.all_to_all(value, axis, split_axis=0, concat_axis=0, tiled=True, axis...  12.1 us
    ppermute x6, waiting for transfers between devices, moved(): lax.ppermute(value, axis, [(i, (i + steps) % count) for i in range(count)])  9.09 us
    pallas_call x1, Pallas kernels, update_call(): pl.pallas_call(update_body, out_shape=(jax.ShapeDtypeStruct(bonds.shape,...  7.46 us
    ppermute x1, starting transfers between devices, local(): over = lax.ppermute(over, 'space', over_pairs)  7.11 us
    pallas_call x1, Pallas kernels, contribution_call(): pl.pallas_call(functools.partial(contribution_body, chunks, group), out_s...  4.85 us
  transfers between devices with their start and end apart: 14, of which 7 were waited for; matrix products, arithmetic and copies ran while one was open for 3% of the time, Pallas kernels for 4%

profile of v3, /device:TPU:6, one launch (start us, length us, event | category | flops | bytes accessed | tf_op | source)
XLA Modules:
  0.0 162.2 jit_solution(781465779589480591)
XLA Ops:
  0.6 1.9 %collective-permute-start = (bf16[64,512]{1,0:T(8,128)(2,1)}, bf16[64,512]{1,0:T(8,128)(2,1)S(1)}, u32[]{:S(2)}, u32[]{:S(2)}) collective-permute-start(bf16[64,512]{1,0:T(8,128)(2,1)} %param.25), channel_id=1, source_target_pairs={{0,4},{4,8},{8,12},{12,16},{16,20},{20,24},{24,28},{28,32},{32,36}... | collective-permute-start | bytes 196616 | tf_op jit(solution)/shard_map/ppermute | solution.py:550
  2.6 3.6 %collective-permute-start.1 = (bf16[64,512]{1,0:T(8,128)(2,1)}, bf16[64,512]{1,0:T(8,128)(2,1)S(1)}, u32[]{:S(2)}, u32[]{:S(2)}) collective-permute-start(bf16[64,512]{1,0:T(8,128)(2,1)} %param.25), channel_id=1, source_target_pairs={{4,0},{8,4},{12,8},{16,12},{20,16},{24,20},{28,24},{32,28},{36,32}... | collective-permute-start | bytes 196616 | tf_op jit(solution)/shard_map/ppermute | solution.py:551
  6.2 1.4 copy.21.down_ref
  7.6 3.1 %entry.1 = bf16[4,1088,128]{2,1,0:T(8,128)(2,1)} custom-call(bf16[2048,128]{1,0:T(8,128)(2,1)} %bonds_ref.1, bf16[512,128]{1,0:T(8,128)(2,1)} %w_hbm.1, bf16[128,64]{1,0:T(8,128)(2,1)} %copy.21.down_ref), custom_call_target="tpu_custom_call" | custom-call | bytes 2000000 | tf_op jit(solution)/shard_map/entry/pallas_call | solution.py:81
  10.8 4.6 %all-to-all-start = ((bf16[4,1088,128]{2,1,0:T(8,128)(2,1)}), bf16[4,1088,128]{2,1,0:T(8,128)(2,1)S(1)}, u32[]{:S(2)}, u32[]{:S(2)}) async-start(bf16[4,1088,128]{2,1,0:T(8,128)(2,1)} %entry.1), calls=%async_computation | async-start | bytes 2228224 | tf_op jit(solution)/shard_map/all_to_all | solution.py:37
  16.9 0.8 select_convert_fusion.label_ref
  17.7 13.9 %all-to-all-done.pack_ref = bf16[4,1088,128]{2,1,0:T(8,128)(2,1)S(1)} async-done(((bf16[4,1088,128]{2,1,0:T(8,128)(2,1)}), bf16[4,1088,128]{2,1,0:T(8,128)(2,1)S(1)}, u32[]{:S(2)}, u32[]{:S(2)}) %all-to-all-start) | async-done | bytes 1114144 | tf_op jit(solution)/shard_map/all_to_all | solution.py:37
  31.6 2.6 %angular.1 = (bf16[4,512,128]{2,1,0:T(8,128)(2,1)S(1)}, bf16[4,4,16,128]{3,2,1,0:T(8,128)(2,1)}) custom-call(s32[16]{0:T(128)S(1)} %copy-done.3, s32[1]{0:T(128)} %bitcast.place_ref, bf16[4,1088,128]{2,1,0:T(8,128)(2,1)S(1)} %all-to-all-done.pack_ref), custom_call_target="tpu_custom_call" | custom-call | flops 600000000 | bytes 2000000 | tf_op jit(solution)/shard_map/angular/pallas_call | solution.py:121
  34.2 3.3 %all-to-all-start.1 = ((bf16[4,4,16,128]{3,2,1,0:T(8,128)(2,1)}), bf16[4,4,16,128]{3,2,1,0:T(8,128)(2,1)S(1)}, u32[]{:S(2)}, u32[]{:S(2)}) async-start(bf16[4,4,16,128]{3,2,1,0:T(8,128)(2,1)} %get-tuple-element.24), calls=%async_computation.1 | async-start | bytes 131072 | tf_op jit(solution)/shard_map/all_to_all | solution.py:37
  37.5 5.6 %all-to-all-done.1 = bf16[4,4,16,128]{3,2,1,0:T(8,128)(2,1)S(1)} async-done(((bf16[4,4,16,128]{3,2,1,0:T(8,128)(2,1)}), bf16[4,4,16,128]{3,2,1,0:T(8,128)(2,1)S(1)}, u32[]{:S(2)}, u32[]{:S(2)}) %all-to-all-start.1) | async-done | bytes 65568 | tf_op jit(solution)/shard_map/all_to_all | solution.py:37
  43.1 0.6 copy-done.7
  43.7 4.9 %contribution.1 = bf16[2176,2,128]{2,1,0:T(2,128)(2,1)} custom-call(s32[112]{0:T(128)} %source_ref.1, s32[112]{0:T(128)} %multiply_add_fusion.slot_ref, bf16[128,2,128]{2,1,0:T(2,128)(2,1)} %select_convert_fusion.label_ref, bf16[16,16,128]{2,1,0:T(8,128)(2,1)} %bitcast.31, bf16[112,128,128]{2,1,0:T(8,128)(2,1)} %coef_hbm.1), custom_call_target="tpu_custom_call" | custom-call | flops 60000000 | bytes 5000000 | tf_op jit(solution)/shard_map/contribution/pallas_call | solution.py:187
  48.6 18.7 %all-to-all-start.2 = ((bf16[128,17,2,128]{3,2,1,0:T(2,128)(2,1)}), bf16[128,17,2,128]{3,2,1,0:T(2,128)(2,1)S(1)}, u32[]{:S(2)}, u32[]{:S(2)}) async-start(bf16[128,17,2,128]{3,2,1,0:T(2,128)(2,1)} %bitcast.29), calls=%async_computation.2 | async-start | bytes 2228224 | tf_op jit(solution)/shard_map/all_to_all | solution.py:37
  67.4 3.1 %collective-permute-start.4 = (bf16[512,128]{1,0:T(8,128)(2,1)S(1)}, bf16[512,128]{1,0:T(8,128)(2,1)S(1)}, u32[]{:S(2)}, u32[]{:S(2)}) collective-permute-start(bf16[512,128]{1,0:T(8,128)(2,1)S(1)} %get-tuple-element.41), channel_id=1, source_target_pairs={{0,3},{1,0},{2,1},{3,2},{4,7},{5,4},{6,5},{7,6},{8,11},{9,8},{10,9... | collective-permute-start | bytes 393224 | tf_op jit(solution)/shard_map/ppermute | solution.py:44
  70.5 3.4 %collective-permute-start.3 = (bf16[512,128]{1,0:T(8,128)(2,1)S(1)}, bf16[512,128]{1,0:T(8,128)(2,1)S(1)}, u32[]{:S(2)}, u32[]{:S(2)}) collective-permute-start(bf16[512,128]{1,0:T(8,128)(2,1)S(1)} %get-tuple-element.42), channel_id=1, source_target_pairs={{0,2},{1,3},{2,0},{3,1},{4,6},{5,7},{6,4},{7,5},{8,10},{9,11},{10,... | collective-permute-start | bytes 393224 | tf_op jit(solution)/shard_map/ppermute | solution.py:44
  73.9 1.9 %collective-permute-start.2 = (bf16[512,128]{1,0:T(8,128)(2,1)S(1)}, bf16[512,128]{1,0:T(8,128)(2,1)S(1)}, u32[]{:S(2)}, u32[]{:S(2)}) collective-permute-start(bf16[512,128]{1,0:T(8,128)(2,1)S(1)} %get-tuple-element.43), channel_id=1, source_target_pairs={{0,1},{1,2},{2,3},{3,0},{4,5},{5,6},{6,7},{7,4},{8,9},{9,10},{10,1... | collective-permute-start | bytes 393224 | tf_op jit(solution)/shard_map/ppermute | solution.py:44
  75.9 5.1 %collective-permute-start.7 = (bf16[64,1856]{1,0:T(8,128)(2,1)S(1)}, bf16[64,1856]{1,0:T(8,128)(2,1)S(1)}, u32[]{:S(2)}, u32[]{:S(2)}) collective-permute-start(bf16[64,1856]{1,0:T(8,128)(2,1)S(1)} %constant_dynamic-update-slice_fusion), channel_id=1, source_target_pairs={{0,3},{1,0},{2,1},{3,2},{4,7},{5,4},{6,5},{7,6},{8,11},{9,8},{10,9... | collective-permute-start | bytes 712712 | tf_op jit(solution)/shard_map/ppermute | solution.py:44
  81.1 2.8 %collective-permute-start.6 = (bf16[64,1856]{1,0:T(8,128)(2,1)S(1)}, bf16[64,1856]{1,0:T(8,128)(2,1)S(1)}, u32[]{:S(2)}, u32[]{:S(2)}) collective-permute-start(bf16[64,1856]{1,0:T(8,128)(2,1)S(1)} %constant_dynamic-update-slice_fusion), channel_id=1, source_target_pairs={{0,2},{1,3},{2,0},{3,1},{4,6},{5,7},{6,4},{7,5},{8,10},{9,11},{10,... | collective-permute-start | bytes 712712 | tf_op jit(solution)/shard_map/ppermute | solution.py:44
  83.8 2.8 %collective-permute-start.5 = (bf16[64,1856]{1,0:T(8,128)(2,1)S(1)}, bf16[64,1856]{1,0:T(8,128)(2,1)S(1)}, u32[]{:S(2)}, u32[]{:S(2)}) collective-permute-start(bf16[64,1856]{1,0:T(8,128)(2,1)S(1)} %constant_dynamic-update-slice_fusion), channel_id=1, source_target_pairs={{0,1},{1,2},{2,3},{3,0},{4,5},{5,6},{6,7},{7,4},{8,9},{9,10},{10,1... | collective-permute-start | bytes 712712 | tf_op jit(solution)/shard_map/ppermute | solution.py:44
  86.6 0.9 pad_maximum_fusion.1.hidden_ref
  87.5 3.5 %collective-permute-done.7 = bf16[64,1856]{1,0:T(8,128)(2,1)S(1)} collective-permute-done((bf16[64,1856]{1,0:T(8,128)(2,1)S(1)}, bf16[64,1856]{1,0:T(8,128)(2,1)S(1)}, u32[]{:S(2)}, u32[]{:S(2)}) %collective-permute-start.7) | collective-permute-done | bytes 237600 | tf_op jit(solution)/shard_map/ppermute | solution.py:44
  91.0 2.3 %collective-permute-done.6 = bf16[64,1856]{1,0:T(8,128)(2,1)S(1)} collective-permute-done((bf16[64,1856]{1,0:T(8,128)(2,1)S(1)}, bf16[64,1856]{1,0:T(8,128)(2,1)S(1)}, u32[]{:S(2)}, u32[]{:S(2)}) %collective-permute-start.6) | collective-permute-done | bytes 237600 | tf_op jit(solution)/shard_map/ppermute | solution.py:44
  93.3 3.3 %collective-permute-done.5 = bf16[64,1856]{1,0:T(8,128)(2,1)S(1)} collective-permute-done((bf16[64,1856]{1,0:T(8,128)(2,1)S(1)}, bf16[64,1856]{1,0:T(8,128)(2,1)S(1)}, u32[]{:S(2)}, u32[]{:S(2)}) %collective-permute-start.5) | collective-permute-done | bytes 237600 | tf_op jit(solution)/shard_map/ppermute | solution.py:44
  96.7 27.8 %all-to-all-done.2 = bf16[128,17,2,128]{3,2,1,0:T(2,128)(2,1)S(1)} async-done(((bf16[128,17,2,128]{3,2,1,0:T(2,128)(2,1)}), bf16[128,17,2,128]{3,2,1,0:T(2,128)(2,1)S(1)}, u32[]{:S(2)}, u32[]{:S(2)}) %all-to-all-start.2) | async-done | bytes 1114144 | tf_op jit(solution)/shard_map/all_to_all | solution.py:37
  124.6 3.8 %message.1 = (bf16[256,128]{1,0:T(8,128)(2,1)S(1)}, f32[3,72,128]{2,1,0:T(8,128)S(1)}, bf16[4,3,72,128]{3,2,1,0:T(8,128)(2,1)}, bf16[2,72,128]{2,1,0:T(8,128)(2,1)S(1)}, bf16[72,128]{1,0:T(8,128)(2,1)S(1)}) custom-call(s32[16]{0:T(128)S(1)} %copy-done.3, s32[1]{0:T(128)} %bitcast.1.place_ref, s32[2,2048]{1,0:T(2,128)S(1)} %copy-done.2, ...), custom_call_target="tpu_custom_call" | custom-call | flops 120000000 | bytes 2000000 | tf_op jit(solution)/shard_map/message/pallas_call | solution.py:307
  128.4 3.5 %all-to-all-start.3 = ((bf16[4,3,72,128]{3,2,1,0:T(8,128)(2,1)}), bf16[4,3,72,128]{3,2,1,0:T(8,128)(2,1)S(1)}, u32[]{:S(2)}, u32[]{:S(2)}) async-start(bf16[4,3,72,128]{3,2,1,0:T(8,128)(2,1)} %get-tuple-element.33), calls=%async_computation.3 | async-start | bytes 442368 | tf_op jit(solution)/shard_map/all_to_all | solution.py:37
  132.0 0.7 collective-permute-start.8
  132.6 7.1 %collective-permute-start.9 = (bf16[72,128]{1,0:T(8,128)(2,1)S(1)}, bf16[72,128]{1,0:T(8,128)(2,1)S(1)}, u32[]{:S(2)}, u32[]{:S(2)}) collective-permute-start(bf16[72,128]{1,0:T(8,128)(2,1)S(1)} %get-tuple-element.35), channel_id=1, source_target_pairs={{0,504},{504,0},{4,508},{508,4},{16,8},{8,16},{20,12},{12,20},{32,... | collective-permute-start | bytes 55304 | tf_op jit(solution)/shard_map/ppermute | solution.py:586
  139.7 1.7 %collective-permute-done.9.over_ref = bf16[72,128]{1,0:T(8,128)(2,1)S(1)} collective-permute-done((bf16[72,128]{1,0:T(8,128)(2,1)S(1)}, bf16[72,128]{1,0:T(8,128)(2,1)S(1)}, u32[]{:S(2)}, u32[]{:S(2)}) %collective-permute-start.9) | collective-permute-done | bytes 18464 | tf_op jit(solution)/shard_map/ppermute | solution.py:586
  141.6 12.1 %all_to_all.25.mean_ref = bf16[4,448,128]{2,1,0:T(8,128)(2,1)S(1)} all-to-all(bf16[4,448,128]{2,1,0:T(8,128)(2,1)S(1)} %mean.1), channel_id=1, replica_groups=mesh['space'=128,'feat'=4] {'feat'}, dimensions={0} | all-to-all | bytes 917504 | tf_op jit(solution)/shard_map/all_to_all | solution.py:37
  153.7 1.0 copy-done.1
  154.7 7.5 %update.1 = (bf16[2048,128]{1,0:T(8,128)(2,1)}, bf16[64,512]{1,0:T(8,128)(2,1)}) custom-call(s32[16]{0:T(128)S(1)} %copy-done.3, s32[1]{0:T(128)} %bitcast.place_ref, bf16[4,448,128]{2,1,0:T(8,128)(2,1)S(1)} %all_to_all.25.mean_ref, bf16[4,64,1856]{2,1,0:T(8,128)(2,1)S(1)} %pad_maximum_fusion.atoms_ref, bf16[256,128]{1,0:T(8,128)(2,1)S(1)} %copy-done.4, ...), custom_call_target="tpu_custom_call" | custom-call | flops 2500000000 | bytes 4000000 | tf_op jit(solution)/shard_map/update/pallas_call | solution.py:496
  (48 shorter events, 1.8 us)
Async XLA Ops:
  0.6 36.9 %collective-permute-start = (bf16[64,512]{1,0:T(8,128)(2,1)}, bf16[64,512]{1,0:T(8,128)(2,1)S(1)}, u32[]{:S(2)}, u32[]{:S(2)}) collective-permute-start(bf16[64,512]{1,0:T(8,128)(2,1)} %param.25), channel_id=1, source_target_pairs={{0,4},{4,8},{8,12},{12,16},{16,20},{20,24},{24,28},{28,32},{32,36}... | collective-permute-start | bytes 196616 | tf_op jit(solution)/shard_map/ppermute | solution.py:550
  2.6 35.0 %collective-permute-start.1 = (bf16[64,512]{1,0:T(8,128)(2,1)}, bf16[64,512]{1,0:T(8,128)(2,1)S(1)}, u32[]{:S(2)}, u32[]{:S(2)}) collective-permute-start(bf16[64,512]{1,0:T(8,128)(2,1)} %param.25), channel_id=1, source_target_pairs={{4,0},{8,4},{12,8},{16,12},{20,16},{24,20},{28,24},{32,28},{36,32}... | collective-permute-start | bytes 196616 | tf_op jit(solution)/shard_map/ppermute | solution.py:551
  10.8 4.6 %copy-start.12 = (s32[112,1]{0,1:T(1,128)S(1)}, s32[112,1]{0,1:T(1,128)}, u32[]{:S(2)}) copy-start(s32[112,1]{0,1:T(1,128)} %param.21) | copy-start | bytes 1348
  10.8 4.8 %copy-start.11 = (s32[112]{0:T(128)S(1)}, s32[112]{0:T(128)}, u32[]{:S(2)}) copy-start(s32[112]{0:T(128)} %param.22) | copy-start | bytes 1348
  10.8 4.9 %copy-start.2 = (s32[2,2048]{1,0:T(2,128)S(1)}, s32[2,2048]{1,0:T(2,128)}, u32[]{:S(2)}) copy-start(s32[2,2048]{1,0:T(2,128)} %ends_ref.1) | copy-start | bytes 49156
  10.8 20.8 %all-to-all-start = ((bf16[4,1088,128]{2,1,0:T(8,128)(2,1)}), bf16[4,1088,128]{2,1,0:T(8,128)(2,1)S(1)}, u32[]{:S(2)}, u32[]{:S(2)}) async-start(bf16[4,1088,128]{2,1,0:T(8,128)(2,1)} %entry.1), calls=%async_computation | async-start | bytes 2228224 | tf_op jit(solution)/shard_map/all_to_all | solution.py:37
  15.4 16.2 %copy-start.3 = (s32[16]{0:T(128)S(1)}, s32[16]{0:T(128)}, u32[]{:S(2)}) copy-start(s32[16]{0:T(128)} %fill_ref.5) | copy-start | bytes 196
  34.2 8.9 %all-to-all-start.1 = ((bf16[4,4,16,128]{3,2,1,0:T(8,128)(2,1)}), bf16[4,4,16,128]{3,2,1,0:T(8,128)(2,1)S(1)}, u32[]{:S(2)}, u32[]{:S(2)}) async-start(bf16[4,4,16,128]{3,2,1,0:T(8,128)(2,1)} %get-tuple-element.24), calls=%async_computation.1 | async-start | bytes 131072 | tf_op jit(solution)/shard_map/all_to_all | solution.py:37
  43.1 0.6 copy-start.7
  48.6 76.0 %all-to-all-start.2 = ((bf16[128,17,2,128]{3,2,1,0:T(2,128)(2,1)}), bf16[128,17,2,128]{3,2,1,0:T(2,128)(2,1)S(1)}, u32[]{:S(2)}, u32[]{:S(2)}) async-start(bf16[128,17,2,128]{3,2,1,0:T(2,128)(2,1)} %bitcast.29), calls=%async_computation.2 | async-start | bytes 2228224 | tf_op jit(solution)/shard_map/all_to_all | solution.py:37
  67.3 8.5 %copy-start.8 = (bf16[64,512]{1,0:T(8,128)(2,1)S(1)}, bf16[64,512]{1,0:T(8,128)(2,1)}, u32[]{:S(2)}) copy-start(bf16[64,512]{1,0:T(8,128)(2,1)} %param.25) | copy-start | bytes 196612
  67.4 8.5 %copy-start.9 = (bf16[64,256]{1,0:T(8,128)(2,1)S(1)}, bf16[64,256]{1,0:T(8,128)(2,1)}, u32[]{:S(2)}) copy-start(bf16[64,256]{1,0:T(8,128)(2,1)} %param.26) | copy-start | bytes 98308
  67.4 8.5 %copy-start.10 = (bf16[64,64]{1,0:T(8,128)(2,1)S(1)}, bf16[64,64]{1,0:T(8,128)(2,1)}, u32[]{:S(2)}) copy-start(bf16[64,64]{1,0:T(8,128)(2,1)} %param.24) | copy-start | bytes 24580
  67.4 16.4 %collective-permute-start.4 = (bf16[512,128]{1,0:T(8,128)(2,1)S(1)}, bf16[512,128]{1,0:T(8,128)(2,1)S(1)}, u32[]{:S(2)}, u32[]{:S(2)}) collective-permute-start(bf16[512,128]{1,0:T(8,128)(2,1)S(1)} %get-tuple-element.41), channel_id=1, source_target_pairs={{0,3},{1,0},{2,1},{3,2},{4,7},{5,4},{6,5},{7,6},{8,11},{9,8},{10,9... | collective-permute-start | bytes 393224 | tf_op jit(solution)/shard_map/ppermute | solution.py:44
  70.5 16.1 %collective-permute-start.3 = (bf16[512,128]{1,0:T(8,128)(2,1)S(1)}, bf16[512,128]{1,0:T(8,128)(2,1)S(1)}, u32[]{:S(2)}, u32[]{:S(2)}) collective-permute-start(bf16[512,128]{1,0:T(8,128)(2,1)S(1)} %get-tuple-element.42), channel_id=1, source_target_pairs={{0,2},{1,3},{2,0},{3,1},{4,6},{5,7},{6,4},{7,5},{8,10},{9,11},{10,... | collective-permute-start | bytes 393224 | tf_op jit(solution)/shard_map/ppermute | solution.py:44
  73.9 12.7 %collective-permute-start.2 = (bf16[512,128]{1,0:T(8,128)(2,1)S(1)}, bf16[512,128]{1,0:T(8,128)(2,1)S(1)}, u32[]{:S(2)}, u32[]{:S(2)}) collective-permute-start(bf16[512,128]{1,0:T(8,128)(2,1)S(1)} %get-tuple-element.43), channel_id=1, source_target_pairs={{0,1},{1,2},{2,3},{3,0},{4,5},{5,6},{6,7},{7,4},{8,9},{9,10},{10,1... | collective-permute-start | bytes 393224 | tf_op jit(solution)/shard_map/ppermute | solution.py:44
  75.9 15.0 %collective-permute-start.7 = (bf16[64,1856]{1,0:T(8,128)(2,1)S(1)}, bf16[64,1856]{1,0:T(8,128)(2,1)S(1)}, u32[]{:S(2)}, u32[]{:S(2)}) collective-permute-start(bf16[64,1856]{1,0:T(8,128)(2,1)S(1)} %constant_dynamic-update-slice_fusion), channel_id=1, source_target_pairs={{0,3},{1,0},{2,1},{3,2},{4,7},{5,4},{6,5},{7,6},{8,11},{9,8},{10,9... | collective-permute-start | bytes 712712 | tf_op jit(solution)/shard_map/ppermute | solution.py:44
  81.1 12.2 %collective-permute-start.6 = (bf16[64,1856]{1,0:T(8,128)(2,1)S(1)}, bf16[64,1856]{1,0:T(8,128)(2,1)S(1)}, u32[]{:S(2)}, u32[]{:S(2)}) collective-permute-start(bf16[64,1856]{1,0:T(8,128)(2,1)S(1)} %constant_dynamic-update-slice_fusion), channel_id=1, source_target_pairs={{0,2},{1,3},{2,0},{3,1},{4,6},{5,7},{6,4},{7,5},{8,10},{9,11},{10,... | collective-permute-start | bytes 712712 | tf_op jit(solution)/shard_map/ppermute | solution.py:44
  83.8 12.7 %collective-permute-start.5 = (bf16[64,1856]{1,0:T(8,128)(2,1)S(1)}, bf16[64,1856]{1,0:T(8,128)(2,1)S(1)}, u32[]{:S(2)}, u32[]{:S(2)}) collective-permute-start(bf16[64,1856]{1,0:T(8,128)(2,1)S(1)} %constant_dynamic-update-slice_fusion), channel_id=1, source_target_pairs={{0,1},{1,2},{2,3},{3,0},{4,5},{5,6},{6,7},{7,4},{8,9},{9,10},{10,1... | collective-permute-start | bytes 712712 | tf_op jit(solution)/shard_map/ppermute | solution.py:44
  128.4 25.3 %copy-start = (bf16[2048,128]{1,0:T(8,128)(2,1)S(1)}, bf16[2048,128]{1,0:T(8,128)(2,1)}, u32[]{:S(2)}) copy-start(bf16[2048,128]{1,0:T(8,128)(2,1)} %bonds_ref.1) | copy-start | bytes 1572868
  128.4 25.3 %copy-start.4 = (bf16[256,128]{1,0:T(8,128)(2,1)S(1)}, bf16[256,128]{1,0:T(8,128)(2,1)}, u32[]{:S(2)}) copy-start(bf16[256,128]{1,0:T(8,128)(2,1)} %left_ref.1) | copy-start | bytes 196612
  128.4 25.3 %copy-start.5 = (bf16[256,128]{1,0:T(8,128)(2,1)S(1)}, bf16[256,128]{1,0:T(8,128)(2,1)}, u32[]{:S(2)}) copy-start(bf16[256,128]{1,0:T(8,128)(2,1)} %right_ref.1) | copy-start | bytes 196612
  128.4 25.3 %copy-start.6 = (bf16[64,128]{1,0:T(8,128)(2,1)S(1)}, bf16[64,128]{1,0:T(8,128)(2,1)}, u32[]{:S(2)}) copy-start(bf16[64,128]{1,0:T(8,128)(2,1)} %gate_ref.1) | copy-start | bytes 49156
  128.4 13.0 %all-to-all-start.3 = ((bf16[4,3,72,128]{3,2,1,0:T(8,128)(2,1)}), bf16[4,3,72,128]{3,2,1,0:T(8,128)(2,1)S(1)}, u32[]{:S(2)}, u32[]{:S(2)}) async-start(bf16[4,3,72,128]{3,2,1,0:T(8,128)(2,1)} %get-tuple-element.33), calls=%async_computation.3 | async-start | bytes 442368 | tf_op jit(solution)/shard_map/all_to_all | solution.py:37
  132.0 9.5 %collective-permute-start.8 = (bf16[2,72,128]{2,1,0:T(8,128)(2,1)S(1)}, bf16[2,72,128]{2,1,0:T(8,128)(2,1)S(1)}, u32[]{:S(2)}, u32[]{:S(2)}) collective-permute-start(bf16[2,72,128]{2,1,0:T(8,128)(2,1)S(1)} %get-tuple-element.34), channel_id=1, source_target_pairs={{0,508},{508,0},{16,12},{12,16},{32,28},{28,32},{48,44},{44,48},{6... | collective-permute-start | bytes 110600 | tf_op jit(solution)/shard_map/ppermute | solution.py:585
  132.6 8.8 %collective-permute-start.9 = (bf16[72,128]{1,0:T(8,128)(2,1)S(1)}, bf16[72,128]{1,0:T(8,128)(2,1)S(1)}, u32[]{:S(2)}, u32[]{:S(2)}) collective-permute-start(bf16[72,128]{1,0:T(8,128)(2,1)S(1)} %get-tuple-element.35), channel_id=1, source_target_pairs={{0,504},{504,0},{4,508},{508,4},{16,8},{8,16},{20,12},{12,20},{32,... | collective-permute-start | bytes 55304 | tf_op jit(solution)/shard_map/ppermute | solution.py:586
  153.7 1.0 copy-start.1

commit v4 on v3

--- a/solution.py
+++ b/solution.py
@@ -52,42 +52,52 @@
     return out
 
 
-def entry_body(x_hbm, w_hbm, down_ref, out_ref, sems):
-    quarters = out_ref.shape[0]
-    bonds = x_hbm.shape[0] // quarters
-    inputs = w_hbm.shape[0]
-    copies = []
+def entry_body(x_hbm, w_hbm, down_ref, out_hbm, x_ref, w_ref, load_sems, store_sems):
+    quarters, rows = x_ref.shape[:2]
+    inputs = w_ref.shape[0]
+    loads = [pltpu.make_async_copy(w_hbm, w_ref, load_sems.at[quarters])]
     for q in range(quarters):
-        copies.append(
-            pltpu.make_async_copy(
-                x_hbm.at[pl.ds(q * bonds, bonds)], out_ref.at[q, pl.ds(0, bonds)], sems.at[2 * q]
-            )
-        )
-        copies.append(
-            pltpu.make_async_copy(w_hbm, out_ref.at[q, pl.ds(bonds, inputs)], sems.at[2 * q + 1])
-        )
-    for copy in copies:
-        copy.start()
-    down = down_ref[...].astype(F32).T.astype(BF16)
+        here = x_hbm.at[pl.ds(q * rows, rows)]
+        loads.append(pltpu.make_async_copy(here, x_ref.at[q], load_sems.at[q]))
+    for load in loads:
+        load.start()
+    stores = []
+
+    def store(source, q, first, kind):
+        there = out_hbm.at[q, pl.ds(first, source.shape[0])]
+        stores.append(pltpu.make_async_copy(source, there, store_sems.at[3 * q + kind]))
+        stores[-1].start()
+
     for q in range(quarters):
-        out_ref[q, bonds + inputs :] = down
-    for copy in copies:
+        store(down_ref, q, rows + inputs, 0)
+    loads[0].wait()
+    for q in range(quarters):
+        store(w_ref, q, rows, 1)
+    for q in range(quarters):
+        loads[1 + q].wait()
+        store(x_ref.at[q], q, 0, 2)
+    for copy in stores:
         copy.wait()
 
 
 def entry_call(x, w, down, quarters):
     bonds, width = x.shape
-    rows = bonds // quarters + w.shape[0] + down.shape[1]
+    rows = bonds // quarters
     return pl.pallas_call(
         entry_body,
-        out_shape=jax.ShapeDtypeStruct((quarters, rows, width), BF16),
+        out_shape=jax.ShapeDtypeStruct((quarters, rows + w.shape[0] + down.shape[0], width), BF16),
         in_specs=[
             pl.BlockSpec(memory_space=pl.ANY),
             pl.BlockSpec(memory_space=pl.ANY),
             vmem(),
         ],
-        out_specs=vmem(),
-        scratch_shapes=[pltpu.SemaphoreType.DMA((2 * quarters,))],
+        out_specs=pl.BlockSpec(memory_space=pl.ANY),
+        scratch_shapes=[
+            pltpu.VMEM((quarters, rows, width), BF16),
+            pltpu.VMEM(w.shape, BF16),
+            pltpu.SemaphoreType.DMA((quarters + 1,)),
+            pltpu.SemaphoreType.DMA((3 * quarters,)),
+        ],
         cost_estimate=pl.CostEstimate(flops=0, bytes_accessed=2_000_000, transcendentals=0),
         compiler_params=pltpu.CompilerParams(vmem_limit_bytes=WIDE),
         name="entry",
@@ -219,6 +229,7 @@
     over_ref,
     sums,
     padded,
+    chosen,
     labels,
     label_ref,
     sem,
@@ -237,6 +248,12 @@
     copy = pltpu.make_async_copy(labels, label_ref, sem)
     copy.start()
     sums[...] = jnp.zeros_like(sums)
+    ends = ends_ref[1:2, :]
+    high = ends // LANES
+    low = ends % LANES
+    chosen[...] = jnp.where(
+        low == lax.broadcasted_iota(jnp.int32, (LANES, bonds), 0), 1.0, 0.0
+    ).astype(BF16)
     copy.wait()
 
     def add(step, carry):
@@ -258,9 +275,6 @@
         masks.append(jnp.where(real[:1], 1.0, 0.0))
     message = jnp.concatenate(pieces, axis=1)
     mask = jnp.concatenate(masks, axis=1)
-    ends = ends_ref[1:2, :]
-    high = ends // LANES
-    low = ends % LANES
     stacked = []
     tallies = []
     for h in range(spans):
@@ -269,10 +283,7 @@
         tallies.append(jnp.where(here, mask, 0.0))
     tallies.append(jnp.zeros((16 - spans, bonds), F32))
     stacked.append(jnp.concatenate(tallies, axis=0).astype(BF16))
-    chosen = jnp.where(
-        low == lax.broadcasted_iota(jnp.int32, (LANES, bonds), 0), 1.0, 0.0
-    ).astype(BF16)
-    window = dot(jnp.concatenate(stacked, axis=0), chosen, BOTH_LAST)
+    window = dot(jnp.concatenate(stacked, axis=0), chosen[...], BOTH_LAST)
     counts = window[spans * channels : spans * channels + spans]
     upper = jnp.floor(counts * (1.0 / 256.0))
     lower = counts - 256.0 * upper
@@ -318,6 +329,7 @@
         scratch_shapes=[
             pltpu.VMEM((blocks + 1, channels, rows), F32),
             pltpu.VMEM((3 * HALO, depth, LANES), BF16),
+            pltpu.VMEM((LANES, blocks * rows), BF16),
             pltpu.VMEM((SLOTS, LANES), jnp.int32),
             pltpu.SMEM((SLOTS, LANES), jnp.int32),
             pltpu.SemaphoreType.DMA(()),
@@ -549,7 +561,7 @@
 
     lower = lax.ppermute(atom_state, "space", [(i, (i + 1) % spaces) for i in range(spaces)])
     upper = lax.ppermute(atom_state, "space", [((i + 1) % spaces, i) for i in range(spaces)])
-    entered = entry_call(bond_state, w_in, w_down, feats)
+    entered = entry_call(bond_state, w_in, w_down.T, feats)
     entered = exchanged(entered, "feat")
     owners = pair_owner[:, 0]
     before = lax.broadcasted_iota(jnp.int32, (pairs, pairs), 1) < lax.broadcasted_iota(

time: 165 us -> 163 us (0.988)
    unnamed x32 -> x31, local copies, waits for them, and re-layouts: 3.56 us -> 2.12 us
  transfers between devices with their start and end apart: 14 -> 14, of which waited for: 7 -> 7; matrix products, arithmetic and copies ran while one was open for 3% -> 2% of each run, Pallas kernels for 4% -> 3%
where the time goes in v4:
time: 163 us; the launch traced here: 160 us
  starting transfers between devices  62.5 us (38%)
  waiting for transfers between devices  58.1 us (36%)
  Pallas kernels  21.6 us (13%)
  blocking collectives  12.1 us (7%)
  other arithmetic  2.73 us (2%)
  local copies, waits for them, and re-layouts  2.31 us (1%)
    all_to_all x4, waiting for transfers between devices, exchanged(): lax.all_to_all(value, axis, split_axis=0, concat_axis=0, tiled=True, axis...  47.3 us
    all_to_all x4, starting transfers between devices, exchanged(): lax.all_to_all(value, axis, split_axis=0, concat_axis=0, tiled=True, axis...  30.2 us
    ppermute x6, starting transfers between devices, moved(): lax.ppermute(value, axis, [(i, (i + steps) % count) for i in range(count)])  19 us
    all_to_all x1, blocking collectives, exchanged(): lax.all_to_all(value, axis, split_axis=0, concat_axis=0, tiled=True, axis...  12.1 us
    ppermute x6, waiting for transfers between devices, moved(): lax.ppermute(value, axis, [(i, (i + steps) % count) for i in range(count)])  9.09 us
    pallas_call x1, Pallas kernels, update_call(): pl.pallas_call(update_body, out_shape=(jax.ShapeDtypeStruct(bonds.shape,...  7.46 us
    ppermute x1, starting transfers between devices, local(): over = lax.ppermute(over, 'space', over_pairs)  7.1 us
    pallas_call x1, Pallas kernels, contribution_call(): pl.pallas_call(functools.partial(contribution_body, chunks, group), out_s...  4.85 us
  transfers between devices with their start and end apart: 14, of which 7 were waited for; matrix products, arithmetic and copies ran while one was open for 2% of the time, Pallas kernels for 3%

profile of v4, /device:TPU:6, one launch (start us, length us, event | category | flops | bytes accessed | tf_op | source)
XLA Modules:
  0.0 160.4 jit_solution(4105589067632506327)
XLA Ops:
  0.6 1.9 %collective-permute-start = (bf16[64,512]{1,0:T(8,128)(2,1)}, bf16[64,512]{1,0:T(8,128)(2,1)S(1)}, u32[]{:S(2)}, u32[]{:S(2)}) collective-permute-start(bf16[64,512]{1,0:T(8,128)(2,1)} %param.25), channel_id=1, source_target_pairs={{0,4},{4,8},{8,12},{12,16},{16,20},{20,24},{24,28},{28,32},{32,36}... | collective-permute-start | bytes 196616 | tf_op jit(solution)/shard_map/ppermute | solution.py:562
  2.6 3.6 %collective-permute-start.1 = (bf16[64,512]{1,0:T(8,128)(2,1)}, bf16[64,512]{1,0:T(8,128)(2,1)S(1)}, u32[]{:S(2)}, u32[]{:S(2)}) collective-permute-start(bf16[64,512]{1,0:T(8,128)(2,1)} %param.25), channel_id=1, source_target_pairs={{4,0},{8,4},{12,8},{16,12},{20,16},{24,20},{28,24},{32,28},{36,32}... | collective-permute-start | bytes 196616 | tf_op jit(solution)/shard_map/ppermute | solution.py:563
  6.2 2.8 %entry.1 = bf16[4,1088,128]{2,1,0:T(8,128)(2,1)} custom-call(bf16[2048,128]{1,0:T(8,128)(2,1)} %bonds_ref.1, bf16[512,128]{1,0:T(8,128)(2,1)} %w_hbm.1, bf16[64,128]{1,0:T(8,128)(2,1)} %bitcast.39), custom_call_target="tpu_custom_call" | custom-call | bytes 2000000 | tf_op jit(solution)/shard_map/entry/pallas_call | solution.py:86
  9.0 4.6 %all-to-all-start = ((bf16[4,1088,128]{2,1,0:T(8,128)(2,1)}), bf16[4,1088,128]{2,1,0:T(8,128)(2,1)S(1)}, u32[]{:S(2)}, u32[]{:S(2)}) async-start(bf16[4,1088,128]{2,1,0:T(8,128)(2,1)} %entry.1), calls=%async_computation | async-start | bytes 2228224 | tf_op jit(solution)/shard_map/all_to_all | solution.py:37
  14.5 0.6 multiply_add_fusion.slot_ref
  15.1 0.8 select_convert_fusion.label_ref
  15.9 13.9 %all-to-all-done.pack_ref = bf16[4,1088,128]{2,1,0:T(8,128)(2,1)S(1)} async-done(((bf16[4,1088,128]{2,1,0:T(8,128)(2,1)}), bf16[4,1088,128]{2,1,0:T(8,128)(2,1)S(1)}, u32[]{:S(2)}, u32[]{:S(2)}) %all-to-all-start) | async-done | bytes 1114144 | tf_op jit(solution)/shard_map/all_to_all | solution.py:37
  29.8 2.6 %angular.1 = (bf16[4,512,128]{2,1,0:T(8,128)(2,1)S(1)}, bf16[4,4,16,128]{3,2,1,0:T(8,128)(2,1)}) custom-call(s32[16]{0:T(128)S(1)} %copy-done.3, s32[1]{0:T(128)} %bitcast.place_ref, bf16[4,1088,128]{2,1,0:T(8,128)(2,1)S(1)} %all-to-all-done.pack_ref), custom_call_target="tpu_custom_call" | custom-call | flops 600000000 | bytes 2000000 | tf_op jit(solution)/shard_map/angular/pallas_call | solution.py:131
  32.4 3.3 %all-to-all-start.1 = ((bf16[4,4,16,128]{3,2,1,0:T(8,128)(2,1)}), bf16[4,4,16,128]{3,2,1,0:T(8,128)(2,1)S(1)}, u32[]{:S(2)}, u32[]{:S(2)}) async-start(bf16[4,4,16,128]{3,2,1,0:T(8,128)(2,1)} %get-tuple-element.24), calls=%async_computation.1 | async-start | bytes 131072 | tf_op jit(solution)/shard_map/all_to_all | solution.py:37
  35.7 5.6 %all-to-all-done.1 = bf16[4,4,16,128]{3,2,1,0:T(8,128)(2,1)S(1)} async-done(((bf16[4,4,16,128]{3,2,1,0:T(8,128)(2,1)}), bf16[4,4,16,128]{3,2,1,0:T(8,128)(2,1)S(1)}, u32[]{:S(2)}, u32[]{:S(2)}) %all-to-all-start.1) | async-done | bytes 65568 | tf_op jit(solution)/shard_map/all_to_all | solution.py:37
  41.3 0.6 copy-done.7
  41.9 4.9 %contribution.1 = bf16[2176,2,128]{2,1,0:T(2,128)(2,1)} custom-call(s32[112]{0:T(128)} %source_ref.1, s32[112]{0:T(128)} %multiply_add_fusion.slot_ref, bf16[128,2,128]{2,1,0:T(2,128)(2,1)} %select_convert_fusion.label_ref, bf16[16,16,128]{2,1,0:T(8,128)(2,1)} %bitcast.32, bf16[112,128,128]{2,1,0:T(8,128)(2,1)} %coef_hbm.1), custom_call_target="tpu_custom_call" | custom-call | flops 60000000 | bytes 5000000 | tf_op jit(solution)/shard_map/contribution/pallas_call | solution.py:197
  46.8 18.7 %all-to-all-start.2 = ((bf16[128,17,2,128]{3,2,1,0:T(2,128)(2,1)}), bf16[128,17,2,128]{3,2,1,0:T(2,128)(2,1)S(1)}, u32[]{:S(2)}, u32[]{:S(2)}) async-start(bf16[128,17,2,128]{3,2,1,0:T(2,128)(2,1)} %bitcast.30), calls=%async_computation.2 | async-start | bytes 2228224 | tf_op jit(solution)/shard_map/all_to_all | solution.py:37
  65.6 3.1 %collective-permute-start.4 = (bf16[512,128]{1,0:T(8,128)(2,1)S(1)}, bf16[512,128]{1,0:T(8,128)(2,1)S(1)}, u32[]{:S(2)}, u32[]{:S(2)}) collective-permute-start(bf16[512,128]{1,0:T(8,128)(2,1)S(1)} %get-tuple-element.41), channel_id=1, source_target_pairs={{0,3},{1,0},{2,1},{3,2},{4,7},{5,4},{6,5},{7,6},{8,11},{9,8},{10,9... | collective-permute-start | bytes 393224 | tf_op jit(solution)/shard_map/ppermute | solution.py:44
  68.7 3.4 %collective-permute-start.3 = (bf16[512,128]{1,0:T(8,128)(2,1)S(1)}, bf16[512,128]{1,0:T(8,128)(2,1)S(1)}, u32[]{:S(2)}, u32[]{:S(2)}) collective-permute-start(bf16[512,128]{1,0:T(8,128)(2,1)S(1)} %get-tuple-element.42), channel_id=1, source_target_pairs={{0,2},{1,3},{2,0},{3,1},{4,6},{5,7},{6,4},{7,5},{8,10},{9,11},{10,... | collective-permute-start | bytes 393224 | tf_op jit(solution)/shard_map/ppermute | solution.py:44
  72.1 1.9 %collective-permute-start.2 = (bf16[512,128]{1,0:T(8,128)(2,1)S(1)}, bf16[512,128]{1,0:T(8,128)(2,1)S(1)}, u32[]{:S(2)}, u32[]{:S(2)}) collective-permute-start(bf16[512,128]{1,0:T(8,128)(2,1)S(1)} %get-tuple-element.43), channel_id=1, source_target_pairs={{0,1},{1,2},{2,3},{3,0},{4,5},{5,6},{6,7},{7,4},{8,9},{9,10},{10,1... | collective-permute-start | bytes 393224 | tf_op jit(solution)/shard_map/ppermute | solution.py:44
  74.1 5.1 %collective-permute-start.7 = (bf16[64,1856]{1,0:T(8,128)(2,1)S(1)}, bf16[64,1856]{1,0:T(8,128)(2,1)S(1)}, u32[]{:S(2)}, u32[]{:S(2)}) collective-permute-start(bf16[64,1856]{1,0:T(8,128)(2,1)S(1)} %constant_dynamic-update-slice_fusion), channel_id=1, source_target_pairs={{0,3},{1,0},{2,1},{3,2},{4,7},{5,4},{6,5},{7,6},{8,11},{9,8},{10,9... | collective-permute-start | bytes 712712 | tf_op jit(solution)/shard_map/ppermute | solution.py:44
  79.3 2.8 %collective-permute-start.6 = (bf16[64,1856]{1,0:T(8,128)(2,1)S(1)}, bf16[64,1856]{1,0:T(8,128)(2,1)S(1)}, u32[]{:S(2)}, u32[]{:S(2)}) collective-permute-start(bf16[64,1856]{1,0:T(8,128)(2,1)S(1)} %constant_dynamic-update-slice_fusion), channel_id=1, source_target_pairs={{0,2},{1,3},{2,0},{3,1},{4,6},{5,7},{6,4},{7,5},{8,10},{9,11},{10,... | collective-permute-start | bytes 712712 | tf_op jit(solution)/shard_map/ppermute | solution.py:44
  82.1 2.8 %collective-permute-start.5 = (bf16[64,1856]{1,0:T(8,128)(2,1)S(1)}, bf16[64,1856]{1,0:T(8,128)(2,1)S(1)}, u32[]{:S(2)}, u32[]{:S(2)}) collective-permute-start(bf16[64,1856]{1,0:T(8,128)(2,1)S(1)} %constant_dynamic-update-slice_fusion), channel_id=1, source_target_pairs={{0,1},{1,2},{2,3},{3,0},{4,5},{5,6},{6,7},{7,4},{8,9},{9,10},{10,1... | collective-permute-start | bytes 712712 | tf_op jit(solution)/shard_map/ppermute | solution.py:44
  84.9 0.9 pad_maximum_fusion.1.hidden_ref
  85.7 3.5 %collective-permute-done.7 = bf16[64,1856]{1,0:T(8,128)(2,1)S(1)} collective-permute-done((bf16[64,1856]{1,0:T(8,128)(2,1)S(1)}, bf16[64,1856]{1,0:T(8,128)(2,1)S(1)}, u32[]{:S(2)}, u32[]{:S(2)}) %collective-permute-start.7) | collective-permute-done | bytes 237600 | tf_op jit(solution)/shard_map/ppermute | solution.py:44
  89.2 2.3 %collective-permute-done.6 = bf16[64,1856]{1,0:T(8,128)(2,1)S(1)} collective-permute-done((bf16[64,1856]{1,0:T(8,128)(2,1)S(1)}, bf16[64,1856]{1,0:T(8,128)(2,1)S(1)}, u32[]{:S(2)}, u32[]{:S(2)}) %collective-permute-start.6) | collective-permute-done | bytes 237600 | tf_op jit(solution)/shard_map/ppermute | solution.py:44
  91.5 3.3 %collective-permute-done.5 = bf16[64,1856]{1,0:T(8,128)(2,1)S(1)} collective-permute-done((bf16[64,1856]{1,0:T(8,128)(2,1)S(1)}, bf16[64,1856]{1,0:T(8,128)(2,1)S(1)}, u32[]{:S(2)}, u32[]{:S(2)}) %collective-permute-start.5) | collective-permute-done | bytes 237600 | tf_op jit(solution)/shard_map/ppermute | solution.py:44
  95.0 27.8 %all-to-all-done.2 = bf16[128,17,2,128]{3,2,1,0:T(2,128)(2,1)S(1)} async-done(((bf16[128,17,2,128]{3,2,1,0:T(2,128)(2,1)}), bf16[128,17,2,128]{3,2,1,0:T(2,128)(2,1)S(1)}, u32[]{:S(2)}, u32[]{:S(2)}) %all-to-all-start.2) | async-done | bytes 1114144 | tf_op jit(solution)/shard_map/all_to_all | solution.py:37
  122.8 3.9 %message.1 = (bf16[256,128]{1,0:T(8,128)(2,1)S(1)}, f32[3,72,128]{2,1,0:T(8,128)S(1)}, bf16[4,3,72,128]{3,2,1,0:T(8,128)(2,1)}, bf16[2,72,128]{2,1,0:T(8,128)(2,1)S(1)}, bf16[72,128]{1,0:T(8,128)(2,1)S(1)}) custom-call(s32[16]{0:T(128)S(1)} %copy-done.3, s32[1]{0:T(128)} %bitcast.1.place_ref, s32[2,2048]{1,0:T(2,128)S(1)} %copy-done.2, ...), custom_call_target="tpu_custom_call" | custom-call | flops 120000000 | bytes 2000000 | tf_op jit(solution)/shard_map/message/pallas_call | solution.py:318
  126.7 3.5 %all-to-all-start.3 = ((bf16[4,3,72,128]{3,2,1,0:T(8,128)(2,1)}), bf16[4,3,72,128]{3,2,1,0:T(8,128)(2,1)S(1)}, u32[]{:S(2)}, u32[]{:S(2)}) async-start(bf16[4,3,72,128]{3,2,1,0:T(8,128)(2,1)} %get-tuple-element.33), calls=%async_computation.3 | async-start | bytes 442368 | tf_op jit(solution)/shard_map/all_to_all | solution.py:37
  130.2 0.7 collective-permute-start.8
  130.9 7.1 %collective-permute-start.9 = (bf16[72,128]{1,0:T(8,128)(2,1)S(1)}, bf16[72,128]{1,0:T(8,128)(2,1)S(1)}, u32[]{:S(2)}, u32[]{:S(2)}) collective-permute-start(bf16[72,128]{1,0:T(8,128)(2,1)S(1)} %get-tuple-element.35), channel_id=1, source_target_pairs={{0,504},{504,0},{4,508},{508,4},{16,8},{8,16},{20,12},{12,20},{32,... | collective-permute-start | bytes 55304 | tf_op jit(solution)/shard_map/ppermute | solution.py:598
  138.0 1.7 %collective-permute-done.9.over_ref = bf16[72,128]{1,0:T(8,128)(2,1)S(1)} collective-permute-done((bf16[72,128]{1,0:T(8,128)(2,1)S(1)}, bf16[72,128]{1,0:T(8,128)(2,1)S(1)}, u32[]{:S(2)}, u32[]{:S(2)}) %collective-permute-start.9) | collective-permute-done | bytes 18464 | tf_op jit(solution)/shard_map/ppermute | solution.py:598
  139.8 12.1 %all_to_all.25.mean_ref = bf16[4,448,128]{2,1,0:T(8,128)(2,1)S(1)} all-to-all(bf16[4,448,128]{2,1,0:T(8,128)(2,1)S(1)} %mean.1), channel_id=1, replica_groups=mesh['space'=128,'feat'=4] {'feat'}, dimensions={0} | all-to-all | bytes 917504 | tf_op jit(solution)/shard_map/all_to_all | solution.py:37
  151.9 1.0 copy-done.1
  152.9 7.5 %update.1 = (bf16[2048,128]{1,0:T(8,128)(2,1)}, bf16[64,512]{1,0:T(8,128)(2,1)}) custom-call(s32[16]{0:T(128)S(1)} %copy-done.3, s32[1]{0:T(128)} %bitcast.place_ref, bf16[4,448,128]{2,1,0:T(8,128)(2,1)S(1)} %all_to_all.25.mean_ref, bf16[4,64,1856]{2,1,0:T(8,128)(2,1)S(1)} %pad_maximum_fusion.atoms_ref, bf16[256,128]{1,0:T(8,128)(2,1)S(1)} %copy-done.4, ...), custom_call_target="tpu_custom_call" | custom-call | flops 2500000000 | bytes 4000000 | tf_op jit(solution)/shard_map/update/pallas_call | solution.py:508
  (47 shorter events, 1.2 us)
Async XLA Ops:
  0.6 35.1 %collective-permute-start = (bf16[64,512]{1,0:T(8,128)(2,1)}, bf16[64,512]{1,0:T(8,128)(2,1)S(1)}, u32[]{:S(2)}, u32[]{:S(2)}) collective-permute-start(bf16[64,512]{1,0:T(8,128)(2,1)} %param.25), channel_id=1, source_target_pairs={{0,4},{4,8},{8,12},{12,16},{16,20},{20,24},{24,28},{28,32},{32,36}... | collective-permute-start | bytes 196616 | tf_op jit(solution)/shard_map/ppermute | solution.py:562
  2.6 33.2 %collective-permute-start.1 = (bf16[64,512]{1,0:T(8,128)(2,1)}, bf16[64,512]{1,0:T(8,128)(2,1)S(1)}, u32[]{:S(2)}, u32[]{:S(2)}) collective-permute-start(bf16[64,512]{1,0:T(8,128)(2,1)} %param.25), channel_id=1, source_target_pairs={{4,0},{8,4},{12,8},{16,12},{20,16},{24,20},{28,24},{32,28},{36,32}... | collective-permute-start | bytes 196616 | tf_op jit(solution)/shard_map/ppermute | solution.py:563
  9.0 4.6 %copy-start.12 = (s32[112,1]{0,1:T(1,128)S(1)}, s32[112,1]{0,1:T(1,128)}, u32[]{:S(2)}) copy-start(s32[112,1]{0,1:T(1,128)} %param.21) | copy-start | bytes 1348
  9.0 4.8 %copy-start.11 = (s32[112]{0:T(128)S(1)}, s32[112]{0:T(128)}, u32[]{:S(2)}) copy-start(s32[112]{0:T(128)} %param.22) | copy-start | bytes 1348
  9.0 4.9 %copy-start.2 = (s32[2,2048]{1,0:T(2,128)S(1)}, s32[2,2048]{1,0:T(2,128)}, u32[]{:S(2)}) copy-start(s32[2,2048]{1,0:T(2,128)} %ends_ref.1) | copy-start | bytes 49156
  9.0 20.8 %all-to-all-start = ((bf16[4,1088,128]{2,1,0:T(8,128)(2,1)}), bf16[4,1088,128]{2,1,0:T(8,128)(2,1)S(1)}, u32[]{:S(2)}, u32[]{:S(2)}) async-start(bf16[4,1088,128]{2,1,0:T(8,128)(2,1)} %entry.1), calls=%async_computation | async-start | bytes 2228224 | tf_op jit(solution)/shard_map/all_to_all | solution.py:37
  13.6 16.2 %copy-start.3 = (s32[16]{0:T(128)S(1)}, s32[16]{0:T(128)}, u32[]{:S(2)}) copy-start(s32[16]{0:T(128)} %fill_ref.5) | copy-start | bytes 196
  32.4 8.9 %all-to-all-start.1 = ((bf16[4,4,16,128]{3,2,1,0:T(8,128)(2,1)}), bf16[4,4,16,128]{3,2,1,0:T(8,128)(2,1)S(1)}, u32[]{:S(2)}, u32[]{:S(2)}) async-start(bf16[4,4,16,128]{3,2,1,0:T(8,128)(2,1)} %get-tuple-element.24), calls=%async_computation.1 | async-start | bytes 131072 | tf_op jit(solution)/shard_map/all_to_all | solution.py:37
  41.3 0.6 copy-start.7
  46.8 76.0 %all-to-all-start.2 = ((bf16[128,17,2,128]{3,2,1,0:T(2,128)(2,1)}), bf16[128,17,2,128]{3,2,1,0:T(2,128)(2,1)S(1)}, u32[]{:S(2)}, u32[]{:S(2)}) async-start(bf16[128,17,2,128]{3,2,1,0:T(2,128)(2,1)} %bitcast.30), calls=%async_computation.2 | async-start | bytes 2228224 | tf_op jit(solution)/shard_map/all_to_all | solution.py:37
  65.6 8.5 %copy-start.8 = (bf16[64,512]{1,0:T(8,128)(2,1)S(1)}, bf16[64,512]{1,0:T(8,128)(2,1)}, u32[]{:S(2)}) copy-start(bf16[64,512]{1,0:T(8,128)(2,1)} %param.25) | copy-start | bytes 196612
  65.6 8.5 %copy-start.9 = (bf16[64,256]{1,0:T(8,128)(2,1)S(1)}, bf16[64,256]{1,0:T(8,128)(2,1)}, u32[]{:S(2)}) copy-start(bf16[64,256]{1,0:T(8,128)(2,1)} %param.26) | copy-start | bytes 98308
  65.6 8.5 %copy-start.10 = (bf16[64,64]{1,0:T(8,128)(2,1)S(1)}, bf16[64,64]{1,0:T(8,128)(2,1)}, u32[]{:S(2)}) copy-start(bf16[64,64]{1,0:T(8,128)(2,1)} %param.24) | copy-start | bytes 24580
  65.6 16.4 %collective-permute-start.4 = (bf16[512,128]{1,0:T(8,128)(2,1)S(1)}, bf16[512,128]{1,0:T(8,128)(2,1)S(1)}, u32[]{:S(2)}, u32[]{:S(2)}) collective-permute-start(bf16[512,128]{1,0:T(8,128)(2,1)S(1)} %get-tuple-element.41), channel_id=1, source_target_pairs={{0,3},{1,0},{2,1},{3,2},{4,7},{5,4},{6,5},{7,6},{8,11},{9,8},{10,9... | collective-permute-start | bytes 393224 | tf_op jit(solution)/shard_map/ppermute | solution.py:44
  68.7 16.1 %collective-permute-start.3 = (bf16[512,128]{1,0:T(8,128)(2,1)S(1)}, bf16[512,128]{1,0:T(8,128)(2,1)S(1)}, u32[]{:S(2)}, u32[]{:S(2)}) collective-permute-start(bf16[512,128]{1,0:T(8,128)(2,1)S(1)} %get-tuple-element.42), channel_id=1, source_target_pairs={{0,2},{1,3},{2,0},{3,1},{4,6},{5,7},{6,4},{7,5},{8,10},{9,11},{10,... | collective-permute-start | bytes 393224 | tf_op jit(solution)/shard_map/ppermute | solution.py:44
  72.1 12.7 %collective-permute-start.2 = (bf16[512,128]{1,0:T(8,128)(2,1)S(1)}, bf16[512,128]{1,0:T(8,128)(2,1)S(1)}, u32[]{:S(2)}, u32[]{:S(2)}) collective-permute-start(bf16[512,128]{1,0:T(8,128)(2,1)S(1)} %get-tuple-element.43), channel_id=1, source_target_pairs={{0,1},{1,2},{2,3},{3,0},{4,5},{5,6},{6,7},{7,4},{8,9},{9,10},{10,1... | collective-permute-start | bytes 393224 | tf_op jit(solution)/shard_map/ppermute | solution.py:44
  74.1 15.0 %collective-permute-start.7 = (bf16[64,1856]{1,0:T(8,128)(2,1)S(1)}, bf16[64,1856]{1,0:T(8,128)(2,1)S(1)}, u32[]{:S(2)}, u32[]{:S(2)}) collective-permute-start(bf16[64,1856]{1,0:T(8,128)(2,1)S(1)} %constant_dynamic-update-slice_fusion), channel_id=1, source_target_pairs={{0,3},{1,0},{2,1},{3,2},{4,7},{5,4},{6,5},{7,6},{8,11},{9,8},{10,9... | collective-permute-start | bytes 712712 | tf_op jit(solution)/shard_map/ppermute | solution.py:44
  79.3 12.2 %collective-permute-start.6 = (bf16[64,1856]{1,0:T(8,128)(2,1)S(1)}, bf16[64,1856]{1,0:T(8,128)(2,1)S(1)}, u32[]{:S(2)}, u32[]{:S(2)}) collective-permute-start(bf16[64,1856]{1,0:T(8,128)(2,1)S(1)} %constant_dynamic-update-slice_fusion), channel_id=1, source_target_pairs={{0,2},{1,3},{2,0},{3,1},{4,6},{5,7},{6,4},{7,5},{8,10},{9,11},{10,... | collective-permute-start | bytes 712712 | tf_op jit(solution)/shard_map/ppermute | solution.py:44
  82.1 12.7 %collective-permute-start.5 = (bf16[64,1856]{1,0:T(8,128)(2,1)S(1)}, bf16[64,1856]{1,0:T(8,128)(2,1)S(1)}, u32[]{:S(2)}, u32[]{:S(2)}) collective-permute-start(bf16[64,1856]{1,0:T(8,128)(2,1)S(1)} %constant_dynamic-update-slice_fusion), channel_id=1, source_target_pairs={{0,1},{1,2},{2,3},{3,0},{4,5},{5,6},{6,7},{7,4},{8,9},{9,10},{10,1... | collective-permute-start | bytes 712712 | tf_op jit(solution)/shard_map/ppermute | solution.py:44
  126.6 25.3 %copy-start = (bf16[2048,128]{1,0:T(8,128)(2,1)S(1)}, bf16[2048,128]{1,0:T(8,128)(2,1)}, u32[]{:S(2)}) copy-start(bf16[2048,128]{1,0:T(8,128)(2,1)} %bonds_ref.1) | copy-start | bytes 1572868
  126.6 25.3 %copy-start.4 = (bf16[256,128]{1,0:T(8,128)(2,1)S(1)}, bf16[256,128]{1,0:T(8,128)(2,1)}, u32[]{:S(2)}) copy-start(bf16[256,128]{1,0:T(8,128)(2,1)} %left_ref.1) | copy-start | bytes 196612
  126.6 25.2 %copy-start.5 = (bf16[256,128]{1,0:T(8,128)(2,1)S(1)}, bf16[256,128]{1,0:T(8,128)(2,1)}, u32[]{:S(2)}) copy-start(bf16[256,128]{1,0:T(8,128)(2,1)} %right_ref.1) | copy-start | bytes 196612
  126.7 25.2 %copy-start.6 = (bf16[64,128]{1,0:T(8,128)(2,1)S(1)}, bf16[64,128]{1,0:T(8,128)(2,1)}, u32[]{:S(2)}) copy-start(bf16[64,128]{1,0:T(8,128)(2,1)} %gate_ref.1) | copy-start | bytes 49156
  126.7 13.0 %all-to-all-start.3 = ((bf16[4,3,72,128]{3,2,1,0:T(8,128)(2,1)}), bf16[4,3,72,128]{3,2,1,0:T(8,128)(2,1)S(1)}, u32[]{:S(2)}, u32[]{:S(2)}) async-start(bf16[4,3,72,128]{3,2,1,0:T(8,128)(2,1)} %get-tuple-element.33), calls=%async_computation.3 | async-start | bytes 442368 | tf_op jit(solution)/shard_map/all_to_all | solution.py:37
  130.2 9.5 %collective-permute-start.8 = (bf16[2,72,128]{2,1,0:T(8,128)(2,1)S(1)}, bf16[2,72,128]{2,1,0:T(8,128)(2,1)S(1)}, u32[]{:S(2)}, u32[]{:S(2)}) collective-permute-start(bf16[2,72,128]{2,1,0:T(8,128)(2,1)S(1)} %get-tuple-element.34), channel_id=1, source_target_pairs={{0,508},{508,0},{16,12},{12,16},{32,28},{28,32},{48,44},{44,48},{6... | collective-permute-start | bytes 110600 | tf_op jit(solution)/shard_map/ppermute | solution.py:597
  130.9 8.8 %collective-permute-start.9 = (bf16[72,128]{1,0:T(8,128)(2,1)S(1)}, bf16[72,128]{1,0:T(8,128)(2,1)S(1)}, u32[]{:S(2)}, u32[]{:S(2)}) collective-permute-start(bf16[72,128]{1,0:T(8,128)(2,1)S(1)} %get-tuple-element.35), channel_id=1, source_target_pairs={{0,504},{504,0},{4,508},{508,4},{16,8},{8,16},{20,12},{12,20},{32,... | collective-permute-start | bytes 55304 | tf_op jit(solution)/shard_map/ppermute | solution.py:598
  151.9 1.0 copy-start.1

commit v5 on v4

--- a/solution.py
+++ b/solution.py
@@ -342,7 +342,7 @@
     )(fill, place, ends, arrived)
 
 
-def mean_body(place_ref, own_ref, near_ref, next_ref, over_ref, message_ref, out_ref, total):
+def mean_body(place_ref, own_ref, near_ref, next_ref, over_ref, out_ref, total):
     copies = out_ref.shape[0]
     depth = own_ref.shape[1]
     channels = (depth - 2 * SPAN) // SPAN
@@ -367,18 +367,15 @@
             row = (k * SPAN + h) * channels
             for m in range(copies):
                 out_ref[m, row : row + channels] = mean
-    for m in range(copies):
-        out_ref[m, HALO * width :] = message_ref[...]
-
-
-def mean_call(place, own, near, beside, over, message, copies):
+
+
+def mean_call(place, own, near, beside, over, copies):
     depth = own.shape[1]
     width = depth - 2 * SPAN
-    rows = HALO * width + message.shape[0]
     return pl.pallas_call(
         mean_body,
-        out_shape=jax.ShapeDtypeStruct((copies, rows, LANES), BF16),
-        in_specs=[smem()] + [vmem()] * 5,
+        out_shape=jax.ShapeDtypeStruct((copies, HALO * width, LANES), BF16),
+        in_specs=[smem()] + [vmem()] * 4,
         out_specs=vmem(),
         scratch_shapes=[pltpu.VMEM((HALO, depth, LANES), F32)],
         cost_estimate=pl.CostEstimate(
@@ -386,7 +383,7 @@
         ),
         compiler_params=pltpu.CompilerParams(vmem_limit_bytes=ROOM),
         name="mean",
-    )(place, own, near, beside, over, message)
+    )(place, own, near, beside, over)
 
 
 def update_body(
@@ -400,17 +397,14 @@
     hidden_ref,
     bonds_ref,
     ends_ref,
-    bond_out_ref,
-    atom_out_ref,
-    table_left,
-    table_right,
-    kept,
+    *refs,
 ):
     quarters = mean_ref.shape[0]
+    pieces = refs[:quarters]
+    bond_out_ref, atom_out_ref, table_left, table_right, kept, message_ref = refs[quarters:]
     channels = gate_ref.shape[0] // quarters
     feat = place_ref[0]
     near = [(feat - q + quarters) % quarters for q in range(quarters)]
-    after = HALO * SPAN * channels
     features = atoms_ref.shape[1]
     window = HALO * SPAN * LANES
     inputs = quarters * features
@@ -458,6 +452,8 @@
         table_right[:, c * width : (c + 1) * width] = table[:, width:]
     own = pl.multiple_of(feat * features, features)
     atom_out_ref[...] = kept[pl.ds(own, features), :]
+    for k in range(quarters):
+        message_ref[near[k]] = pieces[k][...]
     bonds = bonds_ref.shape[0]
     per_quarter = bonds // quarters
     lane = lax.broadcasted_iota(jnp.int32, (tile, tile), 1)
@@ -477,7 +473,7 @@
             [
                 jnp.concatenate(
                     [
-                        mean_ref[f, after + b * channels : after + (b + 1) * channels]
+                        message_ref[f, b * channels : (b + 1) * channels]
                         for f in range(quarters)
                     ],
                     axis=0,
@@ -500,7 +496,7 @@
             ).astype(BF16)
 
 
-def update_call(fill, place, mean, atoms, left, right, gate, hidden, bonds, ends):
+def update_call(fill, place, mean, atoms, left, right, gate, hidden, bonds, ends, messages):
     features = atoms.shape[1]
     window = HALO * SPAN * LANES
     width = left.shape[1]
@@ -511,19 +507,20 @@
             jax.ShapeDtypeStruct(bonds.shape, BF16),
             jax.ShapeDtypeStruct((features, window // HALO), BF16),
         ),
-        in_specs=[smem(), smem()] + [vmem()] * 8,
+        in_specs=[smem(), smem()] + [vmem()] * (8 + len(messages)),
         out_specs=(vmem(), vmem()),
         scratch_shapes=[
             pltpu.VMEM((tile, window // tile * width), BF16),
             pltpu.VMEM((tile, window // tile * width), BF16),
             pltpu.VMEM((mean.shape[0] * features, window // HALO), BF16),
+            pltpu.VMEM((len(messages), *messages[0].shape), BF16),
         ],
         cost_estimate=pl.CostEstimate(
             flops=2_500_000_000, bytes_accessed=4_000_000, transcendentals=2_000_000
         ),
         compiler_params=pltpu.CompilerParams(vmem_limit_bytes=ROOM),
         name="update",
-    )(fill, place, mean, atoms, left, right, gate, hidden, bonds, ends)
+    )(fill, place, mean, atoms, left, right, gate, hidden, bonds, ends, *messages)
 
 
 def local(
@@ -596,10 +593,21 @@
     near = exchanged(near, "space", near_groups)
     beside = lax.ppermute(beside, "space", next_pairs)
     over = lax.ppermute(over, "space", over_pairs)
-    mean = mean_call(space, own, near, beside, over, message, feats)
+    messages = [message if k == 0 else moved(message, "feat", k) for k in range(feats)]
+    mean = mean_call(space, own, near, beside, over, feats)
     mean = exchanged(mean, "feat")
     return update_call(
-        block_fill, feat, mean, atoms, w_left, w_right, w_gate, hidden, bond_state, ends
+        block_fill,
+        feat,
+        mean,
+        atoms,
+        w_left,
+        w_right,
+        w_gate,
+        hidden,
+        bond_state,
+        ends,
+        messages,
     )
 
 

time: 163 us -> 172 us (1.055)
  the two profiles are of different devices: /device:TPU:6 before, /device:TPU:24 now
where the time goes in v5:
time: 172 us; the launch traced here: 171 us
  starting transfers between devices  85.3 us (50%)
  waiting for transfers between devices  57.3 us (33%)
  Pallas kernels  22.3 us (13%)
  other arithmetic  2.69 us (2%)
  local copies, waits for them, and re-layouts  2.3 us (1%)
    all_to_all x5, waiting for transfers between devices, exchanged(): lax.all_to_all(value, axis, split_axis=0, concat_axis=0, tiled=True, axis...  38.3 us
    all_to_all x5, starting transfers between devices, exchanged(): lax.all_to_all(value, axis, split_axis=0, concat_axis=0, tiled=True, axis...  33.8 us
    ppermute x9, starting transfers between devices, moved(): lax.ppermute(value, axis, [(i, (i + steps) % count) for i in range(count)])  29.1 us
    ppermute x1, starting transfers between devices, local(): lax.ppermute(atom_state, 'space', [((i + 1) % spaces, i) for i in range(s...  13 us
    ppermute x9, waiting for transfers between devices, moved(): lax.ppermute(value, axis, [(i, (i + steps) % count) for i in range(count)])  12 us
    pallas_call x1, Pallas kernels, update_call(): pl.pallas_call(update_body, out_shape=(jax.ShapeDtypeStruct(bonds.shape,...  7.44 us
    ppermute x1, waiting for transfers between devices, local(): over = lax.ppermute(over, 'space', over_pairs)  7.05 us
    ppermute x1, starting transfers between devices, local(): beside = lax.ppermute(beside, 'space', next_pairs)  5.47 us
  transfers between devices with their start and end apart: 18, of which 8 were waited for; matrix products, arithmetic and copies ran while one was open for 2% of the time, Pallas kernels for 3%

profile of v5, /device:TPU:24, one launch (start us, length us, event | category | flops | bytes accessed | tf_op | source)
XLA Modules:
  0.0 170.9 jit_solution(13545881515359019162)
XLA Ops:
  0.6 1.9 %collective-permute-start = (bf16[64,512]{1,0:T(8,128)(2,1)}, bf16[64,512]{1,0:T(8,128)(2,1)S(1)}, u32[]{:S(2)}, u32[]{:S(2)}) collective-permute-start(bf16[64,512]{1,0:T(8,128)(2,1)} %param.25), channel_id=1, source_target_pairs={{0,4},{4,8},{8,12},{12,16},{16,20},{20,24},{24,28},{28,32},{32,36}... | collective-permute-start | bytes 196616 | tf_op jit(solution)/shard_map/ppermute | solution.py:559
  2.6 13.0 %collective-permute-start.1 = (bf16[64,512]{1,0:T(8,128)(2,1)}, bf16[64,512]{1,0:T(8,128)(2,1)S(1)}, u32[]{:S(2)}, u32[]{:S(2)}) collective-permute-start(bf16[64,512]{1,0:T(8,128)(2,1)} %param.25), channel_id=1, source_target_pairs={{4,0},{8,4},{12,8},{16,12},{20,16},{24,20},{28,24},{32,28},{36,32}... | collective-permute-start | bytes 196616 | tf_op jit(solution)/shard_map/ppermute | solution.py:560
  15.6 2.8 %entry.1 = bf16[4,1088,128]{2,1,0:T(8,128)(2,1)} custom-call(bf16[2048,128]{1,0:T(8,128)(2,1)} %bonds_ref.1, bf16[512,128]{1,0:T(8,128)(2,1)} %w_hbm.1, bf16[64,128]{1,0:T(8,128)(2,1)} %bitcast.39), custom_call_target="tpu_custom_call" | custom-call | bytes 2000000 | tf_op jit(solution)/shard_map/entry/pallas_call | solution.py:86
  18.4 4.8 %all-to-all-start = ((bf16[4,1088,128]{2,1,0:T(8,128)(2,1)}), bf16[4,1088,128]{2,1,0:T(8,128)(2,1)S(1)}, u32[]{:S(2)}, u32[]{:S(2)}) async-start(bf16[4,1088,128]{2,1,0:T(8,128)(2,1)} %entry.1), calls=%async_computation | async-start | bytes 2228224 | tf_op jit(solution)/shard_map/all_to_all | solution.py:37
  25.5 6.9 %all-to-all-done.pack_ref = bf16[4,1088,128]{2,1,0:T(8,128)(2,1)S(1)} async-done(((bf16[4,1088,128]{2,1,0:T(8,128)(2,1)}), bf16[4,1088,128]{2,1,0:T(8,128)(2,1)S(1)}, u32[]{:S(2)}, u32[]{:S(2)}) %all-to-all-start) | async-done | bytes 1114144 | tf_op jit(solution)/shard_map/all_to_all | solution.py:37
  32.4 2.6 %angular.1 = (bf16[4,512,128]{2,1,0:T(8,128)(2,1)S(1)}, bf16[4,4,16,128]{3,2,1,0:T(8,128)(2,1)}) custom-call(s32[16]{0:T(128)S(1)} %copy-done.3, s32[1]{0:T(128)} %bitcast.place_ref, bf16[4,1088,128]{2,1,0:T(8,128)(2,1)S(1)} %all-to-all-done.pack_ref), custom_call_target="tpu_custom_call" | custom-call | flops 600000000 | bytes 2000000 | tf_op jit(solution)/shard_map/angular/pallas_call | solution.py:131
  35.0 5.3 %all-to-all-start.1 = ((bf16[4,4,16,128]{3,2,1,0:T(8,128)(2,1)}), bf16[4,4,16,128]{3,2,1,0:T(8,128)(2,1)S(1)}, u32[]{:S(2)}, u32[]{:S(2)}) async-start(bf16[4,4,16,128]{3,2,1,0:T(8,128)(2,1)} %get-tuple-element.24), calls=%async_computation.1 | async-start | bytes 131072 | tf_op jit(solution)/shard_map/all_to_all | solution.py:37
  40.4 3.5 %all-to-all-done.1 = bf16[4,4,16,128]{3,2,1,0:T(8,128)(2,1)S(1)} async-done(((bf16[4,4,16,128]{3,2,1,0:T(8,128)(2,1)}), bf16[4,4,16,128]{3,2,1,0:T(8,128)(2,1)S(1)}, u32[]{:S(2)}, u32[]{:S(2)}) %all-to-all-start.1) | async-done | bytes 65568 | tf_op jit(solution)/shard_map/all_to_all | solution.py:37
  44.6 4.8 %contribution.1 = bf16[2176,2,128]{2,1,0:T(2,128)(2,1)} custom-call(s32[112]{0:T(128)} %source_ref.1, s32[112]{0:T(128)} %multiply_add_fusion.slot_ref, bf16[128,2,128]{2,1,0:T(2,128)(2,1)} %select_convert_fusion.label_ref, bf16[16,16,128]{2,1,0:T(8,128)(2,1)} %bitcast.32, bf16[112,128,128]{2,1,0:T(8,128)(2,1)} %coef_hbm.1), custom_call_target="tpu_custom_call" | custom-call | flops 60000000 | bytes 5000000 | tf_op jit(solution)/shard_map/contribution/pallas_call | solution.py:197
  49.4 14.7 %all-to-all-start.2 = ((bf16[128,17,2,128]{3,2,1,0:T(2,128)(2,1)}), bf16[128,17,2,128]{3,2,1,0:T(2,128)(2,1)S(1)}, u32[]{:S(2)}, u32[]{:S(2)}) async-start(bf16[128,17,2,128]{3,2,1,0:T(2,128)(2,1)} %bitcast.30), calls=%async_computation.2 | async-start | bytes 2228224 | tf_op jit(solution)/shard_map/all_to_all | solution.py:37
  64.2 2.3 %collective-permute-start.4 = (bf16[512,128]{1,0:T(8,128)(2,1)S(1)}, bf16[512,128]{1,0:T(8,128)(2,1)S(1)}, u32[]{:S(2)}, u32[]{:S(2)}) collective-permute-start(bf16[512,128]{1,0:T(8,128)(2,1)S(1)} %get-tuple-element.41), channel_id=1, source_target_pairs={{0,3},{1,0},{2,1},{3,2},{4,7},{5,4},{6,5},{7,6},{8,11},{9,8},{10,9... | collective-permute-start | bytes 393224 | tf_op jit(solution)/shard_map/ppermute | solution.py:44
  66.5 5.0 %collective-permute-start.3 = (bf16[512,128]{1,0:T(8,128)(2,1)S(1)}, bf16[512,128]{1,0:T(8,128)(2,1)S(1)}, u32[]{:S(2)}, u32[]{:S(2)}) collective-permute-start(bf16[512,128]{1,0:T(8,128)(2,1)S(1)} %get-tuple-element.42), channel_id=1, source_target_pairs={{0,2},{1,3},{2,0},{3,1},{4,6},{5,7},{6,4},{7,5},{8,10},{9,11},{10,... | collective-permute-start | bytes 393224 | tf_op jit(solution)/shard_map/ppermute | solution.py:44
  71.6 3.1 %collective-permute-start.2 = (bf16[512,128]{1,0:T(8,128)(2,1)S(1)}, bf16[512,128]{1,0:T(8,128)(2,1)S(1)}, u32[]{:S(2)}, u32[]{:S(2)}) collective-permute-start(bf16[512,128]{1,0:T(8,128)(2,1)S(1)} %get-tuple-element.43), channel_id=1, source_target_pairs={{0,1},{1,2},{2,3},{3,0},{4,5},{5,6},{6,7},{7,4},{8,9},{9,10},{10,1... | collective-permute-start | bytes 393224 | tf_op jit(solution)/shard_map/ppermute | solution.py:44
  74.7 2.8 %collective-permute-start.7 = (bf16[64,1856]{1,0:T(8,128)(2,1)S(1)}, bf16[64,1856]{1,0:T(8,128)(2,1)S(1)}, u32[]{:S(2)}, u32[]{:S(2)}) collective-permute-start(bf16[64,1856]{1,0:T(8,128)(2,1)S(1)} %constant_dynamic-update-slice_fusion), channel_id=1, source_target_pairs={{0,3},{1,0},{2,1},{3,2},{4,7},{5,4},{6,5},{7,6},{8,11},{9,8},{10,9... | collective-permute-start | bytes 712712 | tf_op jit(solution)/shard_map/ppermute | solution.py:44
  77.5 2.5 %collective-permute-start.6 = (bf16[64,1856]{1,0:T(8,128)(2,1)S(1)}, bf16[64,1856]{1,0:T(8,128)(2,1)S(1)}, u32[]{:S(2)}, u32[]{:S(2)}) collective-permute-start(bf16[64,1856]{1,0:T(8,128)(2,1)S(1)} %constant_dynamic-update-slice_fusion), channel_id=1, source_target_pairs={{0,2},{1,3},{2,0},{3,1},{4,6},{5,7},{6,4},{7,5},{8,10},{9,11},{10,... | collective-permute-start | bytes 712712 | tf_op jit(solution)/shard_map/ppermute | solution.py:44
  80.1 4.5 %collective-permute-start.5 = (bf16[64,1856]{1,0:T(8,128)(2,1)S(1)}, bf16[64,1856]{1,0:T(8,128)(2,1)S(1)}, u32[]{:S(2)}, u32[]{:S(2)}) collective-permute-start(bf16[64,1856]{1,0:T(8,128)(2,1)S(1)} %constant_dynamic-update-slice_fusion), channel_id=1, source_target_pairs={{0,1},{1,2},{2,3},{3,0},{4,5},{5,6},{6,7},{7,4},{8,9},{9,10},{10,1... | collective-permute-start | bytes 712712 | tf_op jit(solution)/shard_map/ppermute | solution.py:44
  84.6 0.9 pad_maximum_fusion.1.hidden_ref
  85.5 4.3 %collective-permute-done.7 = bf16[64,1856]{1,0:T(8,128)(2,1)S(1)} collective-permute-done((bf16[64,1856]{1,0:T(8,128)(2,1)S(1)}, bf16[64,1856]{1,0:T(8,128)(2,1)S(1)}, u32[]{:S(2)}, u32[]{:S(2)}) %collective-permute-start.7) | collective-permute-done | bytes 237600 | tf_op jit(solution)/shard_map/ppermute | solution.py:44
  89.8 2.5 %collective-permute-done.5 = bf16[64,1856]{1,0:T(8,128)(2,1)S(1)} collective-permute-done((bf16[64,1856]{1,0:T(8,128)(2,1)S(1)}, bf16[64,1856]{1,0:T(8,128)(2,1)S(1)}, u32[]{:S(2)}, u32[]{:S(2)}) %collective-permute-start.5) | collective-permute-done | bytes 237600 | tf_op jit(solution)/shard_map/ppermute | solution.py:44
  92.4 27.8 %all-to-all-done.2 = bf16[128,17,2,128]{3,2,1,0:T(2,128)(2,1)S(1)} async-done(((bf16[128,17,2,128]{3,2,1,0:T(2,128)(2,1)}), bf16[128,17,2,128]{3,2,1,0:T(2,128)(2,1)S(1)}, u32[]{:S(2)}, u32[]{:S(2)}) %all-to-all-start.2) | async-done | bytes 1114144 | tf_op jit(solution)/shard_map/all_to_all | solution.py:37
  120.2 3.8 %message.1 = (bf16[256,128]{1,0:T(8,128)(2,1)S(1)}, f32[3,72,128]{2,1,0:T(8,128)S(1)}, bf16[4,3,72,128]{3,2,1,0:T(8,128)(2,1)}, bf16[2,72,128]{2,1,0:T(8,128)(2,1)S(1)}, bf16[72,128]{1,0:T(8,128)(2,1)S(1)}) custom-call(s32[16]{0:T(128)S(1)} %copy-done.3, s32[1]{0:T(128)} %bitcast.1.place_ref, s32[2,2048]{1,0:T(2,128)S(1)} %copy-done.2, ...), custom_call_target="tpu_custom_call" | custom-call | flops 120000000 | bytes 2000000 | tf_op jit(solution)/shard_map/message/pallas_call | solution.py:318
  124.0 3.6 %all-to-all-start.3 = ((bf16[4,3,72,128]{3,2,1,0:T(8,128)(2,1)}), bf16[4,3,72,128]{3,2,1,0:T(8,128)(2,1)S(1)}, u32[]{:S(2)}, u32[]{:S(2)}) async-start(bf16[4,3,72,128]{3,2,1,0:T(8,128)(2,1)} %get-tuple-element.33), calls=%async_computation.3 | async-start | bytes 442368 | tf_op jit(solution)/shard_map/all_to_all | solution.py:37
  127.6 5.5 %collective-permute-start.8 = (bf16[2,72,128]{2,1,0:T(8,128)(2,1)S(1)}, bf16[2,72,128]{2,1,0:T(8,128)(2,1)S(1)}, u32[]{:S(2)}, u32[]{:S(2)}) collective-permute-start(bf16[2,72,128]{2,1,0:T(8,128)(2,1)S(1)} %get-tuple-element.34), channel_id=1, source_target_pairs={{0,508},{508,0},{16,12},{12,16},{32,28},{28,32},{48,44},{44,48},{6... | collective-permute-start | bytes 110600 | tf_op jit(solution)/shard_map/ppermute | solution.py:594
  133.1 1.9 %collective-permute-start.9 = (bf16[72,128]{1,0:T(8,128)(2,1)S(1)}, bf16[72,128]{1,0:T(8,128)(2,1)S(1)}, u32[]{:S(2)}, u32[]{:S(2)}) collective-permute-start(bf16[72,128]{1,0:T(8,128)(2,1)S(1)} %get-tuple-element.35), channel_id=1, source_target_pairs={{0,504},{504,0},{4,508},{508,4},{16,8},{8,16},{20,12},{12,20},{32,... | collective-permute-start | bytes 55304 | tf_op jit(solution)/shard_map/ppermute | solution.py:595
  135.0 7.0 %collective-permute-done.9.over_ref = bf16[72,128]{1,0:T(8,128)(2,1)S(1)} collective-permute-done((bf16[72,128]{1,0:T(8,128)(2,1)S(1)}, bf16[72,128]{1,0:T(8,128)(2,1)S(1)}, u32[]{:S(2)}, u32[]{:S(2)}) %collective-permute-start.9) | collective-permute-done | bytes 18464 | tf_op jit(solution)/shard_map/ppermute | solution.py:595
  142.8 5.4 %all-to-all-start.4 = ((bf16[4,192,128]{2,1,0:T(8,128)(2,1)}), bf16[4,192,128]{2,1,0:T(8,128)(2,1)S(1)}, u32[]{:S(2)}, u32[]{:S(2)}) async-start(bf16[4,192,128]{2,1,0:T(8,128)(2,1)} %mean.1), calls=%async_computation.4 | async-start | bytes 393216 | tf_op jit(solution)/shard_map/all_to_all | solution.py:37
  148.2 1.9 %collective-permute-start.10 = (bf16[256,128]{1,0:T(8,128)(2,1)S(1)}, bf16[256,128]{1,0:T(8,128)(2,1)S(1)}, u32[]{:S(2)}, u32[]{:S(2)}) collective-permute-start(bf16[256,128]{1,0:T(8,128)(2,1)S(1)} %get-tuple-element.39.refs_0_), channel_id=1, source_target_pairs={{0,1},{1,2},{2,3},{3,0},{4,5},{5,6},{6,7},{7,4},{8,9},{9,10},{10,1... | collective-permute-start | bytes 196616 | tf_op jit(solution)/shard_map/ppermute | solution.py:44
  150.2 4.8 %collective-permute-start.11 = (bf16[256,128]{1,0:T(8,128)(2,1)S(1)}, bf16[256,128]{1,0:T(8,128)(2,1)S(1)}, u32[]{:S(2)}, u32[]{:S(2)}) collective-permute-start(bf16[256,128]{1,0:T(8,128)(2,1)S(1)} %get-tuple-element.39.refs_0_), channel_id=1, source_target_pairs={{0,2},{1,3},{2,0},{3,1},{4,6},{5,7},{6,4},{7,5},{8,10},{9,11},{10,... | collective-permute-start | bytes 196616 | tf_op jit(solution)/shard_map/ppermute | solution.py:44
  155.0 2.1 %collective-permute-start.12 = (bf16[256,128]{1,0:T(8,128)(2,1)S(1)}, bf16[256,128]{1,0:T(8,128)(2,1)S(1)}, u32[]{:S(2)}, u32[]{:S(2)}) collective-permute-start(bf16[256,128]{1,0:T(8,128)(2,1)S(1)} %get-tuple-element.39.refs_0_), channel_id=1, source_target_pairs={{0,3},{1,0},{2,1},{3,2},{4,7},{5,4},{6,5},{7,6},{8,11},{9,8},{10,9... | collective-permute-start | bytes 196616 | tf_op jit(solution)/shard_map/ppermute | solution.py:44
  157.9 4.5 %collective-permute-done.12.refs_3_ = bf16[256,128]{1,0:T(8,128)(2,1)S(1)} collective-permute-done((bf16[256,128]{1,0:T(8,128)(2,1)S(1)}, bf16[256,128]{1,0:T(8,128)(2,1)S(1)}, u32[]{:S(2)}, u32[]{:S(2)}) %collective-permute-start.12) | collective-permute-done | bytes 65568 | tf_op jit(solution)/shard_map/ppermute | solution.py:44
  162.4 1.0 copy-done.1
  163.4 7.4 %update.1 = (bf16[2048,128]{1,0:T(8,128)(2,1)}, bf16[64,512]{1,0:T(8,128)(2,1)}) custom-call(s32[16]{0:T(128)S(1)} %copy-done.3, s32[1]{0:T(128)} %bitcast.place_ref, bf16[4,192,128]{2,1,0:T(8,128)(2,1)S(1)} %all-to-all-done.4.mean_ref, bf16[4,64,1856]{2,1,0:T(8,128)(2,1)S(1)} %pad_maximum_fusion.atoms_ref, bf16[256,128]{1,0:T(8,128)(2,1)S(1)} %copy-done.4, ...), custom_call_target="tpu_custom_call" | custom-call | flops 2500000000 | bytes 4000000 | tf_op jit(solution)/shard_map/update/pallas_call | solution.py:504
  (54 shorter events, 4.6 us)
Async XLA Ops:
  0.6 39.7 %collective-permute-start = (bf16[64,512]{1,0:T(8,128)(2,1)}, bf16[64,512]{1,0:T(8,128)(2,1)S(1)}, u32[]{:S(2)}, u32[]{:S(2)}) collective-permute-start(bf16[64,512]{1,0:T(8,128)(2,1)} %param.25), channel_id=1, source_target_pairs={{0,4},{4,8},{8,12},{12,16},{16,20},{20,24},{24,28},{28,32},{32,36}... | collective-permute-start | bytes 196616 | tf_op jit(solution)/shard_map/ppermute | solution.py:559
  2.6 37.8 %collective-permute-start.1 = (bf16[64,512]{1,0:T(8,128)(2,1)}, bf16[64,512]{1,0:T(8,128)(2,1)S(1)}, u32[]{:S(2)}, u32[]{:S(2)}) collective-permute-start(bf16[64,512]{1,0:T(8,128)(2,1)} %param.25), channel_id=1, source_target_pairs={{4,0},{8,4},{12,8},{16,12},{20,16},{24,20},{28,24},{32,28},{36,32}... | collective-permute-start | bytes 196616 | tf_op jit(solution)/shard_map/ppermute | solution.py:560
  18.4 4.9 %copy-start.12 = (s32[112,1]{0,1:T(1,128)S(1)}, s32[112,1]{0,1:T(1,128)}, u32[]{:S(2)}) copy-start(s32[112,1]{0,1:T(1,128)} %param.21) | copy-start | bytes 1348
  18.4 5.0 %copy-start.11 = (s32[112]{0:T(128)S(1)}, s32[112]{0:T(128)}, u32[]{:S(2)}) copy-start(s32[112]{0:T(128)} %param.22) | copy-start | bytes 1348
  18.4 5.2 %copy-start.2 = (s32[2,2048]{1,0:T(2,128)S(1)}, s32[2,2048]{1,0:T(2,128)}, u32[]{:S(2)}) copy-start(s32[2,2048]{1,0:T(2,128)} %ends_ref.1) | copy-start | bytes 49156
  18.4 14.0 %all-to-all-start = ((bf16[4,1088,128]{2,1,0:T(8,128)(2,1)}), bf16[4,1088,128]{2,1,0:T(8,128)(2,1)S(1)}, u32[]{:S(2)}, u32[]{:S(2)}) async-start(bf16[4,1088,128]{2,1,0:T(8,128)(2,1)} %entry.1), calls=%async_computation | async-start | bytes 2228224 | tf_op jit(solution)/shard_map/all_to_all | solution.py:37
  23.3 9.2 %copy-start.3 = (s32[16]{0:T(128)S(1)}, s32[16]{0:T(128)}, u32[]{:S(2)}) copy-start(s32[16]{0:T(128)} %fill_ref.5) | copy-start | bytes 196
  35.0 8.9 %all-to-all-start.1 = ((bf16[4,4,16,128]{3,2,1,0:T(8,128)(2,1)}), bf16[4,4,16,128]{3,2,1,0:T(8,128)(2,1)S(1)}, u32[]{:S(2)}, u32[]{:S(2)}) async-start(bf16[4,4,16,128]{3,2,1,0:T(8,128)(2,1)} %get-tuple-element.24), calls=%async_computation.1 | async-start | bytes 131072 | tf_op jit(solution)/shard_map/all_to_all | solution.py:37
  43.9 0.6 copy-start.7
  49.4 70.8 %all-to-all-start.2 = ((bf16[128,17,2,128]{3,2,1,0:T(2,128)(2,1)}), bf16[128,17,2,128]{3,2,1,0:T(2,128)(2,1)S(1)}, u32[]{:S(2)}, u32[]{:S(2)}) async-start(bf16[128,17,2,128]{3,2,1,0:T(2,128)(2,1)} %bitcast.30), calls=%async_computation.2 | async-start | bytes 2228224 | tf_op jit(solution)/shard_map/all_to_all | solution.py:37
  64.1 10.5 %copy-start.8 = (bf16[64,512]{1,0:T(8,128)(2,1)S(1)}, bf16[64,512]{1,0:T(8,128)(2,1)}, u32[]{:S(2)}) copy-start(bf16[64,512]{1,0:T(8,128)(2,1)} %param.25) | copy-start | bytes 196612
  64.1 10.6 %copy-start.9 = (bf16[64,256]{1,0:T(8,128)(2,1)S(1)}, bf16[64,256]{1,0:T(8,128)(2,1)}, u32[]{:S(2)}) copy-start(bf16[64,256]{1,0:T(8,128)(2,1)} %param.26) | copy-start | bytes 98308
  64.1 10.6 %copy-start.10 = (bf16[64,64]{1,0:T(8,128)(2,1)S(1)}, bf16[64,64]{1,0:T(8,128)(2,1)}, u32[]{:S(2)}) copy-start(bf16[64,64]{1,0:T(8,128)(2,1)} %param.24) | copy-start | bytes 24580
  64.2 15.9 %collective-permute-start.4 = (bf16[512,128]{1,0:T(8,128)(2,1)S(1)}, bf16[512,128]{1,0:T(8,128)(2,1)S(1)}, u32[]{:S(2)}, u32[]{:S(2)}) collective-permute-start(bf16[512,128]{1,0:T(8,128)(2,1)S(1)} %get-tuple-element.41), channel_id=1, source_target_pairs={{0,3},{1,0},{2,1},{3,2},{4,7},{5,4},{6,5},{7,6},{8,11},{9,8},{10,9... | collective-permute-start | bytes 393224 | tf_op jit(solution)/shard_map/ppermute | solution.py:44
  66.5 18.1 %collective-permute-start.3 = (bf16[512,128]{1,0:T(8,128)(2,1)S(1)}, bf16[512,128]{1,0:T(8,128)(2,1)S(1)}, u32[]{:S(2)}, u32[]{:S(2)}) collective-permute-start(bf16[512,128]{1,0:T(8,128)(2,1)S(1)} %get-tuple-element.42), channel_id=1, source_target_pairs={{0,2},{1,3},{2,0},{3,1},{4,6},{5,7},{6,4},{7,5},{8,10},{9,11},{10,... | collective-permute-start | bytes 393224 | tf_op jit(solution)/shard_map/ppermute | solution.py:44
  71.6 13.1 %collective-permute-start.2 = (bf16[512,128]{1,0:T(8,128)(2,1)S(1)}, bf16[512,128]{1,0:T(8,128)(2,1)S(1)}, u32[]{:S(2)}, u32[]{:S(2)}) collective-permute-start(bf16[512,128]{1,0:T(8,128)(2,1)S(1)} %get-tuple-element.43), channel_id=1, source_target_pairs={{0,1},{1,2},{2,3},{3,0},{4,5},{5,6},{6,7},{7,4},{8,9},{9,10},{10,1... | collective-permute-start | bytes 393224 | tf_op jit(solution)/shard_map/ppermute | solution.py:44
  74.7 15.0 %collective-permute-start.7 = (bf16[64,1856]{1,0:T(8,128)(2,1)S(1)}, bf16[64,1856]{1,0:T(8,128)(2,1)S(1)}, u32[]{:S(2)}, u32[]{:S(2)}) collective-permute-start(bf16[64,1856]{1,0:T(8,128)(2,1)S(1)} %constant_dynamic-update-slice_fusion), channel_id=1, source_target_pairs={{0,3},{1,0},{2,1},{3,2},{4,7},{5,4},{6,5},{7,6},{8,11},{9,8},{10,9... | collective-permute-start | bytes 712712 | tf_op jit(solution)/shard_map/ppermute | solution.py:44
  77.5 12.2 %collective-permute-start.6 = (bf16[64,1856]{1,0:T(8,128)(2,1)S(1)}, bf16[64,1856]{1,0:T(8,128)(2,1)S(1)}, u32[]{:S(2)}, u32[]{:S(2)}) collective-permute-start(bf16[64,1856]{1,0:T(8,128)(2,1)S(1)} %constant_dynamic-update-slice_fusion), channel_id=1, source_target_pairs={{0,2},{1,3},{2,0},{3,1},{4,6},{5,7},{6,4},{7,5},{8,10},{9,11},{10,... | collective-permute-start | bytes 712712 | tf_op jit(solution)/shard_map/ppermute | solution.py:44
  80.1 12.2 %collective-permute-start.5 = (bf16[64,1856]{1,0:T(8,128)(2,1)S(1)}, bf16[64,1856]{1,0:T(8,128)(2,1)S(1)}, u32[]{:S(2)}, u32[]{:S(2)}) collective-permute-start(bf16[64,1856]{1,0:T(8,128)(2,1)S(1)} %constant_dynamic-update-slice_fusion), channel_id=1, source_target_pairs={{0,1},{1,2},{2,3},{3,0},{4,5},{5,6},{6,7},{7,4},{8,9},{9,10},{10,1... | collective-permute-start | bytes 712712 | tf_op jit(solution)/shard_map/ppermute | solution.py:44
  120.2 42.2 %copy-start.4 = (bf16[256,128]{1,0:T(8,128)(2,1)S(1)}, bf16[256,128]{1,0:T(8,128)(2,1)}, u32[]{:S(2)}) copy-start(bf16[256,128]{1,0:T(8,128)(2,1)} %left_ref.1) | copy-start | bytes 196612
  120.2 42.2 %copy-start.5 = (bf16[256,128]{1,0:T(8,128)(2,1)S(1)}, bf16[256,128]{1,0:T(8,128)(2,1)}, u32[]{:S(2)}) copy-start(bf16[256,128]{1,0:T(8,128)(2,1)} %right_ref.1) | copy-start | bytes 196612
  120.2 42.2 %copy-start.6 = (bf16[64,128]{1,0:T(8,128)(2,1)S(1)}, bf16[64,128]{1,0:T(8,128)(2,1)}, u32[]{:S(2)}) copy-start(bf16[64,128]{1,0:T(8,128)(2,1)} %gate_ref.1) | copy-start | bytes 49156
  124.0 38.3 %copy-start = (bf16[2048,128]{1,0:T(8,128)(2,1)S(1)}, bf16[2048,128]{1,0:T(8,128)(2,1)}, u32[]{:S(2)}) copy-start(bf16[2048,128]{1,0:T(8,128)(2,1)} %bonds_ref.1) | copy-start | bytes 1572868
  124.0 18.0 %all-to-all-start.3 = ((bf16[4,3,72,128]{3,2,1,0:T(8,128)(2,1)}), bf16[4,3,72,128]{3,2,1,0:T(8,128)(2,1)S(1)}, u32[]{:S(2)}, u32[]{:S(2)}) async-start(bf16[4,3,72,128]{3,2,1,0:T(8,128)(2,1)} %get-tuple-element.33), calls=%async_computation.3 | async-start | bytes 442368 | tf_op jit(solution)/shard_map/all_to_all | solution.py:37
  127.6 14.5 %collective-permute-start.8 = (bf16[2,72,128]{2,1,0:T(8,128)(2,1)S(1)}, bf16[2,72,128]{2,1,0:T(8,128)(2,1)S(1)}, u32[]{:S(2)}, u32[]{:S(2)}) collective-permute-start(bf16[2,72,128]{2,1,0:T(8,128)(2,1)S(1)} %get-tuple-element.34), channel_id=1, source_target_pairs={{0,508},{508,0},{16,12},{12,16},{32,28},{28,32},{48,44},{44,48},{6... | collective-permute-start | bytes 110600 | tf_op jit(solution)/shard_map/ppermute | solution.py:594
  133.1 9.0 %collective-permute-start.9 = (bf16[72,128]{1,0:T(8,128)(2,1)S(1)}, bf16[72,128]{1,0:T(8,128)(2,1)S(1)}, u32[]{:S(2)}, u32[]{:S(2)}) collective-permute-start(bf16[72,128]{1,0:T(8,128)(2,1)S(1)} %get-tuple-element.35), channel_id=1, source_target_pairs={{0,504},{504,0},{4,508},{508,4},{16,8},{8,16},{20,12},{12,20},{32,... | collective-permute-start | bytes 55304 | tf_op jit(solution)/shard_map/ppermute | solution.py:595
  142.8 19.5 %all-to-all-start.4 = ((bf16[4,192,128]{2,1,0:T(8,128)(2,1)}), bf16[4,192,128]{2,1,0:T(8,128)(2,1)S(1)}, u32[]{:S(2)}, u32[]{:S(2)}) async-start(bf16[4,192,128]{2,1,0:T(8,128)(2,1)} %mean.1), calls=%async_computation.4 | async-start | bytes 393216 | tf_op jit(solution)/shard_map/all_to_all | solution.py:37
  148.2 8.9 %collective-permute-start.10 = (bf16[256,128]{1,0:T(8,128)(2,1)S(1)}, bf16[256,128]{1,0:T(8,128)(2,1)S(1)}, u32[]{:S(2)}, u32[]{:S(2)}) collective-permute-start(bf16[256,128]{1,0:T(8,128)(2,1)S(1)} %get-tuple-element.39.refs_0_), channel_id=1, source_target_pairs={{0,1},{1,2},{2,3},{3,0},{4,5},{5,6},{6,7},{7,4},{8,9},{9,10},{10,1... | collective-permute-start | bytes 196616 | tf_op jit(solution)/shard_map/ppermute | solution.py:44
  150.2 7.7 %collective-permute-start.11 = (bf16[256,128]{1,0:T(8,128)(2,1)S(1)}, bf16[256,128]{1,0:T(8,128)(2,1)S(1)}, u32[]{:S(2)}, u32[]{:S(2)}) collective-permute-start(bf16[256,128]{1,0:T(8,128)(2,1)S(1)} %get-tuple-element.39.refs_0_), channel_id=1, source_target_pairs={{0,2},{1,3},{2,0},{3,1},{4,6},{5,7},{6,4},{7,5},{8,10},{9,11},{10,... | collective-permute-start | bytes 196616 | tf_op jit(solution)/shard_map/ppermute | solution.py:44
  155.0 7.4 %collective-permute-start.12 = (bf16[256,128]{1,0:T(8,128)(2,1)S(1)}, bf16[256,128]{1,0:T(8,128)(2,1)S(1)}, u32[]{:S(2)}, u32[]{:S(2)}) collective-permute-start(bf16[256,128]{1,0:T(8,128)(2,1)S(1)} %get-tuple-element.39.refs_0_), channel_id=1, source_target_pairs={{0,3},{1,0},{2,1},{3,2},{4,7},{5,4},{6,5},{7,6},{8,11},{9,8},{10,9... | collective-permute-start | bytes 196616 | tf_op jit(solution)/shard_map/ppermute | solution.py:44
  162.4 1.0 copy-start.1
